TPU v7x, 32 devices: a whole 2x2x4 slice. The times are simulated.
32 devices in a mesh: batch: 2 (over y), wide: 16 (over z, x, core).
Axes of the slice: x: 2, y: 2, z: 4, core: 2. Of those that a mesh axis runs over, the one named last changes fastest.
Arguments:
- inputs: float32 [4, 1536, 512], P('batch', 'wide'), may hold values from -6 to 6
- lengths: int32 [4], P('batch'), may hold values from 384 to 1536, as said below
- cotangent: float32 [4, 1536, 512], P('batch', 'wide'), may hold values from -6 to 6
- qkv_weight: float32 [2, 512, 1536], P(None, 'wide'), may hold values from -0.25 to 0.25
- proj_weight: float32 [2, 512, 512], P(None, 'wide'), may hold values from -3.5 to 3.5
- up_weight: float32 [2, 512, 2048], P(None, 'wide'), may hold values from -0.25 to 0.25
- down_weight: float32 [2, 2048, 512], P(None, 'wide'), may hold values from -0.125 to 0.125
- pool_weight: float32 [2, 512, 1536], P(None, 'wide'), may hold values from -0.1875 to 0.1875
- norm_params: float32 [2, 512, 4], P(None, 'wide')
- qkv_velocity: float32 [2, 512, 1536], P(None, 'wide'), may hold values from -96 to 96
- proj_velocity: float32 [2, 512, 512], P(None, 'wide'), may hold values from -96 to 96
- up_velocity: float32 [2, 512, 2048], P(None, 'wide'), may hold values from -96 to 96
- down_velocity: float32 [2, 2048, 512], P(None, 'wide'), may hold values from -96 to 96
- pool_velocity: float32 [2, 512, 1536], P(None, 'wide'), may hold values from -96 to 96
- norm_velocity: float32 [2, 512, 4], P(None, 'wide'), may hold values from -224 to 224
- qkv_average: float32 [2, 512, 1536], P(None, 'wide'), may hold values from -0.25 to 0.25
- proj_average: float32 [2, 512, 512], P(None, 'wide'), may hold values from -3.5 to 3.5
- up_average: float32 [2, 512, 2048], P(None, 'wide'), may hold values from -0.25 to 0.25
- down_average: float32 [2, 2048, 512], P(None, 'wide'), may hold values from -0.125 to 0.125
- pool_average: float32 [2, 512, 1536], P(None, 'wide'), may hold values from -0.1875 to 0.1875
- norm_average: float32 [2, 512, 4], P(None, 'wide')
Outputs:
- activations: float32 [4, 1536, 512], P('batch', 'wide')
- input_grad: float32 [4, 1536, 512], P('batch', 'wide')
- qkv_grad: float32 [2, 512, 1536], P(None, 'wide')
- proj_grad: float32 [2, 512, 512], P(None, 'wide')
- up_grad: float32 [2, 512, 2048], P(None, 'wide')
- down_grad: float32 [2, 2048, 512], P(None, 'wide')
- pool_grad: float32 [2, 512, 1536], P(None, 'wide')
- norm_grad: float32 [2, 512, 4], P(None, 'wide')
- qkv_momentum: float32 [2, 512, 1536], P(None, 'wide')
- proj_momentum: float32 [2, 512, 512], P(None, 'wide')
- up_momentum: float32 [2, 512, 2048], P(None, 'wide')
- down_momentum: float32 [2, 2048, 512], P(None, 'wide')
- pool_momentum: float32 [2, 512, 1536], P(None, 'wide')
- norm_momentum: float32 [2, 512, 4], P(None, 'wide')
- qkv_smooth: float32 [2, 512, 1536], P(None, 'wide')
- proj_smooth: float32 [2, 512, 512], P(None, 'wide')
- up_smooth: float32 [2, 512, 2048], P(None, 'wide')
- down_smooth: float32 [2, 2048, 512], P(None, 'wide')
- pool_smooth: float32 [2, 512, 1536], P(None, 'wide')
- norm_smooth: float32 [2, 512, 4], P(None, 'wide')
- qkv_updated: float32 [2, 512, 1536], P(None, 'wide')
- proj_updated: float32 [2, 512, 512], P(None, 'wide')
- up_updated: float32 [2, 512, 2048], P(None, 'wide')
- down_updated: float32 [2, 2048, 512], P(None, 'wide')
- pool_updated: float32 [2, 512, 1536], P(None, 'wide')
- norm_updated: float32 [2, 512, 4], P(None, 'wide')
Inputs may be any that keep to these rules, and one draw needn't show every extreme that they name: `lengths`: every length is a multiple of 3; one sequence has 1536 used positions and one has 384.
All inputs are finite; a program needn't handle non-finite values.
Results may differ from a plain program's by a relative error of at most 0.0003.
Values sent between devices are 32-bit elements; how exact they have to be, the bound alone decides.
No kernel may reach another device: no remote copies, remote signals or barrier semaphores. Data moves between devices by JAX's collectives and lax.ppermute only.
A program may use at most 256 MiB of HBM per device.

v0:
```python
import math

import jax
import jax.numpy as jnp
from jax import lax
from jax.sharding import PartitionSpec as P

HEADS = 8
HEAD_DIM = 64


HIGHEST = lax.Precision.HIGHEST
norm_eps = 1e-05
masked_score = -1e30
momentum_decay = 0.9
average_decay = 0.9
key_step = 128


def from_behind(block, axis, distance):
    devices = range(lax.axis_size(axis))
    route = [(i - distance, i) for i in devices if i - distance in devices]
    return lax.ppermute(block, axis, route)


def matmul(left, right):
    return jnp.dot(left, right, precision=HIGHEST)


def layer_norm(values, gain_col, shift_col):
    centred = values - jnp.mean(values, axis=-1, keepdims=True)
    variance = jnp.mean(centred * centred, axis=-1, keepdims=True)
    return centred * lax.rsqrt(variance + norm_eps) * gain_col + shift_col


def rotate(tensor, positions):
    half_dim = tensor.shape[-1] // 2
    inv_freq = 10000.0 ** (-2.0 * jnp.arange(half_dim, dtype=jnp.float32) / tensor.shape[-1])
    angles = positions.astype(jnp.float32)[:, None] * inv_freq[None, :]
    cosine = jnp.cos(angles)[:, None, :]
    sine_part = jnp.sin(angles)[:, None, :]
    lower_half = tensor[..., :half_dim]
    upper_half = tensor[..., half_dim:]
    return jnp.concatenate(
        [
            lower_half * cosine - upper_half * sine_part,
            lower_half * sine_part + upper_half * cosine,
        ],
        axis=-1,
    )


def project_heads(stream, qkv_mat, norm_cols, positions):
    normed = layer_norm(stream, norm_cols[:, 0], norm_cols[:, 1])
    packed = matmul(normed, qkv_mat).reshape(stream.shape[0], 3, HEADS, HEAD_DIM)
    return (rotate(packed[:, 0], positions), rotate(packed[:, 1], positions), packed[:, 2])


def finish_block(stream, attended, proj_mat, up_mat, down_mat, norm_cols):
    mixed = stream + matmul(attended, proj_mat)
    normed = layer_norm(mixed, norm_cols[:, 2], norm_cols[:, 3])
    return mixed + matmul(jax.nn.gelu(matmul(normed, up_mat), approximate=True), down_mat)


def split_keys(key_rows, value_rows):
    row_count = key_rows.shape[0]
    blocks = -(-row_count // key_step)
    key_blocks = key_rows.reshape(blocks, key_step, HEADS, HEAD_DIM)
    value_blocks = value_rows.reshape(blocks, key_step, HEADS, HEAD_DIM)
    return (row_count, blocks, key_blocks, value_blocks)


def forward_fold(queries, query_pos, length):
    score_scale = HEAD_DIM ** (-0.5)
    last_query = jnp.max(query_pos)

    def folder(running, pieces, offset):
        row_count, blocks, key_blocks, value_blocks = split_keys(pieces[0], pieces[1])

        def advance(status, members):
            key_blk, value_blk, number = members
            first_key = number * key_step
            key_pos = first_key + jnp.arange(key_step, dtype=jnp.int32)

            def compute(state_in):
                row_max, totals, summed = state_in
                allowed = (
                    (key_pos[None, :] <= query_pos[:, None])
                    & (key_pos[None, :] < length)
                    & (key_pos[None, :] < offset + row_count)
                )
                scores = (
                    jnp.einsum("qhe,khe->hqk", queries, key_blk, precision=HIGHEST) * score_scale
                )
                scores = jnp.where(allowed[None], scores, masked_score)
                new_max = jnp.maximum(row_max, jnp.max(scores, axis=-1))
                factor = jnp.exp(row_max - new_max)
                weights = jnp.where(allowed[None], jnp.exp(scores - new_max[..., None]), 0.0)
                totals = totals * factor + jnp.sum(weights, axis=-1)
                summed = summed * factor[..., None] + jnp.einsum(
                    "hqk,khe->hqe", weights, value_blk, precision=HIGHEST
                )
                return (new_max, totals, summed)

            def skipped(state_in):
                return state_in

            active = (first_key <= last_query) & (first_key < length)
            return (lax.cond(active, compute, skipped, status), None)

        outcome, unused = lax.scan(
            advance, running, (key_blocks, value_blocks, jnp.arange(blocks, dtype=jnp.int32))
        )
        return outcome

    return folder


def query_grad_fold(queries, query_pos, length, log_totals, grad_heads, deltas):
    score_scale = HEAD_DIM ** (-0.5)
    last_query = jnp.max(query_pos)

    def folder(running, pieces, offset):
        row_count, blocks, key_blocks, value_blocks = split_keys(pieces[0], pieces[1])

        def advance(grad_query, members):
            key_blk, value_blk, number = members
            first_key = number * key_step
            key_pos = first_key + jnp.arange(key_step, dtype=jnp.int32)

            def compute(grad_in):
                allowed = (
                    (key_pos[None, :] <= query_pos[:, None])
                    & (key_pos[None, :] < length)
                    & (key_pos[None, :] < offset + row_count)
                )
                scores = (
                    jnp.einsum("qhe,khe->hqk", queries, key_blk, precision=HIGHEST) * score_scale
                )
                probs = jnp.where(allowed[None], jnp.exp(scores - log_totals[..., None]), 0.0)
                grad_probs = jnp.einsum("hqe,khe->hqk", grad_heads, value_blk, precision=HIGHEST)
                grad_scores = probs * (grad_probs - deltas[..., None]) * score_scale
                return grad_in + jnp.einsum("hqk,khe->hqe", grad_scores, key_blk, precision=HIGHEST)

            def skipped(grad_in):
                return grad_in

            active = (first_key <= last_query) & (first_key < length)
            return (lax.cond(active, compute, skipped, grad_query), None)

        grad_query, unused = lax.scan(
            advance, running, (key_blocks, value_blocks, jnp.arange(blocks, dtype=jnp.int32))
        )
        return grad_query

    return folder


def key_grad_fold(key_heads, value_heads, key_pos, length):
    score_scale = HEAD_DIM ** (-0.5)
    first_key = jnp.min(key_pos)

    def folder(running, pieces, offset):
        row_count = pieces[0].shape[0]
        query_rows = pieces[0].reshape(row_count, HEADS, HEAD_DIM)
        grad_rows = pieces[1].reshape(row_count, HEADS, HEAD_DIM)
        lse_rows = jnp.transpose(pieces[2])
        delta_rows = jnp.transpose(pieces[3])
        query_pos = jnp.arange(row_count, dtype=jnp.int32)

        def compute(state_in):
            allowed = (key_pos[None, :] <= query_pos[:, None]) & (key_pos[None, :] < length)
            scores = (
                jnp.einsum("qhe,khe->hqk", query_rows, key_heads, precision=HIGHEST) * score_scale
            )
            probs = jnp.where(allowed[None], jnp.exp(scores - lse_rows[..., None]), 0.0)
            grad_value = jnp.einsum("hqk,qhe->khe", probs, grad_rows, precision=HIGHEST)
            grad_probs = jnp.einsum("qhe,khe->hqk", grad_rows, value_heads, precision=HIGHEST)
            grad_scores = probs * (grad_probs - delta_rows[..., None]) * score_scale
            grad_key = jnp.einsum("hqk,qhe->khe", grad_scores, query_rows, precision=HIGHEST)
            return (grad_key, grad_value)

        def skipped(state_in):
            return state_in

        active = (offset + row_count - 1 >= first_key) & (first_key < length)
        return lax.cond(active, compute, skipped, running)

    return folder


def gather_block(which, qkv_weight, proj_weight, up_weight, down_weight, pool_weight, norm_params):
    return (
        lax.all_gather(qkv_weight[which], "wide", axis=0, tiled=True),
        lax.all_gather(proj_weight[which], "wide", axis=0, tiled=True),
        lax.all_gather(up_weight[which], "wide", axis=0, tiled=True),
        lax.all_gather(down_weight[which], "wide", axis=0, tiled=True),
        lax.all_gather(pool_weight[which], "wide", axis=0, tiled=True),
        lax.all_gather(norm_params[which], "wide", axis=0, tiled=True),
    )


def attend_forward(queries, key_heads, value_heads, query_pos, length):
    local_rows = queries.shape[0]
    model_width = HEADS * HEAD_DIM
    start_state = (
        jnp.full((HEADS, local_rows), masked_score, jnp.float32),
        jnp.zeros((HEADS, local_rows), jnp.float32),
        jnp.zeros((HEADS, local_rows, HEAD_DIM), jnp.float32),
    )
    folder = forward_fold(queries, query_pos, length)
    key_flat = key_heads.reshape(local_rows, model_width)
    value_flat = value_heads.reshape(local_rows, model_width)
    row_max, totals, summed = folder(
        start_state,
        (
            lax.all_gather(key_flat, "wide", axis=0, tiled=True),
            lax.all_gather(value_flat, "wide", axis=0, tiled=True),
        ),
        jnp.int32(0),
    )
    attended = jnp.transpose(summed / totals[..., None], (1, 0, 2)).reshape(local_rows, model_width)
    return (attended, row_max + jnp.log(totals), None)


def attend_backward(
    queries, key_heads, value_heads, query_pos, length, log_totals, attended, grad_att
):
    local_rows = queries.shape[0]
    model_width = HEADS * HEAD_DIM
    grad_heads = jnp.transpose(grad_att.reshape(local_rows, HEADS, HEAD_DIM), (1, 0, 2))
    att_heads = jnp.transpose(attended.reshape(local_rows, HEADS, HEAD_DIM), (1, 0, 2))
    deltas = jnp.sum(grad_heads * att_heads, axis=-1)
    folder = query_grad_fold(queries, query_pos, length, log_totals, grad_heads, deltas)
    start_query = jnp.zeros((HEADS, local_rows, HEAD_DIM), jnp.float32)
    key_flat = key_heads.reshape(local_rows, model_width)
    value_flat = value_heads.reshape(local_rows, model_width)
    grad_query = folder(
        start_query,
        (
            lax.all_gather(key_flat, "wide", axis=0, tiled=True),
            lax.all_gather(value_flat, "wide", axis=0, tiled=True),
        ),
        jnp.int32(0),
    )
    key_folder = key_grad_fold(key_heads, value_heads, query_pos, length)
    start_keys = (
        jnp.zeros((local_rows, HEADS, HEAD_DIM), jnp.float32),
        jnp.zeros((local_rows, HEADS, HEAD_DIM), jnp.float32),
    )
    query_flat = queries.reshape(local_rows, model_width)
    grad_key, grad_value = key_folder(
        start_keys,
        (
            lax.all_gather(query_flat, "wide", axis=0, tiled=True),
            lax.all_gather(grad_att, "wide", axis=0, tiled=True),
            lax.all_gather(jnp.transpose(log_totals), "wide", axis=0, tiled=True),
            lax.all_gather(jnp.transpose(deltas), "wide", axis=0, tiled=True),
        ),
        jnp.int32(0),
    )
    return (jnp.transpose(grad_query, (1, 0, 2)), grad_key, grad_value)


def block_forward(stream, weights, positions, length):
    queries, key_heads, value_heads = project_heads(stream, weights[0], weights[5], positions)
    attended, log_totals, gathered = attend_forward(
        queries, key_heads, value_heads, positions, length
    )
    result = finish_block(stream, attended, weights[1], weights[2], weights[3], weights[5])
    return (result, (attended, log_totals, gathered))


def block_backward(grad_result, stream, saved, weights, positions, length):
    attended, log_totals, gathered = saved
    unused, finish_pull = jax.vjp(
        finish_block, stream, attended, weights[1], weights[2], weights[3], weights[5]
    )
    grad_stream, grad_att, grad_proj, grad_up, grad_down, grad_norm = finish_pull(grad_result)

    def heads_of(stream_in, qkv_mat, norm_cols):
        return project_heads(stream_in, qkv_mat, norm_cols, positions)

    projected, heads_pull = jax.vjp(heads_of, stream, weights[0], weights[5])
    queries, key_heads, value_heads = projected
    grad_query, grad_key, grad_value = attend_backward(
        queries, key_heads, value_heads, positions, length, log_totals, attended, grad_att
    )
    grad_inner, grad_qkv, grad_norm_inner = heads_pull((grad_query, grad_key, grad_value))
    return (
        grad_stream + grad_inner,
        (grad_qkv, grad_proj, grad_up, grad_down, grad_norm + grad_norm_inner),
    )


def reduce_grads(grad_qkv, grad_proj, grad_up, grad_down, grad_pool, grad_norm):
    shares = (
        lax.psum_scatter(grad_qkv, "wide", scatter_dimension=0, tiled=True),
        lax.psum_scatter(grad_proj, "wide", scatter_dimension=0, tiled=True),
        lax.psum_scatter(grad_up, "wide", scatter_dimension=0, tiled=True),
        lax.psum_scatter(grad_down, "wide", scatter_dimension=0, tiled=True),
        lax.psum_scatter(grad_pool, "wide", scatter_dimension=0, tiled=True),
        lax.psum_scatter(grad_norm, "wide", scatter_dimension=0, tiled=True),
    )
    return lax.psum((shares[0], shares[1], shares[2], shares[3], shares[4], shares[5]), "batch")


def update(grad, weight, velocity, average, rate):
    momentum = momentum_decay * velocity + grad
    updated = weight - rate * (grad + momentum_decay * momentum)
    smooth = average_decay * average + (1.0 - average_decay) * updated
    return (momentum, smooth, updated)


def shards(
    inputs,
    lengths,
    cotangent,
    qkv_weight,
    proj_weight,
    up_weight,
    down_weight,
    pool_weight,
    norm_params,
    qkv_velocity,
    proj_velocity,
    up_velocity,
    down_velocity,
    pool_velocity,
    norm_velocity,
    qkv_average,
    proj_average,
    up_average,
    down_average,
    pool_average,
    norm_average,
):
    micro_count, local_rows, model_width = inputs.shape
    short_rows = local_rows // 3
    wide_index = lax.axis_index("wide")
    full_pos = wide_index * local_rows + jnp.arange(local_rows, dtype=jnp.int32)
    short_pos = wide_index * short_rows + jnp.arange(short_rows, dtype=jnp.int32)
    first_weights = gather_block(
        0, qkv_weight, proj_weight, up_weight, down_weight, pool_weight, norm_params
    )
    full_list = []
    first_saved = []
    for number in range(micro_count):
        result, saved = block_forward(inputs[number], first_weights, full_pos, lengths[number])
        full_list.append(result)
        first_saved.append(saved)
    full_out = jnp.stack(full_list)
    pool_taps = first_weights[4].reshape(model_width, 3, model_width)
    tails = from_behind(full_out[:, -2:, :], "wide", 1)
    shifted = jnp.concatenate([tails, full_out[:, :-2, :]], axis=1).reshape(
        micro_count, short_rows, 3, model_width
    )
    shortened = jnp.einsum("mjid,die->mje", shifted, pool_taps, precision=HIGHEST)
    second_weights = gather_block(
        1, qkv_weight, proj_weight, up_weight, down_weight, pool_weight, norm_params
    )
    short_list = []
    second_saved = []
    for number in range(micro_count):
        result, saved = block_forward(
            shortened[number], second_weights, short_pos, lengths[number] // 3
        )
        short_list.append(result)
        second_saved.append(saved)
    short_out = jnp.stack(short_list)
    upsampled = jnp.einsum("mjd,de->mje", short_out, second_weights[4], precision=HIGHEST).reshape(
        micro_count, local_rows, model_width
    )
    activations = full_out + upsampled
    valid = (full_pos[None, :] < lengths[:, None]).astype(jnp.float32)
    grad_out = cotangent * valid[..., None]
    grad_groups = grad_out.reshape(micro_count, short_rows, 3 * model_width)
    grad_short = jnp.einsum("mje,de->mjd", grad_groups, second_weights[4], precision=HIGHEST)
    grad_unpool = jnp.einsum("mjd,mje->de", short_out, grad_groups, precision=HIGHEST)
    second_sum = None
    grad_list = []
    for number in range(micro_count):
        grad_in, block_grads = block_backward(
            grad_short[number],
            shortened[number],
            second_saved[number],
            second_weights,
            short_pos,
            lengths[number] // 3,
        )
        grad_list.append(grad_in)
        second_sum = (
            block_grads if second_sum is None else jax.tree.map(jnp.add, second_sum, block_grads)
        )
    grad_shortened = jnp.stack(grad_list)
    second_grads = reduce_grads(
        second_sum[0], second_sum[1], second_sum[2], second_sum[3], grad_unpool, second_sum[4]
    )
    grad_shifted = jnp.einsum(
        "mje,die->mjid", grad_shortened, pool_taps, precision=HIGHEST
    ).reshape(micro_count, local_rows, model_width)
    grad_pool = jnp.einsum("mjid,mje->die", shifted, grad_shortened, precision=HIGHEST).reshape(
        model_width, 3 * model_width
    )
    heads_back = from_behind(grad_shifted[:, :2, :], "wide", -1)
    grad_full = grad_out + jnp.concatenate([grad_shifted[:, 2:, :], heads_back], axis=1)
    first_sum = None
    input_list = []
    for number in range(micro_count):
        grad_in, block_grads = block_backward(
            grad_full[number],
            inputs[number],
            first_saved[number],
            first_weights,
            full_pos,
            lengths[number],
        )
        input_list.append(grad_in)
        first_sum = (
            block_grads if first_sum is None else jax.tree.map(jnp.add, first_sum, block_grads)
        )
    input_grad = jnp.stack(input_list)
    first_grads = reduce_grads(
        first_sum[0], first_sum[1], first_sum[2], first_sum[3], grad_pool, first_sum[4]
    )
    rate = 0.5 / math.sqrt(
        model_width * micro_count * lax.axis_size("batch") * local_rows * lax.axis_size("wide")
    )
    grads = [jnp.stack([first_grads[number], second_grads[number]]) for number in range(6)]
    weights = (qkv_weight, proj_weight, up_weight, down_weight, pool_weight, norm_params)
    velocities = (
        qkv_velocity,
        proj_velocity,
        up_velocity,
        down_velocity,
        pool_velocity,
        norm_velocity,
    )
    averages = (qkv_average, proj_average, up_average, down_average, pool_average, norm_average)
    results = [
        update(grads[number], weights[number], velocities[number], averages[number], rate)
        for number in range(6)
    ]
    return (
        activations,
        input_grad,
        grads[0],
        grads[1],
        grads[2],
        grads[3],
        grads[4],
        grads[5],
        results[0][0],
        results[1][0],
        results[2][0],
        results[3][0],
        results[4][0],
        results[5][0],
        results[0][1],
        results[1][1],
        results[2][1],
        results[3][1],
        results[4][1],
        results[5][1],
        results[0][2],
        results[1][2],
        results[2][2],
        results[3][2],
        results[4][2],
        results[5][2],
    )


def solution(mesh):
    return jax.shard_map(
        shards,
        mesh=mesh,
        in_specs=(
            P("batch", "wide", None),
            P("batch"),
            P("batch", "wide", None),
            P(None, "wide", None),
            P(None, "wide", None),
            P(None, "wide", None),
            P(None, "wide", None),
            P(None, "wide", None),
            P(None, "wide", None),
            P(None, "wide", None),
            P(None, "wide", None),
            P(None, "wide", None),
            P(None, "wide", None),
            P(None, "wide", None),
            P(None, "wide", None),
            P(None, "wide", None),
            P(None, "wide", None),
            P(None, "wide", None),
            P(None, "wide", None),
            P(None, "wide", None),
            P(None, "wide", None),
        ),
        out_specs=(
            P("batch", "wide", None),
            P("batch", "wide", None),
            P(None, "wide", None),
            P(None, "wide", None),
            P(None, "wide", None),
            P(None, "wide", None),
            P(None, "wide", None),
            P(None, "wide", None),
            P(None, "wide", None),
            P(None, "wide", None),
            P(None, "wide", None),
            P(None, "wide", None),
            P(None, "wide", None),
            P(None, "wide", None),
            P(None, "wide", None),
            P(None, "wide", None),
            P(None, "wide", None),
            P(None, "wide", None),
            P(None, "wide", None),
            P(None, "wide", None),
            P(None, "wide", None),
            P(None, "wide", None),
            P(None, "wide", None),
            P(None, "wide", None),
            P(None, "wide", None),
            P(None, "wide", None),
        ),
        check_vma=False,
    )
```

profile of v0, /device:TPU:0, one launch (start us, length us, event | category | flops | bytes accessed | tf_op | source)
XLA Modules:
  0.0 2095.6 jit_solution(17134659221256278948)
XLA Ops:
  110.3 43.8 %all-gather.87.cloned.1.call-done = f32[1,512,1536]{2,0,1:T(1,128)} async-done(((f32[1,32,1536]{2,0,1:T(1,128)}), f32[1,512,1536]{2,0,1:T(1,128)}) %all-gather.87.cloned.1.call-update) | async-done | bytes 3145744 | tf_op jit(solution)/shard_map/all_gather | solution.py:198
  162.5 38.5 %all-gather.47.cloned.1.call-done = f32[1536,512]{1,0:T(8,128)} async-done(((f32[96,512]{1,0:T(8,128)}), f32[1536,512]{1,0:T(8,128)}) %all-gather.47.cloned.1.call-update) | async-done | bytes 3145744 | tf_op jit(solution)/shard_map/all_gather | solution.py:217
  212.8 35.2 %all-gather.49.cloned.1.call-done = f32[1536,512]{1,0:T(8,128)} async-done(((f32[96,512]{1,0:T(8,128)}), f32[1536,512]{1,0:T(8,128)}) %all-gather.49.cloned.1.call-update) | async-done | bytes 3145744 | tf_op jit(solution)/shard_map/all_gather | solution.py:218
  296.2 38.2 %all-gather.51.cloned.1.call-done = f32[1536,512]{1,0:T(8,128)} async-done(((f32[96,512]{1,0:T(8,128)}), f32[1536,512]{1,0:T(8,128)}) %all-gather.51.cloned.1.call-update) | async-done | bytes 3145744 | tf_op jit(solution)/shard_map/all_gather | solution.py:217
  346.2 35.3 %all-gather.53.cloned.1.call-done = f32[1536,512]{1,0:T(8,128)} async-done(((f32[96,512]{1,0:T(8,128)}), f32[1536,512]{1,0:T(8,128)}) %all-gather.53.cloned.1.call-update) | async-done | bytes 3145744 | tf_op jit(solution)/shard_map/all_gather | solution.py:218
  393.4 35.3 %while.117 = (s32[]{:T(128)}, f32[8,96]{1,0:T(8,128)S(1)}, f32[8,96]{1,0:T(8,128)S(1)}, f32[8,96,64]{1,2,0:T(8,128)S(1)}, s32[12]{0:T(128)S(1)}, /*index=5*/s32[...) while((s32[]{:T(128)}, f32[8,96]{1,0:T(8,128)S(1)}, ...), condition=%wide.region_18.19_spmd.clone, body=%wide.region_13.18_spmd.clone.sunk | while | flops 151918560 | bytes 2398043 | solution.py:111
  438.5 46.9 %all-gather.85.cloned.1.call-done = f32[1,2048,512]{2,1,0:T(8,128)} async-done(((f32[1,128,512]{2,1,0:T(8,128)}), f32[1,2048,512]{2,1,0:T(8,128)}) %all-gather.85.cloned.1.call-update) | async-done | bytes 4194320 | tf_op jit(solution)/shard_map/all_gather | solution.py:197
  576.6 34.7 %all-gather.61.cloned.1.call-done = f32[512,512]{1,0:T(8,128)} async-done(((f32[32,512]{1,0:T(8,128)}), f32[512,512]{1,0:T(8,128)}) %all-gather.61.cloned.1.call-update) | async-done | bytes 1048592 | tf_op jit(solution)/shard_map/all_gather | solution.py:218
  654.1 35.6 %all-gather.55.cloned.1.call-done = f32[512,512]{1,0:T(8,128)} async-done(((f32[32,512]{1,0:T(8,128)}), f32[512,512]{1,0:T(8,128)}) %all-gather.55.cloned.1.call-update) | async-done | bytes 1048592 | tf_op jit(solution)/shard_map/all_gather | solution.py:217
  694.7 34.6 %all-gather.57.cloned.1.call-done = f32[512,512]{1,0:T(8,128)} async-done(((f32[32,512]{1,0:T(8,128)}), f32[512,512]{1,0:T(8,128)}) %all-gather.57.cloned.1.call-update) | async-done | bytes 1048592 | tf_op jit(solution)/shard_map/all_gather | solution.py:218
  790.4 42.8 %all-gather.95.cloned.1.call-done = f32[1,2048,512]{2,1,0:T(8,128)} async-done(((f32[1,128,512]{2,1,0:T(8,128)}), f32[1,2048,512]{2,1,0:T(8,128)}) %all-gather.95.cloned.1.call-update) | async-done | bytes 4194320 | tf_op jit(solution)/shard_map/all_gather | solution.py:197
  1220.7 35.3 %while.122 = (s32[]{:T(128)}, f32[8,96,64]{1,2,0:T(8,128)S(1)}, s32[12]{0:T(128)S(1)}, s32[]{:T(128)}, s32[]{:T(128)}, /*index=5*/f32[12,128,8,64]{1,3,2,0:T(8,1...) while((s32[]{:T(128)}, f32[8,96,64]{1,2,0:T(8,128)S(1)}, ...), condition=%wide.region_74.75_spmd.clone, body=%wide.region_71.74_spmd.clone.sunk | while | flops 227168736 | bytes 3182907 | solution.py:151
  1256.7 36.0 %while.123 = (s32[]{:T(128)}, f32[8,96,64]{1,2,0:T(8,128)S(1)}, s32[12]{0:T(128)S(1)}, s32[]{:T(128)}, s32[]{:T(128)}, /*index=5*/f32[12,128,8,64]{1,3,2,0:T(8,1...) while((s32[]{:T(128)}, f32[8,96,64]{1,2,0:T(8,128)S(1)}, ...), condition=%wide.region_85.86_spmd.clone, body=%wide.region_82.85_spmd.clone.sunk | while | flops 227168736 | bytes 3182907 | solution.py:151
  1327.5 34.4 %conditional.15 = (f32[96,8,32]{0,2,1:T(8,128)}, f32[96,8,32]{0,2,1:T(8,128)}, f32[96,8,32]{0,2,1:T(8,128)}, f32[96,3,8,64]{0,3,2,1:T(8,128)}) conditional(s32[]{:T(128)} %convert_element_type.77, () %tuple.201, (s32[96]{0:T(128)}, s32[1536]{0:T(1024)}, s32[]{:T(128)}, f32[1536,512]{1,0:T(8,128)}, f32[96,8,64]{0,2,1:T(8,128)}, ...), branch_computations={%region_80.81_spmd, %region_81.82_spmd} | conditional | flops 3631276032 | bytes 104897728 | solution.py:187
  1395.8 45.3 %reduce-scatter.35.cloned.1.call-done = f32[32,1536]{1,0:T(8,128)} async-done(((f32[512,1536]{1,0:T(8,128)}), f32[32,1536]{1,0:T(8,128)}) %reduce-scatter.35.cloned.1.call-update) | async-done | bytes 196624 | tf_op jit(solution)/shard_map/reduce_scatter | solution.py:302
  1441.1 75.3 %reduce-scatter.27.cloned.1.call-done = f32[32,2048]{1,0:T(8,128)} async-done(((f32[512,2048]{1,0:T(8,128)}), f32[32,2048]{1,0:T(8,128)}) %reduce-scatter.27.cloned.1.call-update) | async-done | bytes 262160 | tf_op jit(solution)/shard_map/reduce_scatter | solution.py:300
  1516.4 76.1 %reduce-scatter.31.cloned.1.call-done = f32[128,512]{1,0:T(8,128)} async-done(((f32[2048,512]{1,0:T(8,128)}), f32[128,512]{1,0:T(8,128)}) %reduce-scatter.31.cloned.1.call-update) | async-done | bytes 262160 | tf_op jit(solution)/shard_map/reduce_scatter | solution.py:301
  1592.5 69.0 %reduce-scatter.19.cloned.1.call-done = f32[32,1536]{1,0:T(8,128)} async-done(((f32[512,1536]{1,0:T(8,128)}), f32[32,1536]{1,0:T(8,128)}) %reduce-scatter.19.cloned.1.call-update) | async-done | bytes 196624 | tf_op jit(solution)/shard_map/reduce_scatter | solution.py:298
  1661.5 69.0 %reduce-scatter.33.cloned.1.call-done = f32[32,1536]{1,0:T(8,128)} async-done(((f32[512,1536]{1,0:T(8,128)}), f32[32,1536]{1,0:T(8,128)}) %reduce-scatter.33.cloned.1.call-update) | async-done | bytes 196624 | tf_op jit(solution)/shard_map/reduce_scatter | solution.py:302
  1730.5 75.3 %reduce-scatter.25.cloned.1.call-done = f32[32,2048]{1,0:T(8,128)} async-done(((f32[512,2048]{1,0:T(8,128)}), f32[32,2048]{1,0:T(8,128)}) %reduce-scatter.25.cloned.1.call-update) | async-done | bytes 262160 | tf_op jit(solution)/shard_map/reduce_scatter | solution.py:300
  1805.8 76.0 %reduce-scatter.29.cloned.1.call-done = f32[128,512]{1,0:T(8,128)} async-done(((f32[2048,512]{1,0:T(8,128)}), f32[128,512]{1,0:T(8,128)}) %reduce-scatter.29.cloned.1.call-update) | async-done | bytes 262160 | tf_op jit(solution)/shard_map/reduce_scatter | solution.py:301
  1881.8 68.9 %reduce-scatter.17.cloned.1.call-done = f32[32,1536]{1,0:T(8,128)} async-done(((f32[512,1536]{1,0:T(8,128)}), f32[32,1536]{1,0:T(8,128)}) %reduce-scatter.17.cloned.1.call-update) | async-done | bytes 196624 | tf_op jit(solution)/shard_map/reduce_scatter | solution.py:298
  1954.9 54.2 %reduce-scatter.37.cloned.1.call-done = f32[32,4]{1,0:T(8,128)} async-done(((f32[512,4]{1,0:T(8,128)}), f32[32,4]{1,0:T(8,128)}) %reduce-scatter.37.cloned.1.call-update) | async-done | bytes 528
  2016.2 56.3 %all-reduce.48.cloned.1.call-done = (f32[1,32,1536]{2,1,0:T(8,128)}, f32[1,32,1536]{2,1,0:T(8,128)}, f32[1,32,512]{2,1,0:T(8,128)}, f32[1,32,512]{2,1,0:T(8,128)...) async-done(((f32[1,32,1536]{2,1,0:T(8,128)}, ...) | async-done | bytes 1966096 | tf_op jit(solution)/shard_map/psum | solution.py:305
  (1274 shorter events, 1095.5 us)
Async XLA Ops:
  73.8 307.7 %all-gather.53.cloned.1.call-start = ((), (), s32[]{:S(2)}) async-start(), calls=%async_computation.15 | async-start | bytes 3342336 | tf_op jit(solution)/shard_map/all_gather | solution.py:218
  74.7 359.1 %all-gather.83.cloned.1.call-start = ((), (), s32[]{:S(2)}) async-start(), calls=%async_computation.40 | async-start | bytes 4456448 | tf_op jit(solution)/shard_map/all_gather | solution.py:196
  75.6 409.9 %all-gather.85.cloned.1.call-start = ((), (), s32[]{:S(2)}) async-start(), calls=%async_computation.41 | async-start | bytes 4456448 | tf_op jit(solution)/shard_map/all_gather | solution.py:197
  76.5 455.8 %all-gather.97.cloned.1.call-start = ((), (), s32[]{:S(2)}) async-start(), calls=%async_computation.47 | async-start | bytes 3342336 | tf_op jit(solution)/shard_map/all_gather | solution.py:198
  77.2 494.4 %all-gather.59.cloned.1.call-start = ((), (), s32[]{:S(2)}) async-start(), calls=%async_computation.18 | async-start | bytes 1114112 | tf_op jit(solution)/shard_map/all_gather | solution.py:217
  518.1 315.1 %all-gather.95.cloned.1.call-start = ((), (), s32[]{:S(2)}) async-start(), calls=%async_computation.46 | async-start | bytes 4456448 | tf_op jit(solution)/shard_map/all_gather | solution.py:197
  518.7 473.2 %all-gather.63.cloned.1.call-start = ((), (), s32[]{:S(2)}) async-start(), calls=%async_computation.20 | async-start | bytes 1114112 | tf_op jit(solution)/shard_map/all_gather | solution.py:255
  539.0 452.9 %all-gather.65.cloned.1.call-start = ((), (), s32[]{:S(2)}) async-start(), calls=%async_computation.21 | async-start | bytes 1114112 | tf_op jit(solution)/shard_map/all_gather | solution.py:256
  862.2 430.5 %all-gather.71.cloned.1.call-start = ((), (), s32[]{:S(2)}) async-start(), calls=%async_computation.24 | async-start | bytes 3342336 | tf_op jit(solution)/shard_map/all_gather | solution.py:255
  865.4 427.4 %all-gather.73.cloned.1.call-start = ((), (), s32[]{:S(2)}) async-start(), calls=%async_computation.25 | async-start | bytes 3342336 | tf_op jit(solution)/shard_map/all_gather | solution.py:256
  1054.5 272.4 %all-gather.75.cloned.1.call-start = ((), (), s32[]{:S(2)}) async-start(), calls=%async_computation.26 | async-start | bytes 3342336 | tf_op jit(solution)/shard_map/all_gather | solution.py:255
  1058.2 324.8 %reduce-scatter.39.cloned.1.call-start = ((), (), s32[]{:S(2)}) async-start(), calls=%async_computation.49 | async-start | bytes 278528
  1062.9 332.9 %reduce-scatter.23.cloned.1.call-start = ((), (), s32[]{:S(2)}) async-start(), calls=%async_computation.31 | async-start | bytes 1114112 | tf_op jit(solution)/shard_map/reduce_scatter | solution.py:299
  1066.3 329.5 %reduce-scatter.21.cloned.1.call-start = ((), (), s32[]{:S(2)}) async-start(), calls=%async_computation.30 | async-start | bytes 1114112 | tf_op jit(solution)/shard_map/reduce_scatter | solution.py:299
  1070.4 370.7 %reduce-scatter.35.cloned.1.call-start = ((), (), s32[]{:S(2)}) async-start(), calls=%async_computation.37 | async-start | bytes 3342336 | tf_op jit(solution)/shard_map/reduce_scatter | solution.py:302
  1083.4 433.0 %reduce-scatter.27.cloned.1.call-start = ((), (), s32[]{:S(2)}) async-start(), calls=%async_computation.33 | async-start | bytes 4456448 | tf_op jit(solution)/shard_map/reduce_scatter | solution.py:300
  1093.5 499.0 %reduce-scatter.31.cloned.1.call-start = ((), (), s32[]{:S(2)}) async-start(), calls=%async_computation.35 | async-start | bytes 4456448 | tf_op jit(solution)/shard_map/reduce_scatter | solution.py:301
  1103.2 558.4 %reduce-scatter.19.cloned.1.call-start = ((), (), s32[]{:S(2)}) async-start(), calls=%async_computation.29 | async-start | bytes 3342336 | tf_op jit(solution)/shard_map/reduce_scatter | solution.py:298
  1111.4 619.2 %reduce-scatter.33.cloned.1.call-start = ((), (), s32[]{:S(2)}) async-start(), calls=%async_computation.36 | async-start | bytes 3342336 | tf_op jit(solution)/shard_map/reduce_scatter | solution.py:302
  1119.9 686.0 %reduce-scatter.25.cloned.1.call-start = ((), (), s32[]{:S(2)}) async-start(), calls=%async_computation.32 | async-start | bytes 4456448 | tf_op jit(solution)/shard_map/reduce_scatter | solution.py:300
  1130.1 751.7 %reduce-scatter.29.cloned.1.call-start = ((), (), s32[]{:S(2)}) async-start(), calls=%async_computation.34 | async-start | bytes 4456448 | tf_op jit(solution)/shard_map/reduce_scatter | solution.py:301
  1139.9 810.9 %reduce-scatter.17.cloned.1.call-start = ((), (), s32[]{:S(2)}) async-start(), calls=%async_computation.28 | async-start | bytes 3342336 | tf_op jit(solution)/shard_map/reduce_scatter | solution.py:298
  1374.0 635.1 %reduce-scatter.37.cloned.1.call-start = ((), (), s32[]{:S(2)}) async-start(), calls=%async_computation.48 | async-start | bytes 278528
  1395.0 677.4 %all-reduce.48.cloned.1.call-start = ((), (), s32[]{:S(2)}) async-start(), calls=%async_computation.50 | async-start | bytes 3932160 | tf_op jit(solution)/shard_map/psum | solution.py:305
  (261 other events, 8358.7 us)
Sparse Core Ops, SparseCore 0:
  10.9 48.0 all-gather.78
  61.8 44.8 all-gather.88
  109.6 44.4 all-gather.86
  384.2 49.5 all-gather.82
  436.4 49.0 all-gather.84
  731.8 49.6 all-gather.92
  784.1 49.0 all-gather.94
  992.1 44.2 all-gather.70
  1054.6 45.6 all-gather.72
  1102.5 44.2 all-gather.74
  1149.0 44.3 all-gather.76
  1197.3 54.2 reduce-scatter.38
  1255.2 56.4 reduce-scatter.22
  1315.7 56.4 reduce-scatter.20
  1375.9 65.1 reduce-scatter.34
  1445.0 71.4 reduce-scatter.26
  1520.8 71.6 reduce-scatter.30
  1596.1 65.3 reduce-scatter.18
  1665.3 65.1 reduce-scatter.32
  1734.4 71.3 reduce-scatter.24
  1810.0 71.7 reduce-scatter.28
  1885.5 65.2 reduce-scatter.16
  1954.8 54.1 reduce-scatter.36
  2011.8 60.6 all-reduce.47
  (15 shorter events, 588.3 us)
where the time goes:
time: 2110 us; the launch traced here: 2100 us
  waiting for transfers between devices  1150 us (55%)
  matrix products  294 us (14%)
  local copies, waits for them, and re-layouts  235 us (11%)
  blocking collectives  209 us (10%)
  loops' own time  112 us (5%)
  other arithmetic  60.2 us (3%)
  between operations  27.4 us (1%)
    dot_general x48, matrix products, matmul(): return jnp.dot(left, right, precision=HIGHEST)  182 us
    reduce_scatter x2, waiting for transfers between devices, reduce_grads(): lax.psum_scatter(grad_down, 'wide', scatter_dimension=0, tiled=True)  152 us
    reduce_scatter x2, waiting for transfers between devices, reduce_grads(): lax.psum_scatter(grad_up, 'wide', scatter_dimension=0, tiled=True)  151 us
    all_gather x4, waiting for transfers between devices, attend_forward(): lax.all_gather(key_flat, 'wide', axis=0, tiled=True)  145 us
    all_gather x4, waiting for transfers between devices, attend_forward(): lax.all_gather(value_flat, 'wide', axis=0, tiled=True)  140 us
    reduce_scatter x2, waiting for transfers between devices, reduce_grads(): lax.psum_scatter(grad_qkv, 'wide', scatter_dimension=0, tiled=True)  138 us
    reduce_scatter x2, waiting for transfers between devices, reduce_grads(): lax.psum_scatter(grad_pool, 'wide', scatter_dimension=0, tiled=True)  114 us
    another operation x8, loops' own time, folder(): lax.scan(advance, running, (key_blocks, value_blocks, jnp.arange(blocks,...  110 us
  transfers between devices with their start and end apart: 41, of which 29 were waited for; matrix products, arithmetic and copies ran while one was open for 27% of the time, Pallas kernels for 0%

commit v1 on v0

v1 whole, which is shorter than its diff:
```python
import functools
import math

import jax
import jax.numpy as jnp
import numpy as np
from jax import lax
from jax.experimental import pallas as pl
from jax.experimental.pallas import tpu as pltpu
from jax.sharding import Mesh, PartitionSpec as P

HEADS = 8
HEAD_DIM = 64
D = HEADS * HEAD_DIM
HIGH = lax.Precision.HIGH
norm_eps = 1e-05
masked_score = -1e30
momentum_decay = 0.9
average_decay = 0.9
F32 = jnp.float32
BF16 = jnp.bfloat16
VMEM_LIMIT = 56 << 20


def matmul(left, right):
    return jnp.dot(left, right, precision=HIGH)


def layer_norm(values, gain, shift):
    centred = values - jnp.mean(values, axis=-1, keepdims=True)
    variance = jnp.mean(centred * centred, axis=-1, keepdims=True)
    return centred * lax.rsqrt(variance + norm_eps) * gain + shift


def split(value):
    high = value.astype(BF16)
    return high, (value - high.astype(F32)).astype(BF16)


def dot(a, b, dims):
    return lax.dot_general(a, b, (dims, ((), ())), preferred_element_type=F32)


NN = ((1,), (0,))
NT = ((1,), (1,))
TN = ((0,), (0,))


def rope_tables(rows):
    half = HEAD_DIM // 2
    freq = (10000.0 ** (-2.0 * np.arange(half, dtype=np.float32) / HEAD_DIM)).astype(np.float32)
    angles = np.arange(rows, dtype=np.float32)[:, None] * freq[None, :]
    cosine = np.cos(angles).astype(np.float32)
    sine = np.sin(angles).astype(np.float32)
    both = np.concatenate([cosine, cosine], axis=1)
    signed = np.concatenate([-sine, sine], axis=1)
    return (
        np.concatenate([both, both], axis=1),
        np.concatenate([signed, signed], axis=1),
        np.ascontiguousarray(cosine.T),
        np.ascontiguousarray(sine.T),
    )


def swap_halves(pair):
    half = HEAD_DIM // 2
    width = pair.shape[1]
    lane = lax.broadcasted_iota(jnp.int32, pair.shape, 1) % HEAD_DIM
    ahead = pltpu.roll(pair, width - half, 1)
    behind = pltpu.roll(pair, half, 1)
    return jnp.where(lane < half, ahead, behind)


def allowed_keys(first_row, rows, keys, length):
    key_pos = lax.broadcasted_iota(jnp.int32, (keys, rows), 0)
    query_pos = lax.broadcasted_iota(jnp.int32, (keys, rows), 1) + first_row
    return (key_pos <= query_pos) & (key_pos < length)


def attend_rows(raw, length, cos_ref, sin_ref, out_refs, rows, step, half_rows):
    packed_ref, turned_ref, lse_ref, qcat_ref, kcat_ref, vcat_ref = out_refs
    scale = HEAD_DIM ** (-0.5)
    for start in range(0, rows, step):
        part = slice(start, start + step)
        pair = raw[part, : 2 * HEAD_DIM]
        pair = pair * cos_ref[part, :] + swap_halves(pair) * sin_ref[part, :]
        lane = lax.broadcasted_iota(jnp.int32, pair.shape, 1)
        pair = jnp.where(lane < HEAD_DIM, pair * scale, pair)
        high, low = split(pair)
        qh, kh = high[:, :HEAD_DIM], high[:, HEAD_DIM:]
        ql, kl = low[:, :HEAD_DIM], low[:, HEAD_DIM:]
        vh, vl = split(raw[part, 2 * HEAD_DIM :])
        qcat_ref[part, :] = jnp.concatenate([qh, ql, qh], axis=1)
        kcat_ref[part, :] = jnp.concatenate([kh, kh, kl], axis=1)
        vcat_ref[part, :] = jnp.concatenate([vh, vh, vl], axis=1)
    value_pair = jnp.transpose(vcat_ref[:, HEAD_DIM:].astype(F32)).astype(BF16)
    value_high = value_pair[:HEAD_DIM]
    for start in range(0, rows, step):
        part = slice(start, start + step)
        keys = start + step
        scores = dot(kcat_ref[:keys, :], qcat_ref[part, :], NT)
        scores = jnp.where(allowed_keys(start, step, keys, length), scores, masked_score)
        row_max = jnp.max(scores, axis=0, keepdims=True)
        weights = jnp.exp(scores - row_max)
        total = jnp.sum(weights, axis=0, keepdims=True)
        wh, wl = split(weights)
        summed = dot(value_pair[:, :keys], wh, NN)
        summed = summed[:HEAD_DIM] + summed[HEAD_DIM:] + dot(value_high[:, :keys], wl, NN)
        turned = summed / total
        lse_ref[:, part] = jnp.broadcast_to(row_max + jnp.log(total), (8, step))
        turned_ref[:, part] = turned
    attended = jnp.transpose(
        jnp.concatenate([turned_ref[...], turned_ref[...]], axis=0)
    ).reshape(rows // (2 * half_rows), 2, half_rows, 2 * HEAD_DIM)
    lane = lax.broadcasted_iota(jnp.int32, attended[:, 0].shape, 2)
    packed_ref[...] = jnp.where(lane < HEAD_DIM, attended[:, 0], attended[:, 1])


def first_attend_kernel(
    half_rows, step, slots, len_ref, chip_ref, xa_ref, xb_ref, w_ref, cos_ref, sin_ref, *refs
):
    out_refs, norm_ref, raw = refs[:6], refs[6], refs[7]
    chips = xa_ref.shape[0]
    rows = chips * 2 * half_rows
    total = jnp.sum(xa_ref[:, half_rows:, :], axis=0) + jnp.sum(xb_ref[:, half_rows:, :], axis=0)
    norm_ref[...] = total
    gain, shift = total[0:1], total[1:2]
    wh, wl = split(w_ref[...])
    for chip in range(chips):
        for side, ref in enumerate((xa_ref, xb_ref)):
            slot = slots[side](chip_ref[0] ^ chip)
            hh, hl = split(layer_norm(ref[slot, :half_rows, :], gain, shift))
            first = (chip * 2 + side) * half_rows
            raw[first : first + half_rows, :] = dot(hh, wh, NN) + dot(hh, wl, NN) + dot(hl, wh, NN)
    attend_rows(raw, len_ref[0], cos_ref, sin_ref, out_refs, rows, step, half_rows)


def unpack_rows(packed_ref, raw, half_rows, width):
    chips = packed_ref.shape[0]
    for chip in range(chips):
        for side in range(2):
            first = (chip * 2 + side) * half_rows
            raw[first : first + half_rows, :] = packed_ref[
                chip, :, side * width : (side + 1) * width
            ]


def second_attend_kernel(half_rows, step, len_ref, packed_ref, cos_ref, sin_ref, *refs):
    out_refs, raw = refs[:6], refs[6]
    rows = packed_ref.shape[0] * 2 * half_rows
    unpack_rows(packed_ref, raw, half_rows, 3 * HEAD_DIM)
    attend_rows(raw, len_ref[0], cos_ref, sin_ref, out_refs, rows, step, half_rows)


def attend_grad(
    rows, step, half_rows, length, refs, grad_ref, tables, out_ref, scratch
):
    qcat_ref, kcat_ref, vcat_ref, turned_ref, lse_ref = refs
    cos_ref, sin_ref, cos_t_ref, sin_t_ref = tables
    grad_rows, dk_acc, dv_acc, dq_t, dqkv = scratch
    scale = HEAD_DIM ** (-0.5)
    unpack_rows(grad_ref, grad_rows, half_rows, HEAD_DIM)
    key_pair = jnp.transpose(kcat_ref[:, HEAD_DIM:].astype(F32)).astype(BF16)
    key_high = key_pair[:HEAD_DIM]
    dk_acc[...] = jnp.zeros_like(dk_acc)
    dv_acc[...] = jnp.zeros_like(dv_acc)
    for start in range(0, rows, step):
        part = slice(start, start + step)
        keys = start + step
        grad = grad_rows[part, :]
        gh, gl = split(grad)
        gcat = jnp.concatenate([gh, gl, gh], axis=1)
        grad_t = jnp.transpose(jnp.concatenate([grad, grad], axis=1))[:HEAD_DIM]
        delta = jnp.sum(grad_t * turned_ref[:, part], axis=0, keepdims=True)
        scores = dot(kcat_ref[:keys, :], qcat_ref[part, :], NT)
        probs = jnp.where(
            allowed_keys(start, step, keys, length), jnp.exp(scores - lse_ref[0:1, part]), 0.0
        )
        grad_probs = dot(vcat_ref[:keys, :], gcat, NT)
        grad_scores = probs * (grad_probs - delta)
        ph, pw = split(probs)
        sh, sl = split(grad_scores)
        dv_acc[:keys, :] += dot(ph, gcat[:, : 2 * HEAD_DIM], NN)
        dv_acc[:keys, :HEAD_DIM] += dot(pw, gh, NN)
        dk_acc[:keys, :] += dot(sh, qcat_ref[part, : 2 * HEAD_DIM], NN)
        dk_acc[:keys, :HEAD_DIM] += dot(sl, qcat_ref[part, :HEAD_DIM], NN)
        turned = dot(key_pair[:, :keys], sh, NN)
        turned = turned[:HEAD_DIM] + turned[HEAD_DIM:] + dot(key_high[:, :keys], sl, NN)
        dq_t[:, part] = turned * scale
    half = HEAD_DIM // 2
    low, high = dq_t[:half, :], dq_t[half:, :]
    back_low = low * cos_t_ref[...] + high * sin_t_ref[...]
    back_high = high * cos_t_ref[...] - low * sin_t_ref[...]
    dq = jnp.transpose(jnp.concatenate([back_low, back_high, back_low, back_high], axis=0))
    for start in range(0, rows, step):
        part = slice(start, start + step)
        dk = dk_acc[part, :HEAD_DIM] + dk_acc[part, HEAD_DIM:]
        dk = jnp.concatenate([dk, dk], axis=1)
        dk = dk * cos_ref[part, :] - swap_halves(dk) * sin_ref[part, :]
        dv = dv_acc[part, :HEAD_DIM] + dv_acc[part, HEAD_DIM:]
        dqkv[part, :] = jnp.concatenate([dq[part, :HEAD_DIM], dk[:, :HEAD_DIM], dv], axis=1)
    chips = out_ref.shape[0]
    for chip in range(chips):
        first = chip * 2 * half_rows
        out_ref[chip, :, :] = jnp.concatenate(
            [dqkv[first : first + half_rows, :], dqkv[first + half_rows : first + 2 * half_rows, :]],
            axis=1,
        )


def second_grad_kernel(
    half_rows, step, len_ref, q_ref, k_ref, v_ref, t_ref, l_ref, g_ref, c, s, ct, st, out_ref, *scratch
):
    rows = q_ref.shape[0]
    refs = (q_ref, k_ref, v_ref, t_ref, l_ref)
    attend_grad(rows, step, half_rows, len_ref[0], refs, g_ref, (c, s, ct, st), out_ref, scratch)


def first_grad_kernel(
    half_rows,
    step,
    slots,
    len_ref,
    chip_ref,
    xa_ref,
    xb_ref,
    q_ref,
    k_ref,
    v_ref,
    t_ref,
    l_ref,
    g_ref,
    c,
    s,
    ct,
    st,
    out_ref,
    m_ref,
    *scratch,
):
    rows = q_ref.shape[0]
    refs = (q_ref, k_ref, v_ref, t_ref, l_ref)
    attend_grad(rows, step, half_rows, len_ref[0], refs, g_ref, (c, s, ct, st), out_ref, scratch[:5])
    dqkv, nh_ref, nl_ref = scratch[4:]
    chips = xa_ref.shape[0]
    for chip in range(chips):
        for side, ref in enumerate((xa_ref, xb_ref)):
            slot = slots[side](chip_ref[0] ^ chip)
            nh, nl = split(layer_norm(ref[slot, :half_rows, :], 1.0, 0.0))
            first = (chip * 2 + side) * half_rows
            nh_ref[first : first + half_rows, :] = nh
            nl_ref[first : first + half_rows, :] = nl
    dh, dl = split(dqkv[...])
    nh = nh_ref[...]
    product = dot(nh, dh, TN) + dot(nh, dl, TN) + dot(nl_ref[...], dh, TN)
    owners, rows_each = m_ref.shape[0], m_ref.shape[1] - 8
    column = jnp.sum(dqkv[...], axis=0, keepdims=True)
    m_ref[:, :rows_each, :] = product.reshape(owners, rows_each, 3 * HEAD_DIM)
    m_ref[:, rows_each:, :] = jnp.broadcast_to(column[None], (owners, 8, 3 * HEAD_DIM))


SMEM = pl.BlockSpec(memory_space=pltpu.SMEM)
VMEM = pl.BlockSpec(memory_space=pltpu.VMEM)


def attend_outs(rows, half_rows):
    width = 3 * HEAD_DIM
    return [
        jax.ShapeDtypeStruct((rows // (2 * half_rows), half_rows, 2 * HEAD_DIM), F32),
        jax.ShapeDtypeStruct((HEAD_DIM, rows), F32),
        jax.ShapeDtypeStruct((8, rows), F32),
        jax.ShapeDtypeStruct((rows, width), BF16),
        jax.ShapeDtypeStruct((rows, width), BF16),
        jax.ShapeDtypeStruct((rows, width), BF16),
    ]


def call(kernel, outs, scratch, scalars, flops, *args):
    size = sum(math.prod(a.shape) * a.dtype.itemsize for a in list(args) + list(outs))
    return pl.pallas_call(
        kernel,
        out_shape=outs,
        in_specs=[SMEM] * scalars + [VMEM] * (len(args) - scalars),
        out_specs=[VMEM] * len(outs),
        scratch_shapes=scratch,
        compiler_params=pltpu.CompilerParams(vmem_limit_bytes=VMEM_LIMIT),
        cost_estimate=pl.CostEstimate(flops=flops, bytes_accessed=size, transcendentals=0),
    )(*args)


def query_step(rows):
    return math.gcd(rows, 256)


def bit_count(size):
    return size.bit_length() - 1


def swap_with(value, axis, size, mask):
    return lax.ppermute(value, axis, [(i, i ^ mask) for i in range(size)])


class Layout:
    def __init__(self, groups, ranks, cores):
        self.groups = groups
        self.ranks = ranks
        self.cores = cores
        self.chips = HEADS * ranks
        self.devices = self.chips * cores
        self.chip_axes = ("h", "r") if ranks > 1 else ("h",)

    def chip(self):
        return lax.axis_index("h") * self.ranks + lax.axis_index("r")

    def swap_chip(self, value, mask):
        if self.ranks == 1:
            return swap_with(value, "h", HEADS, mask)
        route = [(i, i ^ mask) for i in range(self.chips)]
        return lax.ppermute(value, ("h", "r"), route)

    def shift_chip(self, value, distance):
        chips = range(self.chips)
        route = [(i - distance, i) for i in chips if i - distance in chips]
        return lax.ppermute(value, ("h", "r") if self.ranks > 1 else "h", route)

    def gather_chips(self, value, masks):
        held = value[None]
        for mask in masks:
            held = jnp.concatenate([held, self.swap_chip(held, mask)], axis=0)
        return held

    def slot_of(self, masks):
        def slot(distance):
            found = 0
            for place, mask in enumerate(masks):
                bit = mask.bit_length() - 1
                found = found + (((distance >> bit) & 1) << place)
            return found

        return slot

    def heads_to_rows(self, value):
        value = value.reshape((HEADS, self.ranks) + value.shape[1:])
        mine = lax.dynamic_index_in_dim(value, lax.axis_index("r"), 1, keepdims=False)
        return lax.all_to_all(mine, "h", 0, 0, tiled=True)

    def rows_to_heads(self, value):
        got = lax.all_to_all(value, "h", 0, 0, tiled=True)
        if self.ranks > 1:
            got = lax.all_gather(got, "r", axis=1, tiled=False)
            got = got.reshape((self.chips,) + value.shape[1:])
        return got

    def reduce_owned(self, grads, first_batch):
        bits = bit_count(self.chips)
        rows = grads.shape[1]
        state = grads.reshape((2,) * bits + (self.cores, rows, D))
        core = lax.axis_index("s")
        chip = self.chip()
        group = lax.axis_index("b")

        def halve(state, place, bit, send):
            keep = lax.dynamic_index_in_dim(state, bit, place, keepdims=False)
            away = lax.dynamic_index_in_dim(state, 1 - bit, place, keepdims=False)
            return keep + send(away)

        state = halve(state, bits, core, lambda v: swap_with(v, "s", 2, 1))

        def batch_stages(state):
            for place in range(bit_count(self.groups)):
                dim = state.ndim - 2
                count = state.shape[dim]
                state = state.reshape(state.shape[:dim] + (2, count // 2, D))
                state = halve(
                    state,
                    dim,
                    (group >> place) & 1,
                    lambda v, place=place: swap_with(v, "b", self.groups, 1 << place),
                )
            return state

        for number in range(bits):
            if number == first_batch:
                state = batch_stages(state)
            state = halve(
                state,
                bits - 1 - number,
                (chip >> number) & 1,
                lambda v, number=number: self.swap_chip(v, 1 << number),
            )
        if first_batch >= bits:
            state = batch_stages(state)
        for place in reversed(range(bit_count(self.groups))):
            other = swap_with(state, "b", self.groups, 1 << place)
            bit = (group >> place) & 1
            state = jnp.where(
                bit == 0,
                jnp.concatenate([state, other], axis=0),
                jnp.concatenate([other, state], axis=0),
            )
        return state

    def sum_batch(self, value):
        for place in range(bit_count(self.groups)):
            value = value + swap_with(value, "b", self.groups, 1 << place)
        return value


def column_blocks(mat):
    return [mat[:, i * D : (i + 1) * D] for i in range(mat.shape[1] // D)]


def owner_blocks(mat, owners):
    return [b.reshape(owners, -1, D) for b in column_blocks(mat)]


class Packed:
    def __init__(self, gathered):
        self.gathered = gathered
        self.at = 0

    def take(self, rows):
        block = self.gathered[:, self.at : self.at + rows, :]
        self.at += rows
        return block.reshape(-1, D)

    def columns(self, rows, count):
        return jnp.concatenate([self.take(rows) for _ in range(count)], axis=1)


class Unpacked:
    def __init__(self, owned):
        self.owned = owned
        self.at = 0

    def take(self, rows):
        block = self.owned[self.at : self.at + rows]
        self.at += rows
        return block

    def columns(self, rows, count):
        return jnp.concatenate([self.take(rows) for _ in range(count)], axis=1)


def update(grad, weight, velocity, average, rate):
    momentum = momentum_decay * velocity + grad
    updated = weight - rate * (grad + momentum_decay * momentum)
    smooth = average_decay * average + (1.0 - average_decay) * updated
    return (momentum, smooth, updated)


def from_heads(got, half_rows, parts):
    value = got.reshape(HEADS, half_rows, 2, parts, HEAD_DIM)
    return jnp.transpose(value, (2, 1, 3, 0, 4)).reshape(2 * half_rows, parts * D)


def to_heads(value, half_rows, parts):
    value = value.reshape(2, half_rows, parts, HEADS, HEAD_DIM)
    return jnp.transpose(value, (3, 1, 0, 2, 4)).reshape(
        HEADS, half_rows, 2 * parts * HEAD_DIM
    )


def finish_block(stream, attended, proj, up, down, gain, shift):
    mixed = stream + matmul(attended, proj)
    normed = layer_norm(mixed, gain, shift)
    return mixed + matmul(jax.nn.gelu(matmul(normed, up), approximate=True), down)


def norm_rows(vectors, owners):
    each = D // owners
    block = jnp.stack(vectors).reshape(len(vectors), owners, each)
    block = jnp.transpose(block, (1, 0, 2))
    return jnp.pad(block, ((0, 0), (0, 16 - len(vectors)), (0, D - each)))


def shards(layout, rate, args):
    inputs, lengths, cotangent = args[:3]
    weights, velocities, averages = args[3:9], args[9:15], args[15:21]
    qkv_w, proj_w, up_w, down_w, pool_w, norm_w = weights
    half = inputs.shape[1]
    short_half = half // 3
    each = qkv_w.shape[1]
    ff_each = down_w.shape[1]
    up_blocks = up_w.shape[2] // D
    owners = layout.devices
    chip = layout.chip()
    core = lax.axis_index("s")
    owner = chip * layout.cores + core
    length = lax.dynamic_slice_in_dim(lengths, core, 1, 0)
    chip_arg = chip.reshape(1).astype(jnp.int32)
    seq = layout.chips * 2 * half
    short_seq = seq // 3

    norm_local = jnp.transpose(norm_w, (0, 2, 1)).reshape(8, each)
    norm_lanes = lax.dynamic_update_slice(
        jnp.zeros((8, D), F32), norm_local, (0, owner * each)
    )
    carried = jnp.concatenate([inputs, jnp.broadcast_to(norm_lanes, (2, 8, D))], axis=1)
    carried = lax.all_to_all(carried, "s", 0, 0, tiled=True)
    stream = carried[:, :half].reshape(2 * half, D)
    top = layout.chips // 2
    bits = bit_count(layout.chips)
    masks_a = tuple(1 << i for i in reversed(range(bits)))
    masks_b = (1,) + tuple(1 << i for i in reversed(range(1, bits)))
    slots = (layout.slot_of(masks_a), layout.slot_of(masks_b))
    xa = layout.gather_chips(carried[0], masks_a)
    xb = layout.gather_chips(carried[1], masks_b)

    head_cols = jnp.transpose(qkv_w[0].reshape(each, 3, HEADS, HEAD_DIM), (2, 0, 1, 3))
    head_cols = head_cols.reshape(HEADS, each, 3 * HEAD_DIM)
    head_cols = jnp.repeat(head_cols, layout.ranks * layout.cores, axis=0)
    head_w = lax.all_to_all(head_cols, layout.chip_axes + ("s",), 0, 0, tiled=True)
    head_w = head_w.reshape(D, 3 * HEAD_DIM)

    down_local = down_w
    first_pack = jnp.concatenate(
        [proj_w[0]]
        + column_blocks(up_w[0])
        + [down_local[0]]
        + column_blocks(pool_w[0])
        + column_blocks(qkv_w[1])
        + [proj_w[1]]
        + column_blocks(qkv_w[0]),
        axis=0,
    )
    second_pack = jnp.concatenate(
        column_blocks(up_w[1]) + [down_local[1]] + column_blocks(pool_w[1]), axis=0
    )
    wide_axes = layout.chip_axes + ("s",)
    first = Packed(lax.all_gather(first_pack, wide_axes, axis=0, tiled=False))
    second = Packed(lax.all_gather(second_pack, wide_axes, axis=0, tiled=False))
    proj0 = first.take(each)
    up0 = first.columns(each, up_blocks)
    down0 = first.take(ff_each)
    pool0 = jnp.concatenate([first.take(each) for _ in range(3)], axis=0)
    qkv1 = first.columns(each, 3)
    proj1 = first.take(each)
    qkv0 = first.columns(each, 3)
    up1 = second.columns(each, up_blocks)
    down1 = second.take(ff_each)
    pool1 = second.columns(each, 3)

    cos, sin, cos_t, sin_t = rope_tables(seq)
    tables = (cos, sin)
    tables_t = (cos_t, sin_t)
    short_tables = (cos[:short_seq], sin[:short_seq])
    short_tables_t = (cos_t[:, :short_seq], sin_t[:, :short_seq])
    step = query_step(seq)
    short_step = query_step(short_seq)

    outs = call(
        functools.partial(first_attend_kernel, half, step, slots),
        attend_outs(seq, half) + [jax.ShapeDtypeStruct((8, D), F32)],
        [pltpu.VMEM((seq, 3 * HEAD_DIM), F32)],
        2,
        seq * seq * HEAD_DIM * 12 + seq * D * 192 * 6,
        length,
        chip_arg,
        xa,
        xb,
        head_w,
        *tables,
    )
    packed, saved0, norm = outs[0], outs[1:6], outs[6]
    attended0 = from_heads(layout.heads_to_rows(packed), half, 1)
    full, finish0 = jax.vjp(
        finish_block, stream, attended0, proj0, up0, down0, norm[2], norm[3]
    )

    tails = layout.shift_chip(full[-2:], 1)
    shifted = jnp.concatenate([tails, full[:-2]], axis=0).reshape(2 * short_half, 3 * D)
    shortened = matmul(shifted, pool0)
    short_rows = 2 * short_half

    def project(rows, mat, gain, shift):
        return matmul(layer_norm(rows, gain, shift), mat)

    packed_qkv, project1 = jax.vjp(project, shortened, qkv1, norm[4], norm[5])
    got = layout.rows_to_heads(to_heads(packed_qkv, short_half, 3))
    short_length = length // 3
    outs = call(
        functools.partial(second_attend_kernel, short_half, short_step),
        attend_outs(short_seq, short_half),
        [pltpu.VMEM((short_seq, 3 * HEAD_DIM), F32)],
        1,
        short_seq * short_seq * HEAD_DIM * 12,
        short_length,
        got,
        *short_tables,
    )
    packed, saved1 = outs[0], outs[1:6]
    attended1 = from_heads(layout.heads_to_rows(packed), short_half, 1)
    short_out, finish1 = jax.vjp(
        finish_block, shortened, attended1, proj1, up1, down1, norm[6], norm[7]
    )
    activations = full + matmul(short_out, pool1).reshape(2 * half, D)

    positions = chip * 2 * half + jnp.arange(2 * half, dtype=jnp.int32)
    turned = lax.all_to_all(cotangent, "s", 0, 0, tiled=True).reshape(2 * half, D)
    grad_out = turned * (positions < length[0]).astype(F32)[:, None]
    grad_groups = grad_out.reshape(short_rows, 3 * D)
    grad_short = lax.dot_general(grad_groups, pool1, (((1,), (1,)), ((), ())), precision=HIGH)
    grad_pool1 = lax.dot_general(short_out, grad_groups, (((0,), (0,)), ((), ())), precision=HIGH)

    grad_shortened, grad_att1, grad_proj1, grad_up1, grad_down1, g6, g7 = finish1(grad_short)
    own_a = layout.reduce_owned(
        jnp.concatenate(
            owner_blocks(grad_up1, owners) + [grad_down1.reshape(owners, ff_each, D)], axis=1
        ),
        0,
    )
    own_b = None
    got = layout.rows_to_heads(to_heads(grad_att1, short_half, 1))
    scratch = lambda rows: [
        pltpu.VMEM((rows, HEAD_DIM), F32),
        pltpu.VMEM((rows, 2 * HEAD_DIM), F32),
        pltpu.VMEM((rows, 2 * HEAD_DIM), F32),
        pltpu.VMEM((HEAD_DIM, rows), F32),
        pltpu.VMEM((rows, 3 * HEAD_DIM), F32),
    ]
    dqkv_shape = lambda hr: jax.ShapeDtypeStruct((layout.chips, hr, 6 * HEAD_DIM), F32)
    (packed,) = call(
        functools.partial(second_grad_kernel, short_half, short_step),
        [dqkv_shape(short_half)],
        scratch(short_seq),
        1,
        short_seq * short_seq * HEAD_DIM * 30,
        short_length,
        saved1[2],
        saved1[3],
        saved1[4],
        saved1[0],
        saved1[1],
        got,
        *short_tables,
        *short_tables_t,
    )
    grad_packed1 = from_heads(layout.heads_to_rows(packed), short_half, 3)
    grad_inner, grad_qkv1, g4, g5 = project1(grad_packed1)
    grad_shortened = grad_shortened + grad_inner
    grad_shifted = lax.dot_general(
        grad_shortened, pool0, (((1,), (1,)), ((), ())), precision=HIGH
    ).reshape(2 * half, D)
    grad_pool0 = lax.dot_general(shifted, grad_shortened, (((0,), (0,)), ((), ())), precision=HIGH)
    pool0_blocks = [b.reshape(owners, each, D) for b in jnp.split(grad_pool0, 3, axis=0)]
    own_b = layout.reduce_owned(
        jnp.concatenate(
            pool0_blocks
            + owner_blocks(grad_pool1, owners)
            + owner_blocks(grad_qkv1, owners)
            + owner_blocks(grad_proj1, owners)
            + [norm_rows([g4, g5, g6, g7], owners)],
            axis=1,
        ),
        1,
    )
    heads_back = layout.shift_chip(grad_shifted[:2], -1)
    grad_full = grad_out + jnp.concatenate([grad_shifted[2:], heads_back], axis=0)

    grad_stream, grad_att0, grad_proj0, grad_up0, grad_down0, g2, g3 = finish0(grad_full)
    got = layout.rows_to_heads(to_heads(grad_att0, half, 1))
    own_c = layout.reduce_owned(
        jnp.concatenate(
            owner_blocks(grad_up0, owners) + [norm_rows([g2, g3], owners)], axis=1
        ),
        0,
    )
    own_d = layout.reduce_owned(
        jnp.concatenate(
            [grad_down0.reshape(owners, ff_each, D)] + owner_blocks(grad_proj0, owners), axis=1
        ),
        1,
    )
    packed, product = call(
        functools.partial(first_grad_kernel, half, step, slots),
        [
            dqkv_shape(half),
            jax.ShapeDtypeStruct((owners, each + 8, 3 * HEAD_DIM), F32),
        ],
        scratch(seq) + [pltpu.VMEM((seq, D), BF16), pltpu.VMEM((seq, D), BF16)],
        2,
        seq * seq * HEAD_DIM * 30 + seq * D * 192 * 6,
        length,
        chip_arg,
        xa,
        xb,
        saved0[2],
        saved0[3],
        saved0[4],
        saved0[0],
        saved0[1],
        got,
        *tables,
        *tables_t,
    )
    grad_packed0 = from_heads(layout.heads_to_rows(packed), half, 3)
    grad_normed = lax.dot_general(grad_packed0, qkv0, (((1,), (1,)), ((), ())), precision=HIGH)
    unused, norm_pull = jax.vjp(lambda rows: layer_norm(rows, norm[0], norm[1]), stream)
    input_grad = grad_stream + norm_pull(grad_normed)[0]
    input_grad = lax.all_to_all(input_grad.reshape(2, half, D), "s", 0, 0, tiled=True)
    activations = lax.all_to_all(activations.reshape(2, half, D), "s", 0, 0, tiled=True)

    product = product.reshape(HEADS, layout.ranks, layout.cores, each + 8, 3 * HEAD_DIM)
    product = lax.dynamic_index_in_dim(product, lax.axis_index("r"), 1, keepdims=False)
    keep = lax.dynamic_index_in_dim(product, core, 1, keepdims=False)
    away = lax.dynamic_index_in_dim(product, 1 - core, 1, keepdims=False)
    product = layout.sum_batch(keep + swap_with(away, "s", 2, 1))
    product = lax.all_to_all(product, "h", 0, 0, tiled=True)
    product = jnp.transpose(
        product.reshape(HEADS, each + 8, 3, HEAD_DIM), (1, 2, 0, 3)
    ).reshape(each + 8, 3 * D)
    columns = product[each : each + 1]
    product = product[:each]
    gain, shift = norm_w[0][:, 0:1], norm_w[0][:, 1:2]
    grad_qkv0 = product * gain + shift * columns
    own0 = jnp.sum(qkv_w[0] * product, axis=1)
    own1 = jnp.sum(qkv_w[0] * columns, axis=1)

    a, b, c, d = Unpacked(own_a), Unpacked(own_b), Unpacked(own_c), Unpacked(own_d)
    up_g1 = a.columns(each, up_blocks)
    down_g1 = a.take(ff_each)
    pool_g0 = b.columns(each, 3)
    pool_g1 = b.columns(each, 3)
    qkv_g1 = b.columns(each, 3)
    proj_g1 = b.take(each)
    norm_g1 = b.take(16)
    up_g0 = c.columns(each, up_blocks)
    norm_g0 = c.take(16)
    down_g0 = d.take(ff_each)
    proj_g0 = d.take(each)
    norm_first = jnp.stack([own0, own1, norm_g0[0, :each], norm_g0[1, :each]], axis=1)
    norm_second = jnp.transpose(norm_g1[:4, :each])
    grads = [
        jnp.stack([grad_qkv0, qkv_g1]),
        jnp.stack([proj_g0, proj_g1]),
        jnp.stack([up_g0, up_g1]),
        jnp.stack([down_g0, down_g1]),
        jnp.stack([pool_g0, pool_g1]),
        jnp.stack([norm_first, norm_second]),
    ]
    results = [
        update(grads[i], weights[i], velocities[i], averages[i], rate) for i in range(6)
    ]
    return (
        (activations, input_grad)
        + tuple(grads)
        + tuple(r[0] for r in results)
        + tuple(r[1] for r in results)
        + tuple(r[2] for r in results)
    )


def solution(mesh):
    groups, wide = mesh.shape["batch"], mesh.shape["wide"]

    def program(*args):
        cores = args[0].shape[0] // groups
        ranks = wide // (HEADS * cores)
        layout = Layout(groups, ranks, cores)
        rate = 0.5 / math.sqrt(math.prod(args[0].shape))
        fine = Mesh(mesh.devices.reshape(groups, HEADS, ranks, cores), ("b", "h", "r", "s"))
        rows = ("h", "r", "s")
        stream = P("b", rows, None)
        weight = P(None, rows, None)
        return jax.shard_map(
            lambda *local: shards(layout, rate, local),
            mesh=fine,
            in_specs=(stream, P("b"), stream) + (weight,) * 18,
            out_specs=(stream, stream) + (weight,) * 24,
            check_vma=False,
        )(*args)

    return program
```

time: 2110 us -> 739 us (0.35)
  waiting for transfers between devices: 1150 us -> 327 us
  matrix products: 294 us -> 70.6 us
  blocking collectives: 209 us -> 8.34 us
  loops' own time: 112 us -> 0 us
  local copies, waits for them, and re-layouts: 235 us -> 129 us
  starting transfers between devices: 7.62 us -> 99.1 us
  Pallas kernels: 0 us -> 31.8 us
    reduce_scatter x10 -> x0, waiting for transfers between devices: 555 us -> none  [the longest x2 152 us: reduce_grads(): lax.psum_scatter(grad_down, 'wide', scatter_dimension=0, tiled=True)]
    all_gather x26 -> x2, waiting for transfers between devices: 479 us -> 58.6 us  [the longest x1 57 us: shards(): second = Packed(lax.all_gather(second_pack, wide_axes, axis=0, tiled=False))]
    dot_general x90 -> x28, matrix products: 294 us -> 70.6 us  [the longest x23 57 us: matmul(): return jnp.dot(left, right, precision=HIGH)]
    ppermute x2 -> x34, waiting for transfers between devices: 2.07 us -> 225 us  [the longest x32 225 us: swap_with(): return lax.ppermute(value, axis, [(i, i ^ mask) for i in range(size)])]
    all_gather x10 -> x0, blocking collectives: 204 us -> none  [the longest x4 86.5 us: attend_backward(): lax.all_gather(jnp.transpose(log_totals), 'wide', axis=0, tiled=True)]
    another operation x76 -> x0, loops' own time: 112 us -> none  [the longest x8 110 us: folder(): lax.scan(advance, running, (key_blocks, value_blocks, jnp.arange(blocks,...]
    unnamed x41 -> x2, waiting for transfers between devices: 57.7 us -> 0.03 us
    psum x1 -> x0, waiting for transfers between devices: 56.3 us -> none  [reduce_grads(): lax.psum((shares[0], shares[1], shares[2], shares[3], shares[4], shares[5...]
  transfers between devices with their start and end apart: 41 -> 47, of which waited for: 29 -> 27; matrix products, arithmetic and copies ran while one was open for 27% -> 27% of each run, Pallas kernels for 0% -> 3%
where the time goes in v1:
time: 739 us; the launch traced here: 730 us
  waiting for transfers between devices  327 us (44%)
  local copies, waits for them, and re-layouts  129 us (17%)
  starting transfers between devices  99.1 us (13%)
  matrix products  70.6 us (10%)
  other arithmetic  44.6 us (6%)
  Pallas kernels  31.8 us (4%)
  between operations  18.8 us (3%)
  blocking collectives  8.34 us (1%)
    ppermute x32, waiting for transfers between devices, swap_with(): return lax.ppermute(value, axis, [(i, i ^ mask) for i in range(size)])  225 us
    dot_general x23, matrix products, matmul(): return jnp.dot(left, right, precision=HIGH)  57 us
    all_gather x1, waiting for transfers between devices, shards(): second = Packed(lax.all_gather(second_pack, wide_axes, axis=0, tiled=False))  57 us
    ppermute x32, starting transfers between devices, swap_with(): return lax.ppermute(value, axis, [(i, i ^ mask) for i in range(size)])  42.1 us
    unnamed x306, local copies, waits for them, and re-layouts  35.9 us
    pallas_call x4, Pallas kernels, call(): pl.pallas_call(kernel, out_shape=outs, in_specs=[SMEM] * scalars + [VMEM]...  31.8 us
    all_to_all x4, waiting for transfers between devices, heads_to_rows(): return lax.all_to_all(mine, 'h', 0, 0, tiled=True)  27.7 us
    slice x4, local copies, waits for them, and re-layouts, take(): block = self.gathered[:, self.at:self.at + rows, :]  26.8 us
  transfers between devices with their start and end apart: 47, of which 27 were waited for; matrix products, arithmetic and copies ran while one was open for 27% of the time, Pallas kernels for 3%

profile of v1, /device:TPU:0, one launch (start us, length us, event | category | flops | bytes accessed | tf_op | source)
XLA Modules:
  0.0 729.7 jit_solution(17117361910687690345)
XLA Ops:
  22.9 12.5 %collective-permute-done = f32[1,104,512]{2,1,0:T(8,128)S(1)} collective-permute-done((f32[1,104,512]{2,1,0:T(8,128)S(1)}, f32[1,104,512]{2,1,0:T(8,128)S(1)}, u32[]{:S(2)}, u32[]{:S(2)}) %collective-permute-start) | collective-permute-done | bytes 213024 | tf_op jit(solution)/shard_map/ppermute | solution.py:300
  40.4 25.6 %collective-permute-done.1 = f32[2,104,512]{2,1,0:T(8,128)S(1)} collective-permute-done((f32[2,104,512]{2,1,0:T(8,128)S(1)}, f32[2,104,512]{2,1,0:T(8,128)S(1)}, u32[]{:S(2)}, u32[]{:S(2)}) %collective-permute-start.1) | collective-permute-done | bytes 426016 | tf_op jit(solution)/shard_map/ppermute | solution.py:300
  85.4 23.2 %collective-permute-done.2 = f32[4,104,512]{2,1,0:T(8,128)} collective-permute-done((f32[4,104,512]{2,1,0:T(8,128)}, f32[4,104,512]{2,1,0:T(8,128)}, u32[]{:S(2)}, u32[]{:S(2)}) %collective-permute-start.2) | collective-permute-done | bytes 852000 | tf_op jit(solution)/shard_map/ppermute | solution.py:300
  111.1 10.5 %collective-permute-done.5 = f32[4,104,512]{2,1,0:T(8,128)} collective-permute-done((f32[4,104,512]{2,1,0:T(8,128)}, f32[4,104,512]{2,1,0:T(8,128)}, u32[]{:S(2)}, u32[]{:S(2)}) %collective-permute-start.5) | collective-permute-done | bytes 852000 | tf_op jit(solution)/shard_map/ppermute | solution.py:300
  124.2 11.2 %all-to-all-done.1 = f32[16,32,192]{2,1,0:T(8,128)S(1)} async-done(((f32[16,32,192]{2,1,0:T(8,128)}), f32[16,32,192]{2,1,0:T(8,128)S(1)}, u32[]{:S(2)}, u32[]{:S(2)}) %all-to-all-start.1) | async-done | bytes 393248 | tf_op jit(solution)/shard_map/all_to_all | solution.py:513
  136.1 10.0 %shard_map.476 = (f32[8,96,128]{2,1,0:T(8,128)}, f32[64,1536]{1,0:T(8,128)}, f32[8,1536]{1,0:T(8,128)}, bf16[1536,192]{1,0:T(8,128)(2,1)}, bf16[1536,192]{1,0:T(...) custom-call(s32[1]{0:T(128)} %dynamic_slice.160.len_ref, s32[1]{0:T(128)} %bitcast.3.chip_ref, ...), custom_call_target="tpu_custom_call" | custom-call | flops 2717908992 | bytes 7995400 | tf_op jit(solution)/shard_map/pallas_call | solution.py:280
  151.9 14.6 %all-to-all-done.2 = f32[8,96,128]{2,1,0:T(8,128)S(1)} async-done(((f32[8,96,128]{2,1,0:T(8,128)}), f32[8,96,128]{2,1,0:T(8,128)S(1)}, u32[]{:S(2)}, u32[]{:S(2)}) %all-to-all-start.2) | async-done | bytes 393248 | tf_op jit(solution)/shard_map/all_to_all | solution.py:345
  178.3 11.0 %fusion.132 = (f32[16,32,512]{2,1,0:T(8,128)}, f32[16,32,512]{2,1,0:T(8,128)}, f32[16,32,512]{2,1,0:T(8,128)}, f32[16,32,512]{2,1,0:T(8,128)S(1)}, f32[16,32,512...) fusion(f32[16,608,512]{2,1,0:T(8,128)} %bitcast.353), kind=kLoop, calls=%fused_computation.337 | loop fusion | bytes 31457280 | tf_op jit(solution)/shard_map/slice | solution.py:423
  208.6 6.4 all-to-all-start.3
  218.4 57.0 %all-gather.7.cloned.1.call-done = f32[5632,512]{1,0:T(8,128)} async-done(((f32[352,512]{1,0:T(8,128)}), f32[5632,512]{1,0:T(8,128)}) %all-gather.7.cloned.1.call-update) | async-done | bytes 11534352 | tf_op jit(solution)/shard_map/all_gather | solution.py:532
  280.2 6.2 fusion.133
  343.1 6.0 all-to-all-start.8
  406.0 7.2 all-to-all-start.9
  434.1 14.9 %shard_map.479 = (f32[8,96,384]{2,1,0:T(8,128)}, f32[16,40,192]{2,1,0:T(8,128)}) custom-call(s32[1]{0:T(128)} %dynamic_slice.160.len_ref, s32[1]{0:T(128)} %bitcast.3.chip_ref, f32[8,104,512]{2,1,0:T(8,128)} %pad_maximum_fusion.16.xa_ref, f32[8,104,512]{2,1,0:T(8,128)} %pad_maximum_fusion.17.xb_ref, bf16[1536,192]{1,0:T(8,128)(2,1)} %get-tuple-element.49.q_ref, ...), custom_call_target="tpu_custom_call" | custom-call | flops 5435817984 | bytes 9650184 | tf_op jit(solution)/shard_map/pallas_call | solution.py:280
  465.9 6.0 all-to-all-start.12
  504.4 9.9 %all-to-all-done.10 = f32[8,96,384]{2,1,0:T(8,128)} async-done(((f32[8,96,384]{2,1,0:T(8,128)}), f32[8,96,384]{2,1,0:T(8,128)}, u32[]{:S(2)}, u32[]{:S(2)}) %all-to-all-start.10) | async-done | bytes 1179680 | tf_op jit(solution)/shard_map/all_to_all | solution.py:345
  539.2 6.8 collective-permute-done.24
  571.7 27.8 %collective-permute-done.18 = f32[2,2,80,512]{3,2,1,0:T(8,128)S(1)} collective-permute-done((f32[2,2,80,512]{3,2,1,0:T(8,128)S(1)}, f32[2,2,80,512]{3,2,1,0:T(8,128)S(1)}, u32[]{:S(2)}, u32[]{:S(2)}) %collective-permute-start.18) | collective-permute-done | bytes 655392 | tf_op jit(solution)/shard_map/ppermute | solution.py:300
  601.2 8.1 %collective-permute-done.19 = f32[2,80,512]{2,1,0:T(8,128)S(1)} collective-permute-done((f32[2,80,512]{2,1,0:T(8,128)S(1)}, f32[2,80,512]{2,1,0:T(8,128)S(1)}, u32[]{:S(2)}, u32[]{:S(2)}) %collective-permute-start.19) | collective-permute-done | bytes 327712 | tf_op jit(solution)/shard_map/ppermute | solution.py:300
  609.5 33.9 %collective-permute-done.30 = f32[2,2,128,512]{3,2,1,0:T(8,128)S(1)} collective-permute-done((f32[2,2,128,512]{3,2,1,0:T(8,128)S(1)}, f32[2,2,128,512]{3,2,1,0:T(8,128)S(1)}, u32[]{:S(2)}, u32[]{:S(2)}) %collective-permute-start.30) | collective-permute-done | bytes 1048608 | tf_op jit(solution)/shard_map/ppermute | solution.py:300
  648.6 6.6 collective-permute-done.31
  655.4 24.7 %collective-permute-done.21 = f32[80,512]{1,0:T(8,128)S(1)} collective-permute-done((f32[80,512]{1,0:T(8,128)S(1)}, f32[80,512]{1,0:T(8,128)S(1)}, u32[]{:S(2)}, u32[]{:S(2)}) %collective-permute-start.21) | collective-permute-done | bytes 163872 | tf_op jit(solution)/shard_map/ppermute | solution.py:300
  686.8 10.5 %collective-permute-done.13 = f32[2,168,512]{2,1,0:T(8,128)S(1)} collective-permute-done((f32[2,168,512]{2,1,0:T(8,128)S(1)}, f32[2,168,512]{2,1,0:T(8,128)S(1)}, u32[]{:S(2)}, u32[]{:S(2)}) %collective-permute-start.13) | collective-permute-done | bytes 688160 | tf_op jit(solution)/shard_map/ppermute | solution.py:300
  699.0 10.4 %collective-permute-done.14 = f32[168,512]{1,0:T(8,128)S(1)} collective-permute-done((f32[168,512]{1,0:T(8,128)S(1)}, f32[168,512]{1,0:T(8,128)S(1)}, u32[]{:S(2)}, u32[]{:S(2)}) %collective-permute-start.14) | collective-permute-done | bytes 344096 | tf_op jit(solution)/shard_map/ppermute | solution.py:300
  (604 shorter events, 350.1 us)
Async XLA Ops:
  7.2 166.4 %all-gather.5.cloned.1.call-start = ((), (), s32[]{:S(2)}) async-start(), calls=%async_computation.13 | async-start | bytes 21168128 | tf_op jit(solution)/shard_map/all_gather | solution.py:531
  11.9 263.6 %all-gather.7.cloned.1.call-start = ((), (), s32[]{:S(2)}) async-start(), calls=%async_computation.14 | async-start | bytes 12255232 | tf_op jit(solution)/shard_map/all_gather | solution.py:532
  36.9 37.2 %collective-permute-start.4 = (f32[2,104,512]{2,1,0:T(8,128)S(1)}, f32[2,104,512]{2,1,0:T(8,128)S(1)}, u32[]{:S(2)}, u32[]{:S(2)}) collective-permute-start(f32[2,104,512]{2,1,0:T(8,128)S(1)} %pad_maximum_fusion.24), channel_id=1, source_target_pairs={{0,8},{2,10},{4,12},{6,14},{8,0},{10,2},{12,4},{14,6},{1,9},{3,11}... | collective-permute-start | bytes 1277960 | tf_op jit(solution)/shard_map/ppermute | solution.py:300
  66.9 41.6 %collective-permute-start.2 = (f32[4,104,512]{2,1,0:T(8,128)}, f32[4,104,512]{2,1,0:T(8,128)}, u32[]{:S(2)}, u32[]{:S(2)}) collective-permute-start(f32[4,104,512]{2,1,0:T(8,128)} %pad_maximum_fusion.18), channel_id=1, source_target_pairs={{0,2},{2,0},{4,6},{6,4},{8,10},{10,8},{12,14},{14,12},{1,3},{3,1},... | collective-permute-start | bytes 2555912 | tf_op jit(solution)/shard_map/ppermute | solution.py:300
  75.1 46.5 %collective-permute-start.5 = (f32[4,104,512]{2,1,0:T(8,128)}, f32[4,104,512]{2,1,0:T(8,128)}, u32[]{:S(2)}, u32[]{:S(2)}) collective-permute-start(f32[4,104,512]{2,1,0:T(8,128)} %pad_maximum_fusion.19), channel_id=1, source_target_pairs={{0,4},{2,6},{4,0},{6,2},{8,12},{10,14},{12,8},{14,10},{1,5},{3,7},... | collective-permute-start | bytes 2555912 | tf_op jit(solution)/shard_map/ppermute | solution.py:300
  80.5 54.9 %all-to-all-start.1 = ((f32[16,32,192]{2,1,0:T(8,128)}), f32[16,32,192]{2,1,0:T(8,128)S(1)}, u32[]{:S(2)}, u32[]{:S(2)}) async-start(f32[16,32,192]{2,1,0:T(8,128)} %bitcast.5), calls=%async_computation.1 | async-start | bytes 1048576 | tf_op jit(solution)/shard_map/all_to_all | solution.py:513
  166.5 42.1 %all-to-all-start.6 = ((f32[2,96,512]{2,1,0:T(8,128)}), f32[2,96,512]{2,1,0:T(8,128)S(1)}, u32[]{:S(2)}, u32[]{:S(2)}) async-start(f32[2,96,512]{2,1,0:T(8,128)} %param.31), calls=%async_computation.6 | async-start | bytes 786432 | tf_op jit(solution)/shard_map/all_to_all | solution.py:600
  208.6 81.1 %all-to-all-start.3 = ((f32[8,32,384]{2,1,0:T(8,128)}), f32[8,32,384]{2,1,0:T(8,128)S(1)}, u32[]{:S(2)}, u32[]{:S(2)}) async-start(f32[8,32,384]{2,1,0:T(8,128)} %reshape.612), calls=%async_computation.3 | async-start | bytes 786432 | tf_op jit(solution)/shard_map/all_to_all | solution.py:348
  357.0 175.9 %collective-permute-start.28 = (f32[2,2,2,256,512]{4,3,2,1,0:T(8,128)}, f32[2,2,2,256,512]{4,3,2,1,0:T(8,128)}, u32[]{:S(2)}, u32[]{:S(2)}) collective-permute-start(f32[2,2,2,256,512]{4,3,2,1,0:T(8,128)} %dynamic-slice_bitcast_fusion.1), channel_id=1, source_target_pairs={{0,1},{1,0},{2,3},{3,2},{4,5},{5,4},{6,7},{7,6},{8,9},{9,8},{10,11... | collective-permute-start | bytes 12582920 | tf_op jit(solution)/shard_map/ppermute | solution.py:300
  420.5 78.3 %collective-permute-start.16 = (f32[2,2,2,160,512]{4,3,2,1,0:T(8,128)}, f32[2,2,2,160,512]{4,3,2,1,0:T(8,128)}, u32[]{:S(2)}, u32[]{:S(2)}) collective-permute-start(f32[2,2,2,160,512]{4,3,2,1,0:T(8,128)} %dynamic-slice_bitcast_fusion.3), channel_id=1, source_target_pairs={{0,1},{1,0},{2,3},{3,2},{4,5},{5,4},{6,7},{7,6},{8,9},{9,8},{10,11... | collective-permute-start | bytes 7864328 | tf_op jit(solution)/shard_map/ppermute | solution.py:300
  430.4 35.5 %all-to-all-start.5 = ((f32[2,96,512]{2,1,0:T(8,128)}), f32[2,96,512]{2,1,0:T(8,128)S(1)}, u32[]{:S(2)}, u32[]{:S(2)}) async-start(f32[2,96,512]{2,1,0:T(8,128)} %bitcast.50), calls=%async_computation.5 | async-start | bytes 786432 | tf_op jit(solution)/shard_map/all_to_all | solution.py:702
  454.9 38.7 %collective-permute-start.22 = (f32[2,2,2,144,512]{4,3,2,1,0:T(8,128)}, f32[2,2,2,144,512]{4,3,2,1,0:T(8,128)S(1)}, u32[]{:S(2)}, u32[]{:S(2)}) collective-permute-start(f32[2,2,2,144,512]{4,3,2,1,0:T(8,128)} %dynamic-slice_bitcast_fusion.4), channel_id=1, source_target_pairs={{0,1},{1,0},{2,3},{3,2},{4,5},{5,4},{6,7},{7,6},{8,9},{9,8},{10,11... | collective-permute-start | bytes 7077896 | tf_op jit(solution)/shard_map/ppermute | solution.py:300
  477.5 77.9 %collective-permute-start.10 = (f32[2,2,2,336,512]{4,3,2,1,0:T(8,128)}, f32[2,2,2,336,512]{4,3,2,1,0:T(8,128)}, u32[]{:S(2)}, u32[]{:S(2)}) collective-permute-start(f32[2,2,2,336,512]{4,3,2,1,0:T(8,128)} %dynamic-slice_bitcast_fusion), channel_id=1, source_target_pairs={{0,1},{1,0},{2,3},{3,2},{4,5},{5,4},{6,7},{7,6},{8,9},{9,8},{10,11... | collective-permute-start | bytes 16515080 | tf_op jit(solution)/shard_map/ppermute | solution.py:300
  482.1 32.3 %all-to-all-start.10 = ((f32[8,96,384]{2,1,0:T(8,128)}), f32[8,96,384]{2,1,0:T(8,128)}, u32[]{:S(2)}, u32[]{:S(2)}) async-start(f32[8,96,384]{2,1,0:T(8,128)} %get-tuple-element.54), calls=%async_computation.10 | async-start | bytes 2359296 | tf_op jit(solution)/shard_map/all_to_all | solution.py:345
  497.2 32.4 %collective-permute-start.23 = (f32[2,2,2,72,512]{4,3,2,1,0:T(8,128)}, f32[2,2,2,72,512]{4,3,2,1,0:T(8,128)}, u32[]{:S(2)}, u32[]{:S(2)}) collective-permute-start(f32[2,2,2,72,512]{4,3,2,1,0:T(8,128)} %dynamic-slice_bitcast_fusion.8), channel_id=1, source_target_pairs={{0,16},{16,0},{1,17},{17,1},{2,18},{18,2},{3,19},{19,3},{4,20},{20... | collective-permute-start | bytes 3538952 | tf_op jit(solution)/shard_map/ppermute | solution.py:300
  502.4 47.3 %collective-permute-start.17 = (f32[2,2,160,512]{3,2,1,0:T(8,128)}, f32[2,2,160,512]{3,2,1,0:T(8,128)}, u32[]{:S(2)}, u32[]{:S(2)}) collective-permute-start(f32[2,2,160,512]{3,2,1,0:T(8,128)} %dynamic-slice_bitcast_fusion.7), channel_id=1, source_target_pairs={{0,2},{2,0},{4,6},{6,4},{8,10},{10,8},{12,14},{14,12},{1,3},{3,1},... | collective-permute-start | bytes 3932168 | tf_op jit(solution)/shard_map/ppermute | solution.py:300
  537.6 62.1 %collective-permute-start.29 = (f32[2,2,2,128,512]{4,3,2,1,0:T(8,128)S(1)}, f32[2,2,2,128,512]{4,3,2,1,0:T(8,128)S(1)}, u32[]{:S(2)}, u32[]{:S(2)}) collective-permute-start(f32[2,2,2,128,512]{4,3,2,1,0:T(8,128)S(1)} %dynamic-slice_bitcast_fusion.5), channel_id=1, source_target_pairs={{0,16},{16,0},{1,17},{17,1},{2,18},{18,2},{3,19},{19,3},{4,20},{20... | collective-permute-start | bytes 6291464 | tf_op jit(solution)/shard_map/ppermute | solution.py:300
  551.3 48.2 %collective-permute-start.18 = (f32[2,2,80,512]{3,2,1,0:T(8,128)S(1)}, f32[2,2,80,512]{3,2,1,0:T(8,128)S(1)}, u32[]{:S(2)}, u32[]{:S(2)}) collective-permute-start(f32[2,2,80,512]{3,2,1,0:T(8,128)S(1)} %dynamic-slice_bitcast_fusion.11), channel_id=1, source_target_pairs={{0,16},{16,0},{1,17},{17,1},{2,18},{18,2},{3,19},{19,3},{4,20},{20... | collective-permute-start | bytes 1966088 | tf_op jit(solution)/shard_map/ppermute | solution.py:300
  561.3 83.8 %collective-permute-start.11 = (f32[2,2,336,512]{3,2,1,0:T(8,128)S(1)}, f32[2,2,336,512]{3,2,1,0:T(8,128)S(1)}, u32[]{:S(2)}, u32[]{:S(2)}) collective-permute-start(f32[2,2,336,512]{3,2,1,0:T(8,128)S(1)} %dynamic-slice_bitcast_fusion.2), channel_id=1, source_target_pairs={{0,2},{2,0},{4,6},{6,4},{8,10},{10,8},{12,14},{14,12},{1,3},{3,1},... | collective-permute-start | bytes 8257544 | tf_op jit(solution)/shard_map/ppermute | solution.py:300
  569.2 31.9 %collective-permute-start.27 = (f32[72,512]{1,0:T(8,128)S(1)}, f32[72,512]{1,0:T(8,128)S(1)}, u32[]{:S(2)}, u32[]{:S(2)}) collective-permute-start(f32[72,512]{1,0:T(8,128)S(1)} %bitcast_add_fusion.20), channel_id=1, source_target_pairs={{0,16},{16,0},{1,17},{17,1},{2,18},{18,2},{3,19},{19,3},{4,20},{20... | collective-permute-start | bytes 442376 | tf_op jit(solution)/shard_map/ppermute | solution.py:300
  600.3 43.1 %collective-permute-start.30 = (f32[2,2,128,512]{3,2,1,0:T(8,128)S(1)}, f32[2,2,128,512]{3,2,1,0:T(8,128)S(1)}, u32[]{:S(2)}, u32[]{:S(2)}) collective-permute-start(f32[2,2,128,512]{3,2,1,0:T(8,128)S(1)} %dynamic-slice_bitcast_fusion.9), channel_id=1, source_target_pairs={{0,2},{2,0},{4,6},{6,4},{8,10},{10,8},{12,14},{14,12},{1,3},{3,1},... | collective-permute-start | bytes 3145736 | tf_op jit(solution)/shard_map/ppermute | solution.py:300
  609.4 39.1 %collective-permute-start.20 = (f32[80,512]{1,0:T(8,128)S(1)}, f32[80,512]{1,0:T(8,128)S(1)}, u32[]{:S(2)}, u32[]{:S(2)}) collective-permute-start(f32[80,512]{1,0:T(8,128)S(1)} %dynamic-slice_bitcast_fusion.19), channel_id=1, source_target_pairs={{0,8},{2,10},{4,12},{6,14},{8,0},{10,2},{12,4},{14,6},{1,9},{3,11}... | collective-permute-start | bytes 491528 | tf_op jit(solution)/shard_map/ppermute | solution.py:300
  645.9 36.4 %collective-permute-start.12 = (f32[2,2,168,512]{3,2,1,0:T(8,128)S(1)}, f32[2,2,168,512]{3,2,1,0:T(8,128)S(1)}, u32[]{:S(2)}, u32[]{:S(2)}) collective-permute-start(f32[2,2,168,512]{3,2,1,0:T(8,128)S(1)} %dynamic-slice_bitcast_fusion.6), channel_id=1, source_target_pairs={{0,16},{16,0},{1,17},{17,1},{2,18},{18,2},{3,19},{19,3},{4,20},{20... | collective-permute-start | bytes 4128776 | tf_op jit(solution)/shard_map/ppermute | solution.py:300
  648.5 31.6 %collective-permute-start.21 = (f32[80,512]{1,0:T(8,128)S(1)}, f32[80,512]{1,0:T(8,128)S(1)}, u32[]{:S(2)}, u32[]{:S(2)}) collective-permute-start(f32[80,512]{1,0:T(8,128)S(1)} %bitcast_add_fusion.19), channel_id=1, source_target_pairs={{0,16},{16,0},{1,17},{17,1},{2,18},{18,2},{3,19},{19,3},{4,20},{20... | collective-permute-start | bytes 491528 | tf_op jit(solution)/shard_map/ppermute | solution.py:300
  (156 other events, 1449.5 us)
Sparse Core Ops, SparseCore 0:
  12.0 161.5 all-gather.4
  175.9 99.5 all-gather.6

commit v2 on v1

v2 whole, which is shorter than its diff:
```python
import functools
import math

import jax
import jax.numpy as jnp
import numpy as np
from jax import lax
from jax.experimental import pallas as pl
from jax.experimental.pallas import tpu as pltpu
from jax.sharding import Mesh, PartitionSpec as P

HEADS = 8
HEAD_DIM = 64
D = HEADS * HEAD_DIM
norm_eps = 1e-05
masked_score = -1e30
momentum_decay = 0.9
average_decay = 0.9
F32 = jnp.float32
BF16 = jnp.bfloat16
VMEM_LIMIT = 56 << 20
ROOT = math.sqrt(2.0 / math.pi)
CUBE = 0.044715
CHIP, CORE, SIDE, COLUMN, LENGTH, SHORT_LENGTH = range(6)


def split(value):
    high = value.astype(BF16)
    return high, (value - high.astype(F32)).astype(BF16)


def dot(a, b, dims):
    return lax.dot_general(a, b, (dims, ((), ())), preferred_element_type=F32)


NN = ((1,), (0,))
NT = ((1,), (1,))
TN = ((0,), (0,))


def matmul(left, right, dims=NN):
    rows = left.shape[0]
    high, low = split(left)
    right_high, right_low = split(right)
    both = dot(jnp.concatenate([high, low], axis=0), right_high, dims)
    return both[:rows] + both[rows:] + dot(high, right_low, dims)


def outer(left, right):
    columns = right.shape[1]
    high, low = split(left)
    right_high, right_low = split(right)
    both = dot(high, jnp.concatenate([right_high, right_low], axis=1), TN)
    return both[:, :columns] + both[:, columns:] + dot(low, right_high, TN)


def normalized(values):
    centred = values - jnp.mean(values, axis=-1, keepdims=True)
    variance = jnp.mean(centred * centred, axis=-1, keepdims=True)
    scale = lax.rsqrt(variance + norm_eps)
    return centred * scale, scale


def normalized_grad(grad, gain, normed, scale):
    inner = grad * gain
    along = jnp.mean(inner * normed, axis=-1, keepdims=True)
    return scale * (inner - jnp.mean(inner, axis=-1, keepdims=True) - normed * along)


def gelu_parts(u):
    curve = jnp.tanh(ROOT * (u + CUBE * u * u * u))
    return curve, 0.5 * u * (1.0 + curve)


def gelu_slope(u, curve):
    inner = ROOT * (1.0 + 3.0 * CUBE * u * u)
    return 0.5 * (1.0 + curve) + 0.5 * u * (1.0 - curve * curve) * inner


def rope_tables(rows):
    half = HEAD_DIM // 2
    freq = (10000.0 ** (-2.0 * np.arange(half, dtype=np.float32) / HEAD_DIM)).astype(np.float32)
    angles = np.arange(rows, dtype=np.float32)[:, None] * freq[None, :]
    cosine = np.cos(angles).astype(np.float32)
    sine = np.sin(angles).astype(np.float32)
    both = np.concatenate([cosine, cosine], axis=1)
    signed = np.concatenate([-sine, sine], axis=1)
    return (
        np.concatenate([both, both], axis=1),
        np.concatenate([signed, signed], axis=1),
        np.ascontiguousarray(cosine.T),
        np.ascontiguousarray(sine.T),
    )


def swap_halves(pair):
    half = HEAD_DIM // 2
    width = pair.shape[1]
    lane = lax.broadcasted_iota(jnp.int32, pair.shape, 1) % HEAD_DIM
    ahead = pltpu.roll(pair, width - half, 1)
    behind = pltpu.roll(pair, half, 1)
    return jnp.where(lane < half, ahead, behind)


def rows_from_heads(ref, parts):
    pair = 2 * HEAD_DIM
    top, bottom = [], []
    for part in range(parts):
        lanes = slice(part * pair, (part + 1) * pair)
        for k in range(HEADS // 2):
            even, odd = ref[2 * k, :, lanes], ref[2 * k + 1, :, lanes]
            first = lax.broadcasted_iota(jnp.int32, even.shape, 1) < HEAD_DIM
            top.append(jnp.where(first, even, pltpu.roll(odd, HEAD_DIM, 1)))
            bottom.append(jnp.where(first, pltpu.roll(even, HEAD_DIM, 1), odd))
    return jnp.concatenate(
        [jnp.concatenate(top, axis=1), jnp.concatenate(bottom, axis=1)], axis=0
    )


def rows_to_heads(rows, ref, parts):
    pair = 2 * HEAD_DIM
    half = rows.shape[0] // 2
    for part in range(parts):
        lanes = slice(part * pair, (part + 1) * pair)
        for k in range(HEADS // 2):
            at = part * D + k * pair
            top, bottom = rows[:half, at : at + pair], rows[half:, at : at + pair]
            first = lax.broadcasted_iota(jnp.int32, top.shape, 1) < HEAD_DIM
            ref[2 * k, :, lanes] = jnp.where(first, top, pltpu.roll(bottom, HEAD_DIM, 1))
            ref[2 * k + 1, :, lanes] = jnp.where(first, pltpu.roll(top, HEAD_DIM, 1), bottom)


def allowed_keys(first_row, rows, keys, length):
    key_pos = lax.broadcasted_iota(jnp.int32, (keys, rows), 0)
    query_pos = lax.broadcasted_iota(jnp.int32, (keys, rows), 1) + first_row
    return (key_pos <= query_pos) & (key_pos < length)


def attend_rows(raw, length, cos_ref, sin_ref, out_refs, rows, step, half_rows):
    packed_ref, turned_ref, lse_ref, qcat_ref, kcat_ref, vcat_ref = out_refs
    scale = HEAD_DIM ** (-0.5)
    for start in range(0, rows, step):
        part = slice(start, start + step)
        pair = raw[part, : 2 * HEAD_DIM]
        pair = pair * cos_ref[part, :] + swap_halves(pair) * sin_ref[part, :]
        lane = lax.broadcasted_iota(jnp.int32, pair.shape, 1)
        pair = jnp.where(lane < HEAD_DIM, pair * scale, pair)
        high, low = split(pair)
        qh, kh = high[:, :HEAD_DIM], high[:, HEAD_DIM:]
        ql, kl = low[:, :HEAD_DIM], low[:, HEAD_DIM:]
        vh, vl = split(raw[part, 2 * HEAD_DIM :])
        qcat_ref[part, :] = jnp.concatenate([qh, ql, qh], axis=1)
        kcat_ref[part, :] = jnp.concatenate([kh, kh, kl], axis=1)
        vcat_ref[part, :] = jnp.concatenate([vh, vh, vl], axis=1)
    value_pair = jnp.transpose(vcat_ref[:, HEAD_DIM:].astype(F32)).astype(BF16)
    value_high = value_pair[:HEAD_DIM]
    for start in range(0, rows, step):
        part = slice(start, start + step)
        keys = start + step
        scores = dot(kcat_ref[:keys, :], qcat_ref[part, :], NT)
        scores = jnp.where(allowed_keys(start, step, keys, length), scores, masked_score)
        row_max = jnp.max(scores, axis=0, keepdims=True)
        weights = jnp.exp(scores - row_max)
        total = jnp.sum(weights, axis=0, keepdims=True)
        wh, wl = split(weights)
        summed = dot(value_pair[:, :keys], wh, NN)
        summed = summed[:HEAD_DIM] + summed[HEAD_DIM:] + dot(value_high[:, :keys], wl, NN)
        turned = summed / total
        lse_ref[:, part] = jnp.broadcast_to(row_max + jnp.log(total), (8, step))
        turned_ref[:, part] = turned
    attended = jnp.transpose(
        jnp.concatenate([turned_ref[...], turned_ref[...]], axis=0)
    ).reshape(rows // (2 * half_rows), 2, half_rows, 2 * HEAD_DIM)
    lane = lax.broadcasted_iota(jnp.int32, attended[:, 0].shape, 2)
    packed_ref[...] = jnp.where(lane < HEAD_DIM, attended[:, 0], attended[:, 1])


def gathered_blocks(ids_ref, refs, distances, half_rows):
    for number, ref in enumerate(refs):
        side, part = divmod(number, 2)
        count = ref.shape[0]
        for slot in range(count):
            chip = ids_ref[CHIP] ^ distances[side][part * count + slot]
            first = pl.multiple_of((chip * 2 + side) * half_rows, 8)
            yield ref, slot, first


def first_attend_kernel(half_rows, step, distances, ids_ref, *refs):
    x_refs, (w_ref, cos_ref, sin_ref) = refs[:4], refs[4:7]
    out_refs, norm_ref, raw = refs[7:13], refs[13], refs[14]
    rows = raw.shape[0]
    total = sum(jnp.sum(ref[:, half_rows:, :], axis=0) for ref in x_refs)
    norm_ref[...] = total
    gain, shift = total[0:1], total[1:2]
    wh, wl = split(w_ref[...])
    for ref, slot, first in gathered_blocks(ids_ref, x_refs, distances, half_rows):
        hh, hl = split(normalized(ref[slot, :half_rows, :])[0] * gain + shift)
        raw[pl.ds(first, half_rows), :] = dot(hh, wh, NN) + dot(hh, wl, NN) + dot(hl, wh, NN)
    attend_rows(raw, ids_ref[LENGTH], cos_ref, sin_ref, out_refs, rows, step, half_rows)


def unpack_rows(packed_ref, raw, half_rows, parts):
    chips = packed_ref.shape[0]
    for chip in range(chips):
        for side in range(2):
            first = (chip * 2 + side) * half_rows
            pieces = [
                packed_ref[chip, :, (2 * part + side) * HEAD_DIM : (2 * part + side + 1) * HEAD_DIM]
                for part in range(parts)
            ]
            piece = pieces[0] if parts == 1 else jnp.concatenate(pieces, axis=1)
            raw[first : first + half_rows, :] = piece


def second_attend_kernel(half_rows, step, ids_ref, packed_ref, cos_ref, sin_ref, *refs):
    out_refs, raw = refs[:6], refs[6]
    rows = packed_ref.shape[0] * 2 * half_rows
    unpack_rows(packed_ref, raw, half_rows, 3)
    attend_rows(raw, ids_ref[SHORT_LENGTH], cos_ref, sin_ref, out_refs, rows, step, half_rows)


def attend_grad(
    rows, step, half_rows, length, refs, grad_ref, tables, out_ref, scratch
):
    qcat_ref, kcat_ref, vcat_ref, turned_ref, lse_ref = refs
    cos_ref, sin_ref, cos_t_ref, sin_t_ref = tables
    grad_rows, dk_acc, dv_acc, dq_t, dqkv = scratch
    scale = HEAD_DIM ** (-0.5)
    unpack_rows(grad_ref, grad_rows, half_rows, 1)
    key_pair = jnp.transpose(kcat_ref[:, HEAD_DIM:].astype(F32)).astype(BF16)
    key_high = key_pair[:HEAD_DIM]
    dk_acc[...] = jnp.zeros_like(dk_acc)
    dv_acc[...] = jnp.zeros_like(dv_acc)
    for start in range(0, rows, step):
        part = slice(start, start + step)
        keys = start + step
        grad = grad_rows[part, :]
        gh, gl = split(grad)
        gcat = jnp.concatenate([gh, gl, gh], axis=1)
        grad_t = jnp.transpose(jnp.concatenate([grad, grad], axis=1))[:HEAD_DIM]
        delta = jnp.sum(grad_t * turned_ref[:, part], axis=0, keepdims=True)
        scores = dot(kcat_ref[:keys, :], qcat_ref[part, :], NT)
        probs = jnp.where(
            allowed_keys(start, step, keys, length), jnp.exp(scores - lse_ref[0:1, part]), 0.0
        )
        grad_probs = dot(vcat_ref[:keys, :], gcat, NT)
        grad_scores = probs * (grad_probs - delta)
        ph, pw = split(probs)
        sh, sl = split(grad_scores)
        dv_acc[:keys, :] += dot(ph, gcat[:, : 2 * HEAD_DIM], NN)
        dv_acc[:keys, :HEAD_DIM] += dot(pw, gh, NN)
        dk_acc[:keys, :] += dot(sh, qcat_ref[part, : 2 * HEAD_DIM], NN)
        dk_acc[:keys, :HEAD_DIM] += dot(sl, qcat_ref[part, :HEAD_DIM], NN)
        turned = dot(key_pair[:, :keys], sh, NN)
        turned = turned[:HEAD_DIM] + turned[HEAD_DIM:] + dot(key_high[:, :keys], sl, NN)
        dq_t[:, part] = turned * scale
    half = HEAD_DIM // 2
    low, high = dq_t[:half, :], dq_t[half:, :]
    back_low = low * cos_t_ref[...] + high * sin_t_ref[...]
    back_high = high * cos_t_ref[...] - low * sin_t_ref[...]
    dq = jnp.transpose(jnp.concatenate([back_low, back_high, back_low, back_high], axis=0))
    for start in range(0, rows, step):
        part = slice(start, start + step)
        dk = dk_acc[part, :HEAD_DIM] + dk_acc[part, HEAD_DIM:]
        dk = jnp.concatenate([dk, dk], axis=1)
        dk = dk * cos_ref[part, :] - swap_halves(dk) * sin_ref[part, :]
        dv = dv_acc[part, :HEAD_DIM] + dv_acc[part, HEAD_DIM:]
        dqkv[part, :] = jnp.concatenate([dq[part, :HEAD_DIM], dk[:, :HEAD_DIM], dv], axis=1)
    chips = out_ref.shape[0]
    for chip in range(chips):
        first = chip * 2 * half_rows
        top = dqkv[first : first + half_rows, :]
        bottom = dqkv[first + half_rows : first + 2 * half_rows, :]
        pieces = []
        for part in range(3):
            lanes = slice(part * HEAD_DIM, (part + 1) * HEAD_DIM)
            pieces += [top[:, lanes], bottom[:, lanes]]
        out_ref[chip, :, :] = jnp.concatenate(pieces, axis=1)


def second_grad_kernel(half_rows, step, ids_ref, *refs):
    saved, grad_ref, tables, out_ref, scratch = refs[:5], refs[5], refs[6:10], refs[10], refs[11:]
    rows = saved[0].shape[0]
    length = ids_ref[SHORT_LENGTH]
    attend_grad(rows, step, half_rows, length, saved, grad_ref, tables, out_ref, scratch)


def first_grad_kernel(half_rows, step, distances, ids_ref, *refs):
    x_refs, saved, grad_ref, tables = refs[:4], refs[4:9], refs[9], refs[10:14]
    out_ref, m_ref, scratch = refs[14], refs[15], refs[16:]
    rows = saved[0].shape[0]
    length = ids_ref[LENGTH]
    attend_grad(rows, step, half_rows, length, saved, grad_ref, tables, out_ref, scratch[:5])
    dqkv, nh_ref, nl_ref = scratch[4:]
    for ref, slot, first in gathered_blocks(ids_ref, x_refs, distances, half_rows):
        nh, nl = split(normalized(ref[slot, :half_rows, :])[0])
        nh_ref[pl.ds(first, half_rows), :] = nh
        nl_ref[pl.ds(first, half_rows), :] = nl
    dh, dl = split(dqkv[...])
    nh = nh_ref[...]
    product = dot(nh, dh, TN) + dot(nh, dl, TN) + dot(nl_ref[...], dh, TN)
    owners, rows_each = m_ref.shape[0], m_ref.shape[1] - 8
    column = jnp.sum(dqkv[...], axis=0, keepdims=True)
    m_ref[:, :rows_each, :] = product.reshape(owners, rows_each, 3 * HEAD_DIM)
    m_ref[:, rows_each:, :] = jnp.broadcast_to(column[None], (owners, 8, 3 * HEAD_DIM))


class Loader:
    def __init__(self, ids_ref, sems):
        self.ids_ref = ids_ref
        self.sems = sems
        self.used = 0

    def start(self, src, dst):
        sem = self.sems.at[self.used]
        self.used += 1
        copy = pltpu.make_async_copy(src, dst, sem)
        copy.start()
        return copy

    def columns(self, gathered, unit, dst):
        return [[self.start(gathered.at[:, unit + k], dst.at[k])] for k in range(dst.shape[0])]

    def rows(self, gathered, unit, dst):
        run = dst.shape[0] // 4
        waits = []
        for k in range(4):
            owners = pl.ds(k * run, run)
            waits.append([self.start(gathered.at[owners, unit : unit + 4], dst.at[owners])])
        return waits


def ready(waits):
    for copy in waits:
        copy.wait()


def square(ref):
    return ref[...].reshape(D, D)


def pick(first, zero, one):
    return jnp.where(first, zero, one)


class Halves:
    def __init__(self, ids_ref, keep_ref, send_ref):
        self.zero = ids_ref[CORE] == 0
        self.keep_ref, self.send_ref = keep_ref, send_ref
        self.at = 0

    def put(self, keep, send):
        width = keep.shape[1]
        self.keep_ref[:, self.at : self.at + width] = keep
        self.send_ref[:, self.at : self.at + width] = send
        self.at += width

    def whole(self, value):
        self.put(value, value)

    def halved(self, zero, one):
        self.put(pick(self.zero, zero, one), pick(self.zero, one, zero))

    def granules(self, value, size, at):
        for k in range(value.shape[1] // (2 * size)):
            zero = value[:, 2 * k * size : (2 * k + 1) * size]
            one = value[:, (2 * k + 1) * size : (2 * k + 2) * size]
            lanes = slice(at + k * size, at + (k + 1) * size)
            self.keep_ref[:, lanes] = pick(self.zero, zero, one)
            self.send_ref[:, lanes] = pick(self.zero, one, zero)


def first_dense_kernel(
    ids_ref, stream_ref, got_ref, norm_ref, g_ref, full_ref, mixed_ref, u_ref, proj, up, down, sems
):
    load = Loader(ids_ref, sems)
    proj_wait = load.columns(g_ref, 0, proj)
    up_wait = load.columns(g_ref, 1, up)
    down_wait = load.rows(g_ref, 5, down)
    attended = rows_from_heads(got_ref, 1)
    ready(proj_wait[0])
    mixed = stream_ref[...] + matmul(attended, square(proj))
    mixed_ref[...] = mixed
    inner = normalized(mixed)[0] * norm_ref[2:3, :] + norm_ref[3:4, :]
    run = down.shape[0] // 4
    result = mixed
    for k in range(4):
        ready(up_wait[k])
        u = matmul(inner, up[k].reshape(D, D))
        u_ref[:, k * D : (k + 1) * D] = u
        hidden = gelu_parts(u)[1]
        ready(down_wait[k])
        result = result + matmul(hidden, down[k * run : (k + 1) * run].reshape(D, D))
    full_ref[...] = result


def shorten_kernel(
    ids_ref, full_ref, tail_ref, norm_ref, g_ref, short_ref, packed_ref, pool, qkv, moved, sems
):
    load = Loader(ids_ref, sems)
    pool_wait = load.columns(g_ref, 9, pool)
    qkv_wait = load.columns(g_ref, 12, qkv)
    shift_rows(full_ref, tail_ref, moved)
    rows = short_ref.shape[0]
    short = jnp.zeros((rows, D), F32)
    for i in range(3):
        ready(pool_wait[i])
        short = short + matmul(load_thirds(moved, 6 + i, rows), pool[i].reshape(D, D))
    short_ref[...] = short
    inner = normalized(short)[0] * norm_ref[4:5, :] + norm_ref[5:6, :]
    parts = []
    for i in range(3):
        ready(qkv_wait[i])
        parts.append(matmul(inner, qkv[i].reshape(D, D)))
    rows_to_heads(jnp.concatenate(parts, axis=1), packed_ref, 3)


LANES = 128
LANE_BLOCKS = D // LANES


def shift_rows(full_ref, tail_ref, moved):
    rows = full_ref.shape[0]
    for k in range(LANE_BLOCKS):
        lanes = slice(k * LANES, (k + 1) * LANES)
        moved[k, 6:8, :] = tail_ref[:, lanes]
        moved[k, 8 : 8 + rows, :] = full_ref[:, lanes]


def load_thirds(buffer, start, rows):
    pieces = [buffer[k, pl.ds(start, rows, stride=3), :] for k in range(LANE_BLOCKS)]
    return jnp.concatenate(pieces, axis=1)


def store_thirds(buffer, start, value):
    rows = value.shape[0]
    for k in range(LANE_BLOCKS):
        buffer[k, pl.ds(start, rows, stride=3), :] = value[:, k * LANES : (k + 1) * LANES]


def to_blocks(value, buffer):
    for k in range(LANE_BLOCKS):
        buffer[k] = value[:, k * LANES : (k + 1) * LANES]


def from_blocks(buffer):
    return jnp.concatenate([buffer[k] for k in range(LANE_BLOCKS)], axis=1)


def kept_cotangent(ids_ref, cot_ref):
    rows = cot_ref.shape[0]
    position = lax.broadcasted_iota(jnp.int32, cot_ref.shape, 0) + ids_ref[CHIP] * rows
    return jnp.where(position < ids_ref[LENGTH], cot_ref[...], 0.0)


def ffn_backward(grad, mixed, gain, u_of, curves, up_of, down_of, proj_of, halves, size):
    normed, scale = normalized(mixed)
    halves.whole(normed)
    base = halves.at
    halves.at += 4 * D
    halves.whole(grad)
    inner = jnp.zeros_like(mixed)
    each = D // 2
    for k in range(4):
        u = u_of(k)
        curve, hidden = curves(k, u)
        du = matmul(grad, down_of(k), NT) * gelu_slope(u, curve)
        halves.granules(du, size, base + k * each)
        halves.granules(hidden, size, base + 2 * D + k * each)
        inner = inner + matmul(du, up_of(k), NT)
    grad_mixed = grad + normalized_grad(inner, gain, normed, scale)
    return grad_mixed, matmul(grad_mixed, proj_of(), NT)


def middle_kernel(size, *refs):
    (ids_ref, short_ref, got_ref, norm_ref, full_ref, cot_ref, g_ref), refs = refs[:7], refs[7:]
    late_ref, refs = refs[0], refs[1:]
    (act_ref, grad_ref, mixed_ref, keep_ref, send_ref), refs = refs[:5], refs[5:]
    proj, up, down, pool, kept, act, sems = refs
    load = Loader(ids_ref, sems)
    proj_wait = load.columns(g_ref, 15, proj)
    up_wait = load.columns(late_ref, 0, up)
    down_wait = load.rows(late_ref, 4, down)
    pool_wait = load.columns(g_ref, 16, pool)
    to_blocks(kept_cotangent(ids_ref, cot_ref), kept)
    to_blocks(full_ref[...], act)
    attended = rows_from_heads(got_ref, 1)
    run = down.shape[0] // 4
    rows = short_ref.shape[0]
    up_of = lambda k: up[k].reshape(D, D)
    down_of = lambda k: down[k * run : (k + 1) * run].reshape(D, D)
    ready(proj_wait[0])
    mixed = short_ref[...] + matmul(attended, square(proj))
    gain = norm_ref[6:7, :]
    inner = normalized(mixed)[0] * gain + norm_ref[7:8, :]
    for wait in up_wait:
        ready(wait)
    us = [matmul(inner, up_of(k)) for k in range(4)]
    gelus = [gelu_parts(u) for u in us]
    for wait in down_wait:
        ready(wait)
    result = mixed
    for k in range(4):
        result = result + matmul(gelus[k][1], down_of(k))
    grad = jnp.zeros((rows, D), F32)
    groups = []
    for i in range(3):
        ready(pool_wait[i])
        tap = pool[i].reshape(D, D)
        store_thirds(act, i, load_thirds(act, i, rows) + matmul(result, tap))
        groups.append(load_thirds(kept, i, rows))
        grad = grad + matmul(groups[i], tap, NT)
    act_ref[...] = from_blocks(act)
    halves = Halves(ids_ref, keep_ref, send_ref)
    grad_mixed, grad_attended = ffn_backward(
        grad,
        mixed,
        gain,
        lambda k: us[k],
        lambda k, u: gelus[k],
        up_of,
        down_of,
        lambda: square(proj),
        halves,
        size,
    )
    rows_to_heads(grad_attended, grad_ref, 1)
    mixed_ref[...] = grad_mixed
    halves.whole(attended)
    halves.halved(grad_mixed[:, : D // 2], grad_mixed[:, D // 2 :])
    halves.whole(result)
    wide = jnp.concatenate(groups, axis=1)
    halves.halved(wide[:, : 3 * D // 2], wide[:, 3 * D // 2 :])


def lengthen_grad_kernel(
    ids_ref,
    got_ref,
    short_ref,
    mixed_ref,
    norm_ref,
    full_ref,
    tail_ref,
    g_ref,
    shifted_ref,
    keep_ref,
    send_ref,
    pool,
    qkv,
    moved,
    back,
    sems,
):
    load = Loader(ids_ref, sems)
    qkv_wait = load.columns(g_ref, 12, qkv)
    pool_wait = load.columns(g_ref, 9, pool)
    dqkv = rows_from_heads(got_ref, 3)
    rows = short_ref.shape[0]
    normed, scale = normalized(short_ref[...])
    inner = jnp.zeros((rows, D), F32)
    for i in range(3):
        ready(qkv_wait[i])
        inner = inner + matmul(dqkv[:, i * D : (i + 1) * D], qkv[i].reshape(D, D), NT)
    grad = mixed_ref[...] + normalized_grad(inner, norm_ref[4:5, :], normed, scale)
    for i in range(3):
        ready(pool_wait[i])
        store_thirds(back, i, matmul(grad, pool[i].reshape(D, D), NT))
    shifted_ref[...] = from_blocks(back)
    shift_rows(full_ref, tail_ref, moved)
    halves = Halves(ids_ref, keep_ref, send_ref)
    halves.whole(normed)
    halves.halved(dqkv[:, : 3 * D // 2], dqkv[:, 3 * D // 2 :])
    for i in range(3):
        halves.whole(load_thirds(moved, 6 + i, rows))
    halves.halved(grad[:, : D // 2], grad[:, D // 2 :])


def first_dense_grad_kernel(
    size,
    ids_ref,
    shifted_ref,
    next_ref,
    cot_ref,
    mixed_in_ref,
    u_ref,
    got_ref,
    norm_ref,
    g_ref,
    grad_ref,
    mixed_ref,
    keep_ref,
    send_ref,
    proj,
    up,
    down,
    moved,
    sems,
):
    load = Loader(ids_ref, sems)
    down_wait = load.rows(g_ref, 5, down)
    up_wait = load.columns(g_ref, 1, up)
    proj_wait = load.columns(g_ref, 0, proj)
    rows = cot_ref.shape[0]
    moved[:rows, :] = shifted_ref[...]
    moved[rows : rows + 2, :] = next_ref[...]
    grad = kept_cotangent(ids_ref, cot_ref) + moved[2 : 2 + rows, :]
    run = down.shape[0] // 4

    def up_of(k):
        ready(up_wait[k])
        return up[k].reshape(D, D)

    def down_of(k):
        ready(down_wait[k])
        return down[k * run : (k + 1) * run].reshape(D, D)

    def proj_of():
        ready(proj_wait[0])
        return square(proj)

    halves = Halves(ids_ref, keep_ref, send_ref)
    grad_mixed, grad_attended = ffn_backward(
        grad,
        mixed_in_ref[...],
        norm_ref[2:3, :],
        lambda k: u_ref[:, k * D : (k + 1) * D],
        lambda k, u: gelu_parts(u),
        up_of,
        down_of,
        proj_of,
        halves,
        size,
    )
    rows_to_heads(grad_attended, grad_ref, 1)
    mixed_ref[...] = grad_mixed
    halves.whole(rows_from_heads(got_ref, 1))
    halves.halved(grad_mixed[:, : D // 2], grad_mixed[:, D // 2 :])


def input_grad_kernel(
    ids_ref, got_ref, stream_ref, mixed_ref, norm_ref, g_ref, out_ref, qkv, sems
):
    load = Loader(ids_ref, sems)
    qkv_wait = load.columns(g_ref, 0, qkv)
    dqkv = rows_from_heads(got_ref, 3)
    normed, scale = normalized(stream_ref[...])
    inner = jnp.zeros_like(normed)
    for i in range(3):
        ready(qkv_wait[i])
        inner = inner + matmul(dqkv[:, i * D : (i + 1) * D], qkv[i].reshape(D, D), NT)
    out_ref[...] = mixed_ref[...] + normalized_grad(inner, norm_ref[0:1, :], normed, scale)


class Factors:
    def __init__(self, keep_ref, got_ref):
        self.keep_ref, self.got_ref = keep_ref, got_ref
        self.at = 0

    def take(self, width):
        lanes = slice(self.at, self.at + width)
        self.at += width
        return jnp.concatenate([self.keep_ref[:, lanes], self.got_ref[:, lanes]], axis=0)


def side_halves(ids_ref, value):
    width = value.shape[1] // 2
    zero = ids_ref[SIDE] == 0
    first, second = value[:, :width], value[:, width:]
    return pick(zero, first, second), pick(zero, second, first)


def place_by_column(ids_ref, ref, rows, block, ranks):
    for depth in range(4):
        for column in range(2):
            for rank in range(ranks):
                chip = (depth * 2 + column) * ranks + rank
                ref[column ^ ids_ref[COLUMN], depth * ranks + rank, rows, :] = block(chip)


def packed_rows(rows):
    count = rows.shape[0] // 4
    return jnp.concatenate([rows[i * count : (i + 1) * count] for i in range(4)], axis=1)


def place_blocks(ids_ref, ref, at, product, each, ranks):
    rows = slice(at, at + each)
    place_by_column(
        ids_ref, ref, rows, lambda chip: product[chip * each : (chip + 1) * each], ranks
    )
    return at + each


def place_sums(ids_ref, ref, at, value, ranks):
    total = jnp.broadcast_to(jnp.sum(value, axis=0, keepdims=True), (8, value.shape[1]))
    place_by_column(ids_ref, ref, slice(at, at + 8), lambda chip: total, ranks)
    return at + 8


def place_packed(ids_ref, ref, at, product, each, ranks):
    rows = slice(at, at + each // 4)
    place_by_column(
        ids_ref,
        ref,
        rows,
        lambda chip: packed_rows(product[chip * each : (chip + 1) * each]),
        ranks,
    )
    return at + each // 4


def place_by_side(ids_ref, refs, at, products, each, ranks):
    zero = ids_ref[COLUMN] == 0
    for depth in range(4):
        for rank in range(ranks):
            first = ((depth * 2) * ranks + rank) * each
            second = ((depth * 2 + 1) * ranks + rank) * each
            place = depth * ranks + rank
            for side in range(2):
                far = side ^ ids_ref[SIDE]
                one = products[side][first : first + each]
                two = products[side][second : second + each]
                refs[0][place, far, at : at + each, :] = pick(zero, one, two)
                refs[1][place, far, at : at + each, :] = pick(zero, two, one)
    return at + each


def middle_products_kernel(ranks, size, each, ids_ref, keep_ref, got_ref, *refs):
    up_refs, down_refs = refs[:2], refs[2:]
    factors = Factors(keep_ref, got_ref)
    normed, du, hidden, grad = (factors.take(w * D) for w in (1, 2, 2, 1))
    attended, grad_mixed = factors.take(D), factors.take(D // 2)
    for ref, half, narrow in zip(
        up_refs, side_halves(ids_ref, du), side_halves(ids_ref, grad_mixed)
    ):
        at = place_blocks(ids_ref, ref, 0, outer(normed, half), each, ranks)
        at = place_sums(ids_ref, ref, at, half, ranks)
        place_packed(ids_ref, ref, at, outer(attended, narrow), each, ranks)
    product = outer(hidden, grad).reshape(D // each, 2, size // 2, D)
    sides = [product[:, side].reshape(-1, D) for side in range(2)]
    place_by_side(ids_ref, down_refs, 0, sides, size // 2, ranks)


def first_products_kernel(ranks, size, each, ids_ref, keep_ref, got_ref, *refs):
    factors = Factors(keep_ref, got_ref)
    normed, du, hidden, grad = (factors.take(w * D) for w in (1, 2, 2, 1))
    attended, grad_mixed = factors.take(D), factors.take(D // 2)
    product = outer(hidden, grad).reshape(D // each, 2, size // 2, D)
    zero = ids_ref[SIDE] == 0
    downs = [
        pick(zero, product[:, far], product[:, 1 - far]).reshape(-1, D) for far in range(2)
    ]
    for ref, half, narrow, down in zip(
        refs, side_halves(ids_ref, du), side_halves(ids_ref, grad_mixed), downs
    ):
        at = place_blocks(ids_ref, ref, 0, outer(normed, half), each, ranks)
        at = place_sums(ids_ref, ref, at, half, ranks)
        at = place_blocks(ids_ref, ref, at, down, size // 2, ranks)
        place_packed(ids_ref, ref, at, outer(attended, narrow), each, ranks)


def shorten_products_kernel(
    ranks, each, ids_ref, keep_ref, got_ref, up_keep_ref, up_got_ref, *refs
):
    qkv_refs, pool_refs = refs[:2], refs[2:]
    factors = Factors(keep_ref, got_ref)
    normed, dqkv = factors.take(D), factors.take(3 * D // 2)
    shifted = [factors.take(D) for _ in range(3)]
    grad = factors.take(D // 2)
    for ref, half in zip(qkv_refs, side_halves(ids_ref, dqkv)):
        at = place_blocks(ids_ref, ref, 0, outer(normed, half), each, ranks)
        place_sums(ids_ref, ref, at, half, ranks)
    narrow, wide = D // 4, 3 * D // 4
    taps = [
        jnp.concatenate(
            [outer(rows, grad[:, side * narrow : (side + 1) * narrow]) for rows in shifted],
            axis=1,
        )
        for side in range(2)
    ]
    at = place_by_side(ids_ref, pool_refs, 0, taps, each, ranks)
    factors = Factors(up_keep_ref, up_got_ref)
    factors.at = 15 * D // 2
    short, groups = factors.take(D), factors.take(3 * D // 2)
    taps = [outer(short, groups[:, side * wide : (side + 1) * wide]) for side in range(2)]
    place_by_side(ids_ref, pool_refs, at, taps, each, ranks)


PER_US = 3.3e+09
SMEM = pl.BlockSpec(memory_space=pltpu.SMEM)
VMEM = pl.BlockSpec(memory_space=pltpu.VMEM)
ANY = pl.BlockSpec(memory_space=pl.ANY)


def attend_outs(rows, half_rows):
    width = 3 * HEAD_DIM
    return [
        shape(rows // (2 * half_rows), half_rows, 2 * HEAD_DIM),
        shape(HEAD_DIM, rows),
        shape(8, rows),
        jax.ShapeDtypeStruct((rows, width), BF16),
        jax.ShapeDtypeStruct((rows, width), BF16),
        jax.ShapeDtypeStruct((rows, width), BF16),
    ]


def shape(*dims):
    return jax.ShapeDtypeStruct(dims, F32)


def call(time, kernel, outs, scratch, ids, args, weights=(), copies=0):
    scratch = list(scratch)
    if copies:
        scratch.append(pltpu.SemaphoreType.DMA((copies,)))
    return pl.pallas_call(
        kernel,
        out_shape=list(outs),
        in_specs=[SMEM] + [VMEM] * len(args) + [ANY] * len(weights),
        out_specs=[VMEM] * len(outs),
        scratch_shapes=scratch,
        compiler_params=pltpu.CompilerParams(vmem_limit_bytes=VMEM_LIMIT),
        cost_estimate=pl.CostEstimate(
            flops=int(time * PER_US), bytes_accessed=0, transcendentals=0
        ),
    )(ids, *args, *weights)


def query_step(rows):
    return math.gcd(rows, 256)


def bit_count(size):
    return size.bit_length() - 1


def swap_with(value, axis, size, mask):
    return lax.ppermute(value, axis, [(i, i ^ mask) for i in range(size)])


def by_bit(bit, own, other):
    return jnp.where(bit == 0, jnp.stack([own, other]), jnp.stack([other, own]))


class Layout:
    def __init__(self, groups, ranks, cores):
        self.groups = groups
        self.ranks = ranks
        self.cores = cores
        self.chips = HEADS * ranks
        self.devices = self.chips * cores
        self.chip_axes = ("z", "x", "r") if ranks > 1 else ("z", "x")

    def chip(self):
        return lax.axis_index(("z", "x", "r"))

    def swap_chip(self, value, mask):
        return swap_with(value, self.chip_axes, self.chips, mask)

    def swap_core(self, value):
        return swap_with(value, "s", 2, 1)

    def shift_chip(self, value, distance):
        chips = range(self.chips)
        route = [(i - distance, i) for i in chips if i - distance in chips]
        return lax.ppermute(value, self.chip_axes, route)

    def gather_chips(self, value, masks):
        held = value[None]
        for mask in masks[:-1]:
            held = jnp.concatenate([held, self.swap_chip(held, mask)], axis=0)
        return [held, self.swap_chip(held, masks[-1])]

    def distances(self, masks):
        found = [0]
        for mask in masks:
            found = found + [d ^ mask for d in found]
        return found

    def heads_to_rows(self, value):
        value = value.reshape((HEADS, self.ranks) + value.shape[1:])
        mine = lax.dynamic_index_in_dim(value, lax.axis_index("r"), 1, keepdims=False)
        return lax.all_to_all(mine, ("z", "x"), 0, 0, tiled=True)

    def rows_to_heads(self, value):
        got = lax.all_to_all(value, ("z", "x"), 0, 0, tiled=True)
        if self.ranks > 1:
            got = lax.all_gather(got, "r", axis=1, tiled=False)
            got = got.reshape((self.chips,) + value.shape[1:])
        return got

    def join_sides(self, value):
        return by_bit(lax.axis_index("b") % 2, value, swap_with(value, "b", self.groups, 1))

    def join_cores(self, value, each):
        core = lax.axis_index("s")
        both = value[:, 2 * each :]

        def rows_of(owner):
            rows = lax.dynamic_slice_in_dim(value, owner * each, each, 1)
            return jnp.concatenate([rows, both], axis=1)

        return by_bit(core, rows_of(core), self.swap_core(rows_of(1 - core)))

    def sum_batch(self, value):
        for place in range(bit_count(self.groups)):
            value = value + swap_with(value, "b", self.groups, 1 << place)
        return value


class Reduction:
    def __init__(self, layout, batch_first, keep, send):
        self.layout = layout
        self.batch_first = batch_first
        self.keep, self.send = keep, send
        self.stage = 0

    def step(self):
        groups = self.layout.groups
        axis, size = ("b", groups) if self.batch_first == (self.stage == 0) else ("x", 2)
        if self.stage < 2:
            got = swap_with(self.send, axis, size, 1)
        if self.stage == 0 and self.batch_first:
            self.keep, self.send = self.keep[0] + got[0], self.keep[1] + got[1]
        elif self.stage == 0:
            self.keep, self.send = self.keep[:, 0] + got[:, 0], self.keep[:, 1] + got[:, 1]
        elif self.stage == 1:
            self.send = self.keep + got
            self.keep = self.send
        else:
            self.keep = self.over_depth()
        self.stage += 1

    def over_depth(self):
        ranks = self.layout.ranks
        got = lax.all_to_all(self.send, "z", 0, 0, tiled=True)
        own = lax.broadcasted_iota(jnp.int32, got.shape, 0) // ranks == lax.axis_index("z")
        value = jnp.where(own, self.keep, got)
        value = jnp.sum(value.reshape((4, ranks) + value.shape[1:]), axis=0)
        if ranks > 1:
            rank = lax.axis_index("r")
            keep = lax.dynamic_index_in_dim(value, rank, 0, keepdims=False)
            send = lax.dynamic_index_in_dim(value, 1 - rank, 0, keepdims=False)
            value = keep + swap_with(send, "r", 2, 1)
        else:
            value = value[0]
        for place in range(1, bit_count(self.layout.groups)):
            value = value + swap_with(value, "b", self.layout.groups, 1 << place)
        return value

    def finish(self):
        while self.stage < 3:
            self.step()
        return self.keep


def tied(value, *reductions):
    value, kept = lax.optimization_barrier((value, [r.keep for r in reductions]))
    for r, keep in zip(reductions, kept):
        r.keep = keep
    return value


def column_blocks(mat):
    return [mat[:, i * D : (i + 1) * D] for i in range(mat.shape[1] // D)]


def update(grad, weight, velocity, average, rate):
    momentum = momentum_decay * velocity + grad
    updated = weight - rate * (grad + momentum_decay * momentum)
    smooth = average_decay * average + (1.0 - average_decay) * updated
    return (momentum, smooth, updated)


def with_norm(product, columns, gain, shift, weight):
    grad = gain * product + shift * columns
    return grad, jnp.sum(weight * product, axis=1), jnp.sum(weight * columns, axis=1)


def shards(layout, rate, args):
    inputs, lengths, cotangent = args[:3]
    weights, velocities, averages = args[3:9], args[9:15], args[15:21]
    qkv_w, proj_w, up_w, down_w, pool_w, norm_w = weights
    half = inputs.shape[1]
    rows = 2 * half
    short_half, short_rows = half // 3, rows // 3
    each = qkv_w.shape[1]
    ff_each = down_w.shape[1]
    owners, chips, ranks = layout.devices, layout.chips, layout.ranks
    chip = layout.chip()
    core = lax.axis_index("s")
    side = lax.axis_index("b") % 2
    owner = chip * layout.cores + core
    length = lengths[core]
    ids = jnp.stack([chip, core, side, lax.axis_index("x"), length, length // 3]).astype(jnp.int32)
    seq = chips * rows
    short_seq = seq // 3
    bits = bit_count(chips)

    norm_local = jnp.transpose(norm_w, (0, 2, 1)).reshape(8, each)
    norm_lanes = lax.dynamic_update_slice(
        jnp.zeros((8, D), F32), norm_local, (0, owner * each)
    )
    carried = jnp.concatenate([inputs, jnp.broadcast_to(norm_lanes, (2, 8, D))], axis=1)
    carried = lax.all_to_all(carried, "s", 0, 0, tiled=True)
    stream = carried[:, :half].reshape(rows, D)
    masks_a = tuple(1 << i for i in reversed(range(bits)))
    masks_b = (1,) + tuple(1 << i for i in reversed(range(1, bits)))
    distances = (layout.distances(masks_a), layout.distances(masks_b))
    blocks = layout.gather_chips(carried[0], masks_a) + layout.gather_chips(carried[1], masks_b)

    head_cols = jnp.transpose(qkv_w[0].reshape(each, 3, HEADS, HEAD_DIM), (2, 0, 1, 3))
    head_cols = head_cols.reshape(HEADS, each, 3 * HEAD_DIM)
    head_cols = jnp.repeat(head_cols, ranks * layout.cores, axis=0)
    wide_axes = layout.chip_axes + ("s",)
    head_w = lax.all_to_all(head_cols, wide_axes, 0, 0, tiled=True)
    head_w = head_w.reshape(D, 3 * HEAD_DIM)

    units = lambda pieces: jnp.concatenate(pieces, axis=0).reshape(-1, each, D)
    packed = units(
        [proj_w[0]]
        + column_blocks(up_w[0])
        + [down_w[0]]
        + column_blocks(pool_w[0])
        + column_blocks(qkv_w[1])
        + [proj_w[1]]
        + column_blocks(pool_w[1])
    )
    gathered = lax.all_gather(packed, wide_axes, axis=0, tiled=False)
    second = units(column_blocks(up_w[1]) + [down_w[1]])
    second = lax.all_gather(second, wide_axes, axis=0, tiled=False)
    last = units(column_blocks(qkv_w[0]))
    last = lax.all_gather(last, wide_axes, axis=0, tiled=False)

    cos, sin, cos_t, sin_t = rope_tables(seq)
    tables = (cos, sin)
    tables_t = (cos_t, sin_t)
    short_tables = (cos[:short_seq], sin[:short_seq])
    short_tables_t = (cos_t[:, :short_seq], sin_t[:, :short_seq])
    step = query_step(seq)
    short_step = query_step(short_seq)
    vmem = lambda *dims: pltpu.VMEM(dims, F32)
    column_buffer = lambda count: vmem(count, owners, each, D)
    row_buffer = vmem(owners, 4, each, D)
    blocks_of = lambda count: vmem(LANE_BLOCKS, count, LANES)

    outs = call(
        10,
        functools.partial(first_attend_kernel, half, step, distances),
        attend_outs(seq, half) + [shape(8, D)],
        [vmem(seq, 3 * HEAD_DIM)],
        ids,
        [*blocks, head_w, *tables],
    )
    saved0, norm = (outs[3], outs[4], outs[5], outs[1], outs[2]), outs[6]
    got0 = layout.heads_to_rows(outs[0])
    full, mixed0, u0 = call(
        8,
        first_dense_kernel,
        [shape(rows, D), shape(rows, D), shape(rows, 4 * D)],
        [column_buffer(1), column_buffer(4), row_buffer],
        ids,
        [stream, got0, norm],
        [gathered],
        9,
    )

    tail = layout.shift_chip(full[-2:], 1)
    shortened, to_send = call(
        5,
        shorten_kernel,
        [shape(short_rows, D), shape(HEADS, short_half, 6 * HEAD_DIM)],
        [column_buffer(3), column_buffer(3), blocks_of(rows + 8)],
        ids,
        [full, tail, norm],
        [gathered],
        6,
    )
    outs = call(
        3,
        functools.partial(second_attend_kernel, short_half, short_step),
        attend_outs(short_seq, short_half),
        [vmem(short_seq, 3 * HEAD_DIM)],
        ids,
        [layout.rows_to_heads(to_send), *short_tables],
    )
    saved1 = (outs[3], outs[4], outs[5], outs[1], outs[2])
    got1 = layout.heads_to_rows(outs[0])
    cot = lax.all_to_all(cotangent, "s", 0, 0, tiled=True).reshape(rows, D)
    middle_wide = 10 * D
    activations, grad_att1, grad_mixed1, keep_a, send_a = call(
        13,
        functools.partial(middle_kernel, ff_each),
        [
            shape(rows, D),
            shape(HEADS, short_half, 2 * HEAD_DIM),
            shape(short_rows, D),
            shape(short_rows, middle_wide),
            shape(short_rows, middle_wide),
        ],
        [column_buffer(1), column_buffer(4), row_buffer, column_buffer(3)]
        + [blocks_of(rows), blocks_of(rows)],
        ids,
        [shortened, got1, norm, full, cot],
        [gathered, second],
        12,
    )

    depth = 4 * ranks
    pair = 2 * each
    up_rows = pair + 8
    up_out = shape(2, depth, up_rows + each // 2, D)
    down_out = shape(depth, 2, ff_each // 2, D)
    got_a = layout.swap_core(send_a)
    up_keep, up_send, down_keep, down_send = call(
        6,
        functools.partial(middle_products_kernel, ranks, ff_each, pair),
        [up_out, up_out, down_out, down_out],
        [],
        ids,
        [keep_a, got_a],
    )
    red_up1 = Reduction(layout, True, up_keep, up_send)
    red_down1 = Reduction(layout, False, down_keep, down_send)

    scratch = lambda count: [
        vmem(count, HEAD_DIM),
        vmem(count, 2 * HEAD_DIM),
        vmem(count, 2 * HEAD_DIM),
        vmem(HEAD_DIM, count),
        vmem(count, 3 * HEAD_DIM),
    ]
    got = layout.rows_to_heads(grad_att1)
    got = tied(got, red_up1, red_down1)
    (to_send,) = call(
        4,
        functools.partial(second_grad_kernel, short_half, short_step),
        [shape(chips, short_half, 6 * HEAD_DIM)],
        scratch(short_seq),
        ids,
        [*saved1, got, *short_tables, *short_tables_t],
    )
    got = layout.heads_to_rows(to_send)
    grad_shifted, keep_b, send_b = call(
        6.5,
        lengthen_grad_kernel,
        [shape(rows, D), shape(short_rows, 6 * D), shape(short_rows, 6 * D)],
        [column_buffer(3), column_buffer(3), blocks_of(rows + 8), blocks_of(rows)],
        ids,
        [got, shortened, grad_mixed1, norm, full, tail],
        [gathered],
        6,
    )
    head = layout.shift_chip(grad_shifted[:2], -1)
    qkv_out = shape(2, depth, up_rows, 3 * D // 4)
    pool_out = shape(depth, 2, 2 * pair, 3 * D // 4)
    qkv_keep, qkv_send, pool_keep, pool_send = call(
        7,
        functools.partial(shorten_products_kernel, ranks, pair),
        [qkv_out, qkv_out, pool_out, pool_out],
        [],
        ids,
        [keep_b, layout.swap_core(send_b), keep_a, got_a],
    )
    red_qkv1 = Reduction(layout, True, qkv_keep, qkv_send)
    red_pool = Reduction(layout, False, pool_keep, pool_send)
    red_up1.step()
    head = tied(head, red_qkv1, red_pool)
    first_wide = 15 * D // 2
    grad_att0, grad_mixed0, keep_c, send_c = call(
        12.5,
        functools.partial(first_dense_grad_kernel, ff_each),
        [
            shape(HEADS, half, 2 * HEAD_DIM),
            shape(rows, D),
            shape(rows, first_wide),
            shape(rows, first_wide),
        ],
        [column_buffer(1), column_buffer(4), row_buffer, vmem(rows + 8, D)],
        ids,
        [grad_shifted, head, cot, mixed0, u0, got0, norm],
        [gathered],
        9,
    )
    all_out = shape(2, depth, up_rows + ff_each // 2 + each // 2, D)
    all_keep, all_send = call(
        9,
        functools.partial(first_products_kernel, ranks, ff_each, pair),
        [all_out, all_out],
        [],
        ids,
        [keep_c, layout.swap_core(send_c)],
    )
    red_first = Reduction(layout, True, all_keep, all_send)
    got = layout.rows_to_heads(grad_att0)
    red_up1.step()
    red_down1.step()
    red_qkv1.step()
    got = tied(got, red_first)
    to_send, product = call(
        16,
        functools.partial(first_grad_kernel, half, step, distances),
        [shape(chips, half, 6 * HEAD_DIM), shape(owners, each + 8, 3 * HEAD_DIM)],
        scratch(seq) + [pltpu.VMEM((seq, D), BF16), pltpu.VMEM((seq, D), BF16)],
        ids,
        [*blocks, *saved0, got, *tables, *tables_t],
    )
    got = layout.heads_to_rows(to_send)
    red_up1.step()
    red_down1.step()
    red_qkv1.step()
    red_first.step()
    red_pool.step()
    (input_grad,) = call(
        5,
        input_grad_kernel,
        [shape(rows, D)],
        [column_buffer(3)],
        ids,
        [got, stream, grad_mixed0, norm],
        [last],
        3,
    )
    input_grad = lax.all_to_all(input_grad.reshape(2, half, D), "s", 0, 0, tiled=True)
    activations = lax.all_to_all(activations.reshape(2, half, D), "s", 0, 0, tiled=True)

    product = product.reshape(HEADS, ranks, layout.cores, each + 8, 3 * HEAD_DIM)
    product = lax.dynamic_index_in_dim(product, lax.axis_index("r"), 1, keepdims=False)
    keep = lax.dynamic_index_in_dim(product, core, 1, keepdims=False)
    away = lax.dynamic_index_in_dim(product, 1 - core, 1, keepdims=False)
    product = layout.sum_batch(keep + layout.swap_core(away))
    product = lax.all_to_all(product, ("z", "x"), 0, 0, tiled=True)
    product = jnp.transpose(
        product.reshape(HEADS, each + 8, 3, HEAD_DIM), (1, 2, 0, 3)
    ).reshape(each + 8, 3 * D)

    def up_columns(joined):
        value = joined.reshape(2, 2, each + 8, D // ff_each, ff_each)
        return jnp.transpose(value, (2, 1, 3, 0, 4)).reshape(each + 8, 4 * D)

    def plain_columns(joined):
        return jnp.transpose(joined, (2, 0, 1, 3)).reshape(joined.shape[2], -1)

    def packed_columns(value):
        value = value.reshape(2, each // 2, 4, D // 4)
        value = jnp.transpose(value, (0, 2, 1, 3)).reshape(2, pair, D // 4)
        return plain_columns(layout.join_cores(value, each))

    half_ff = ff_each // 2
    joined = layout.join_sides(
        jnp.concatenate([red_up1.finish(), red_down1.finish()], axis=0)
    )
    up_g1 = up_columns(layout.join_cores(joined[:, :up_rows], each))
    proj_g1 = packed_columns(joined[:, up_rows : up_rows + each // 2])
    down_g1 = joined[:, up_rows + each // 2 :].reshape(ff_each, D)
    joined = layout.join_sides(jnp.concatenate([red_qkv1.finish(), red_pool.finish()], axis=0))
    qkv_g1 = plain_columns(layout.join_cores(joined[:, :up_rows], each))
    taps = layout.join_cores(joined[:, up_rows : up_rows + pair], each)
    taps = taps.reshape(2, 2, each, 3, D // 4)
    pool_g0 = jnp.transpose(taps, (2, 3, 0, 1, 4)).reshape(each, 3 * D)
    pool_g1 = plain_columns(layout.join_cores(joined[:, up_rows + pair :], each))
    joined = layout.join_sides(red_first.finish())
    up_g0 = up_columns(layout.join_cores(joined[:, :up_rows], each))
    down_g0 = joined[:, up_rows : up_rows + half_ff].reshape(ff_each, D)
    proj_g0 = packed_columns(joined[:, up_rows + half_ff :])

    def own(block, number):
        return norm_w[block][:, number : number + 1]

    qkv_g0, own0, own1 = with_norm(
        product[:each], product[each : each + 1], own(0, 0), own(0, 1), qkv_w[0]
    )
    up_g0, own2, own3 = with_norm(
        up_g0[:each], up_g0[each : each + 1], own(0, 2), own(0, 3), up_w[0]
    )
    qkv_g1, own4, own5 = with_norm(
        qkv_g1[:each], qkv_g1[each : each + 1], own(1, 0), own(1, 1), qkv_w[1]
    )
    up_g1, own6, own7 = with_norm(
        up_g1[:each], up_g1[each : each + 1], own(1, 2), own(1, 3), up_w[1]
    )
    norm_g0 = jnp.stack([own0, own1, own2, own3], axis=1)
    norm_g1 = jnp.stack([own4, own5, own6, own7], axis=1)
    grads = [
        jnp.stack(pair)
        for pair in (
            (qkv_g0, qkv_g1),
            (proj_g0, proj_g1),
            (up_g0, up_g1),
            (down_g0, down_g1),
            (pool_g0, pool_g1),
            (norm_g0, norm_g1),
        )
    ]
    results = [
        update(grads[i], weights[i], velocities[i], averages[i], rate) for i in range(6)
    ]
    return (
        (activations, input_grad)
        + tuple(grads)
        + tuple(r[0] for r in results)
        + tuple(r[1] for r in results)
        + tuple(r[2] for r in results)
    )


def solution(mesh):
    groups, wide = mesh.shape["batch"], mesh.shape["wide"]

    def program(*args):
        cores = args[0].shape[0] // groups
        ranks = wide // (HEADS * cores)
        layout = Layout(groups, ranks, cores)
        rate = 0.5 / math.sqrt(math.prod(args[0].shape))
        dims = (groups, 4, 2, ranks, cores)
        fine = Mesh(mesh.devices.reshape(dims), ("b", "z", "x", "r", "s"))
        rows = ("z", "x", "r", "s")
        stream = P("b", rows, None)
        weight = P(None, rows, None)
        return jax.shard_map(
            lambda *local: shards(layout, rate, local),
            mesh=fine,
            in_specs=(stream, P("b"), stream) + (weight,) * 18,
            out_specs=(stream, stream) + (weight,) * 24,
            check_vma=False,
        )(*args)

    return program
```

time: 739 us -> 622 us (0.84)
  local copies, waits for them, and re-layouts: 129 us -> 31.5 us
  Pallas kernels: 31.8 us -> 103 us
  matrix products: 70.6 us -> 0 us
  waiting for transfers between devices: 327 us -> 284 us
  blocking collectives: 8.34 us -> 36.6 us
    ppermute x32 -> x31, waiting for transfers between devices: 225 us -> 116 us  [swap_with(): return lax.ppermute(value, axis, [(i, i ^ mask) for i in range(size)])]
    pallas_call x4 -> x13, Pallas kernels: 31.8 us -> 103 us  [call(): pl.pallas_call(kernel, out_shape=list(outs), in_specs=[SMEM] + [VMEM] * l...]
    dot_general x28 -> x0, matrix products: 70.6 us -> none  [the longest x23 57 us: matmul(): return jnp.dot(left, right, precision=HIGH)]
    all_to_all x11 -> x14, waiting for transfers between devices: 43.4 us -> 113 us  [the longest x1 42.2 us: shards(): head_w = lax.all_to_all(head_cols, wide_axes, 0, 0, tiled=True)]
    all_to_all x0 -> x2, blocking collectives: none -> 27.1 us  [the longest x1 22 us: rows_to_heads(): got = lax.all_to_all(value, ('z', 'x'), 0, 0, tiled=True)]
    slice x18 -> x35, local copies, waits for them, and re-layouts: 31.6 us -> 6.56 us  [the longest x4 1.84 us: shards(): qkv_g1[:each]]
    unnamed x306 -> x135, local copies, waits for them, and re-layouts: 35.9 us -> 10.9 us
    squeeze x23 -> x3, local copies, waits for them, and re-layouts: 21.2 us -> 1.16 us  [the longest x1 1.12 us: shards(): last = units(column_blocks(qkv_w[0]))]
  transfers between devices with their start and end apart: 47 -> 50, of which waited for: 27 -> 21; matrix products, arithmetic and copies ran while one was open for 27% -> 10% of each run, Pallas kernels for 3% -> 14%
where the time goes in v2:
time: 622 us; the launch traced here: 613 us
  waiting for transfers between devices  284 us (46%)
  Pallas kernels  103 us (17%)
  starting transfers between devices  97 us (16%)
  other arithmetic  43.5 us (7%)
  blocking collectives  36.6 us (6%)
  local copies, waits for them, and re-layouts  31.5 us (5%)
  between operations  17.8 us (3%)
    ppermute x31, waiting for transfers between devices, swap_with(): return lax.ppermute(value, axis, [(i, i ^ mask) for i in range(size)])  116 us
    pallas_call x13, Pallas kernels, call(): pl.pallas_call(kernel, out_shape=list(outs), in_specs=[SMEM] + [VMEM] * l...  103 us
    all_to_all x1, waiting for transfers between devices, shards(): head_w = lax.all_to_all(head_cols, wide_axes, 0, 0, tiled=True)  42.2 us
    all_to_all x4, waiting for transfers between devices, heads_to_rows(): return lax.all_to_all(mine, ('z', 'x'), 0, 0, tiled=True)  41.1 us
    all_gather x1, waiting for transfers between devices, shards(): second = lax.all_gather(second, wide_axes, axis=0, tiled=False)  34.9 us
    ppermute x31, starting transfers between devices, swap_with(): return lax.ppermute(value, axis, [(i, i ^ mask) for i in range(size)])  27.8 us
    all_to_all x5, starting transfers between devices, over_depth(): got = lax.all_to_all(self.send, 'z', 0, 0, tiled=True)  23.8 us
    all_to_all x1, blocking collectives, rows_to_heads(): got = lax.all_to_all(value, ('z', 'x'), 0, 0, tiled=True)  22 us
  transfers between devices with their start and end apart: 50, of which 21 were waited for; matrix products, arithmetic and copies ran while one was open for 10% of the time, Pallas kernels for 14%

profile of v2, /device:TPU:0, one launch (start us, length us, event | category | flops | bytes accessed | tf_op | source)
XLA Modules:
  0.0 613.1 jit_solution(9876351199210558555)
XLA Ops:
  22.5 6.8 %collective-permute-done.3 = f32[1,104,512]{2,1,0:T(8,128)S(1)} collective-permute-done((f32[1,104,512]{2,1,0:T(8,128)S(1)}, f32[1,104,512]{2,1,0:T(8,128)S(1)}, u32[]{:S(2)}, u32[]{:S(2)}) %collective-permute-start.3) | collective-permute-done | bytes 213024 | tf_op jit(solution)/shard_map/ppermute | solution.py:836
  29.4 12.8 %collective-permute-done = f32[1,104,512]{2,1,0:T(8,128)S(1)} collective-permute-done((f32[1,104,512]{2,1,0:T(8,128)S(1)}, f32[1,104,512]{2,1,0:T(8,128)S(1)}, u32[]{:S(2)}, u32[]{:S(2)}) %collective-permute-start) | collective-permute-done | bytes 213024 | tf_op jit(solution)/shard_map/ppermute | solution.py:836
  42.3 22.0 %collective-permute-done.4 = f32[2,104,512]{2,1,0:T(8,128)S(1)} collective-permute-done((f32[2,104,512]{2,1,0:T(8,128)S(1)}, f32[2,104,512]{2,1,0:T(8,128)S(1)}, u32[]{:S(2)}, u32[]{:S(2)}) %collective-permute-start.4) | collective-permute-done | bytes 426016 | tf_op jit(solution)/shard_map/ppermute | solution.py:836
  71.2 8.2 %all-to-all-start.1 = ((f32[16,32,192]{2,1,0:T(8,128)}), f32[16,32,192]{2,1,0:T(8,128)S(1)}, u32[]{:S(2)}, u32[]{:S(2)}) async-start(f32[16,32,192]{2,1,0:T(8,128)} %bitcast.11), calls=%async_computation.1 | async-start | bytes 1048576 | tf_op jit(solution)/shard_map/all_to_all | solution.py:1014
  83.2 42.2 %all-to-all-done.1 = f32[16,32,192]{2,1,0:T(8,128)S(1)} async-done(((f32[16,32,192]{2,1,0:T(8,128)}), f32[16,32,192]{2,1,0:T(8,128)S(1)}, u32[]{:S(2)}, u32[]{:S(2)}) %all-to-all-start.1) | async-done | bytes 393248 | tf_op jit(solution)/shard_map/all_to_all | solution.py:1014
  126.2 9.8 %shard_map.476 = (f32[8,96,128]{2,1,0:T(8,128)}, f32[64,1536]{1,0:T(8,128)}, f32[8,1536]{1,0:T(8,128)}, bf16[1536,192]{1,0:T(8,128)(2,1)}, bf16[1536,192]{1,0:T(...) custom-call(s32[6]{0:T(128)} %stack.217.ids_ref.refs_0_, f32[4,104,512]{2,1,0:T(8,128)} %copy-done.23, ...), custom_call_target="tpu_custom_call" | custom-call | flops 32999999488 | tf_op jit(solution)/shard_map/pallas_call | solution.py:814
  140.4 16.1 %all-to-all-done.2.got_ref = f32[8,96,128]{2,1,0:T(8,128)S(1)} async-done(((f32[8,96,128]{2,1,0:T(8,128)}), f32[8,96,128]{2,1,0:T(8,128)S(1)}, u32[]{:S(2)}, u32[]{:S(2)}) %all-to-all-start.2) | async-done | bytes 393248 | tf_op jit(solution)/shard_map/all_to_all | solution.py:881
  156.5 17.7 %all-gather.4.cloned.1.call-done.g_ref.refs_6_ = f32[16,19,32,512]{3,2,1,0:T(8,128)} async-done(((f32[1,19,32,512]{3,2,1,0:T(8,128)}), f32[16,19,32,512]{3,2,1,0:T(8,128)}) %all-gather.4.cloned.1.call-update) | async-done | bytes 19922960 | tf_op jit(solution)/shard_map/all_gather | solution.py:1027
  174.2 8.2 %shard_map.477 = (f32[192,512]{1,0:T(8,128)}, f32[192,512]{1,0:T(8,128)}, f32[192,2048]{1,0:T(8,128)}) custom-call(s32[6]{0:T(128)} %stack.217.ids_ref.refs_0_, f32[192,512]{1,0:T(8,128)} %bitcast.200, f32[8,96,128]{2,1,0:T(8,128)} %copy-done.34, f32[8,512]{1,0:T(8,128)} %get-tuple-element.77.norm_ref.refs_3_, ...), custom_call_target="tpu_custom_call" | custom-call | flops 26400000000 | tf_op jit(solution)/shard_map/pallas_call | solution.py:814
  192.5 22.0 %all_to_all.91.packed_ref = f32[8,32,384]{2,1,0:T(8,128)} all-to-all(f32[8,32,384]{2,1,0:T(8,128)} %get-tuple-element.80), channel_id=1, replica_groups=mesh['b'=2,'z'=4,'x'=2,'r'=1,'s'=2] {'z','x'}, dimensions={0} | all-to-all | bytes 786432 | tf_op jit(solution)/shard_map/all_to_all | solution.py:884
  224.7 34.9 %all-gather.6.cloned.1.call-done.refs_7_ = f32[16,8,32,512]{3,2,1,0:T(8,128)} async-done(((f32[1,8,32,512]{3,2,1,0:T(8,128)}), f32[16,8,32,512]{3,2,1,0:T(8,128)}) %all-gather.6.cloned.1.call-update) | async-done | bytes 8388624 | tf_op jit(solution)/shard_map/all_gather | solution.py:1029
  260.2 12.8 %shard_map.480 = (f32[192,512]{1,0:T(8,128)}, f32[8,32,128]{2,1,0:T(8,128)}, f32[64,512]{1,0:T(8,128)}, f32[64,5120]{1,0:T(8,128)}, f32[64,5120]{1,0:T(8,128)}) custom-call(s32[6]{0:T(128)} %stack.217.ids_ref.refs_0_, f32[64,512]{1,0:T(8,128)} %get-tuple-element.79.refs_1_.short_ref, f32[8,32,128]{2,1,0:T(8,128)} %copy-done.47, ...), custom_call_target="tpu_custom_call" | custom-call | flops 42900000768 | tf_op jit(solution)/shard_map/pallas_call | solution.py:814
  297.4 8.3 %all-to-all-done.8.got_ref = f32[8,32,384]{2,1,0:T(8,128)S(1)} async-done(((f32[8,32,384]{2,1,0:T(8,128)}), f32[8,32,384]{2,1,0:T(8,128)S(1)}, u32[]{:S(2)}, u32[]{:S(2)}) %all-to-all-start.8) | async-done | bytes 393248 | tf_op jit(solution)/shard_map/all_to_all | solution.py:881
  315.2 8.6 %collective-permute-done.25 = f32[4,2,64,512]{3,2,1,0:T(8,128)S(1)} collective-permute-done((f32[4,2,64,512]{3,2,1,0:T(8,128)}, f32[4,2,64,512]{3,2,1,0:T(8,128)S(1)}, u32[]{:S(2)}, u32[]{:S(2)}) %collective-permute-start.25) | collective-permute-done | bytes 1048608 | tf_op jit(solution)/shard_map/ppermute | solution.py:836
  346.1 12.5 %shard_map.485 = (f32[8,96,128]{2,1,0:T(8,128)}, f32[192,512]{1,0:T(8,128)}, f32[192,3840]{1,0:T(8,128)}, f32[192,3840]{1,0:T(8,128)}) custom-call(s32[6]{0:T(128)} %stack.217.ids_ref.refs_0_, f32[192,512]{1,0:T(8,128)} %get-tuple-element.100.shifted_ref, f32[2,512]{1,0:T(2,128)} %copy-done.55, f32[192,512]{1,0:T(8,128)} %bitcast.204, ...), custom_call_target="tpu_custom_call" | custom-call | flops 41250000896 | tf_op jit(solution)/shard_map/pallas_call | solution.py:814
  371.7 10.9 %collective-permute-done.15 = f32[4,2,128,384]{3,2,1,0:T(8,128)S(1)} collective-permute-done((f32[4,2,128,384]{3,2,1,0:T(8,128)}, f32[4,2,128,384]{3,2,1,0:T(8,128)S(1)}, u32[]{:S(2)}, u32[]{:S(2)}) %collective-permute-start.15) | collective-permute-done | bytes 1572896 | tf_op jit(solution)/shard_map/ppermute | solution.py:836
  407.6 8.4 %shard_map.486 = (f32[2,4,152,512]{3,2,1,0:T(8,128)}, f32[2,4,152,512]{3,2,1,0:T(8,128)}) custom-call(s32[6]{0:T(128)} %stack.217.ids_ref.refs_0_, f32[192,3840]{1,0:T(8,128)} %get-tuple-element.109.keep_ref, f32[192,3840]{1,0:T(8,128)} %collective-permute-done.10.got_ref), custom_call_target="tpu_custom_call" | custom-call | flops 29699999744 | tf_op jit(solution)/shard_map/pallas_call | solution.py:814
  416.0 6.6 %all-to-all-done.9.refs_9_ = f32[8,96,128]{2,1,0:T(8,128)} async-done(((f32[8,96,128]{2,1,0:T(8,128)}), f32[8,96,128]{2,1,0:T(8,128)}, u32[]{:S(2)}, u32[]{:S(2)}) %all-to-all-start.9) | async-done | bytes 393248 | tf_op jit(solution)/shard_map/all_to_all | solution.py:884
  427.7 15.8 %shard_map.487 = (f32[8,96,384]{2,1,0:T(8,128)}, f32[16,40,192]{2,1,0:T(8,128)}) custom-call(s32[6]{0:T(128)} %stack.217.ids_ref.refs_0_, f32[4,104,512]{2,1,0:T(8,128)} %copy-done.23, f32[4,104,512]{2,1,0:T(8,128)} %collective-permute-done.2.refs_1_, f32[4,104,512]{2,1,0:T(8,128)} %copy-done.22, f32[4,104,512]{2,1,0:T(8,128)} %collective-permute-done.5.refs_3_, ...), custom_call_target="tpu_custom_call" | custom-call | flops 52800000000 | tf_op jit(solution)/shard_map/pallas_call | solution.py:814
  450.5 31.9 %collective-permute-done.19 = f32[2,4,152,512]{3,2,1,0:T(8,128)} collective-permute-done((f32[2,4,152,512]{3,2,1,0:T(8,128)}, f32[2,4,152,512]{3,2,1,0:T(8,128)}, u32[]{:S(2)}, u32[]{:S(2)}) %collective-permute-start.19) | collective-permute-done | bytes 2490400 | tf_op jit(solution)/shard_map/ppermute | solution.py:836
  493.0 6.9 %collective-permute-done.12 = f32[8,40,192]{2,1,0:T(8,128)S(1)} collective-permute-done((f32[8,40,192]{2,1,0:T(8,128)S(1)}, f32[8,40,192]{2,1,0:T(8,128)S(1)}, u32[]{:S(2)}, u32[]{:S(2)}) %collective-permute-start.12) | collective-permute-done | bytes 245792 | tf_op jit(solution)/shard_map/ppermute | solution.py:836
  508.4 8.7 %collective-permute-done.20 = f32[4,152,512]{2,1,0:T(8,128)} collective-permute-done((f32[4,152,512]{2,1,0:T(8,128)}, f32[4,152,512]{2,1,0:T(8,128)}, u32[]{:S(2)}, u32[]{:S(2)}) %collective-permute-start.20) | collective-permute-done | bytes 1245216 | tf_op jit(solution)/shard_map/ppermute | solution.py:836
  533.6 18.6 %all-to-all-done.15 = f32[4,152,512]{2,1,0:T(8,128)S(1)} async-done(((f32[4,152,512]{2,1,0:T(8,128)}), f32[4,152,512]{2,1,0:T(8,128)S(1)}, u32[]{:S(2)}, u32[]{:S(2)}) %all-to-all-start.15) | async-done | bytes 1245216 | tf_op jit(solution)/shard_map/all_to_all | solution.py:934
  568.0 16.7 %all-to-all-done.10.got_ref = f32[8,96,384]{2,1,0:T(8,128)} async-done(((f32[8,96,384]{2,1,0:T(8,128)}), f32[8,96,384]{2,1,0:T(8,128)}, u32[]{:S(2)}, u32[]{:S(2)}) %all-to-all-start.10) | async-done | bytes 1179680 | tf_op jit(solution)/shard_map/all_to_all | solution.py:881
  (368 shorter events, 228.0 us)
Async XLA Ops:
  7.2 167.0 %all-gather.4.cloned.1.call-start = ((), (), s32[]{:S(2)}) async-start(), calls=%async_computation.18 | async-start | bytes 21168128 | tf_op jit(solution)/shard_map/all_gather | solution.py:1027
  11.6 247.9 %all-gather.6.cloned.1.call-start = ((), (), s32[]{:S(2)}) async-start(), calls=%async_computation.19 | async-start | bytes 8912896 | tf_op jit(solution)/shard_map/all_gather | solution.py:1029
  29.3 35.1 %collective-permute-start.4 = (f32[2,104,512]{2,1,0:T(8,128)S(1)}, f32[2,104,512]{2,1,0:T(8,128)S(1)}, u32[]{:S(2)}, u32[]{:S(2)}) collective-permute-start(f32[2,104,512]{2,1,0:T(8,128)S(1)} %pad_maximum_fusion.6), channel_id=1, source_target_pairs={{0,8},{2,10},{4,12},{6,14},{8,0},{10,2},{12,4},{14,6},{1,9},{3,11}... | collective-permute-start | bytes 1277960 | tf_op jit(solution)/shard_map/ppermute | solution.py:836
  64.4 61.0 %collective-permute-start.5 = (f32[4,104,512]{2,1,0:T(8,128)S(1)}, f32[4,104,512]{2,1,0:T(8,128)}, u32[]{:S(2)}, u32[]{:S(2)}) collective-permute-start(f32[4,104,512]{2,1,0:T(8,128)S(1)} %pad_maximum_fusion.1.refs_2_), channel_id=1, source_target_pairs={{0,4},{2,6},{4,0},{6,2},{8,12},{10,14},{12,8},{14,10},{1,5},{3,7},... | collective-permute-start | bytes 2555912 | tf_op jit(solution)/shard_map/ppermute | solution.py:836
  69.3 56.2 %collective-permute-start.2 = (f32[4,104,512]{2,1,0:T(8,128)S(1)}, f32[4,104,512]{2,1,0:T(8,128)}, u32[]{:S(2)}, u32[]{:S(2)}) collective-permute-start(f32[4,104,512]{2,1,0:T(8,128)S(1)} %pad_maximum_fusion.refs_0_), channel_id=1, source_target_pairs={{0,2},{2,0},{4,6},{6,4},{8,10},{10,8},{12,14},{14,12},{1,3},{3,1},... | collective-permute-start | bytes 2555912 | tf_op jit(solution)/shard_map/ppermute | solution.py:836
  71.2 54.2 %all-to-all-start.1 = ((f32[16,32,192]{2,1,0:T(8,128)}), f32[16,32,192]{2,1,0:T(8,128)S(1)}, u32[]{:S(2)}, u32[]{:S(2)}) async-start(f32[16,32,192]{2,1,0:T(8,128)} %bitcast.11), calls=%async_computation.1 | async-start | bytes 1048576 | tf_op jit(solution)/shard_map/all_to_all | solution.py:1014
  221.2 38.3 %all-to-all-start.4 = ((f32[8,32,128]{2,1,0:T(8,128)}), f32[8,32,128]{2,1,0:T(8,128)S(1)}, u32[]{:S(2)}, u32[]{:S(2)}) async-start(f32[8,32,128]{2,1,0:T(8,128)} %get-tuple-element.81), calls=%async_computation.4 | async-start | bytes 262144 | tf_op jit(solution)/shard_map/all_to_all | solution.py:881
  293.9 34.6 %collective-permute-start.23 = (f32[2,4,88,512]{3,2,1,0:T(8,128)}, f32[2,4,88,512]{3,2,1,0:T(8,128)S(1)}, u32[]{:S(2)}, u32[]{:S(2)}) collective-permute-start(f32[2,4,88,512]{3,2,1,0:T(8,128)} %get-tuple-element.123), channel_id=1, source_target_pairs={{0,16},{16,0},{1,17},{17,1},{2,18},{18,2},{3,19},{19,3},{4,20},{20... | collective-permute-start | bytes 4325384 | tf_op jit(solution)/shard_map/ppermute | solution.py:836
  295.4 28.4 %collective-permute-start.25 = (f32[4,2,64,512]{3,2,1,0:T(8,128)}, f32[4,2,64,512]{3,2,1,0:T(8,128)S(1)}, u32[]{:S(2)}, u32[]{:S(2)}) collective-permute-start(f32[4,2,64,512]{3,2,1,0:T(8,128)} %get-tuple-element.125), channel_id=1, source_target_pairs={{0,2},{2,0},{1,3},{3,1},{4,6},{6,4},{5,7},{7,5},{8,10},{10,8},{9,1... | collective-permute-start | bytes 3145736 | tf_op jit(solution)/shard_map/ppermute | solution.py:836
  328.6 30.0 %collective-permute-start.24 = (f32[4,88,512]{2,1,0:T(8,128)S(1)}, f32[4,88,512]{2,1,0:T(8,128)}, u32[]{:S(2)}, u32[]{:S(2)}) collective-permute-start(f32[4,88,512]{2,1,0:T(8,128)S(1)} %fusion.7), channel_id=1, source_target_pairs={{0,2},{2,0},{1,3},{3,1},{4,6},{6,4},{5,7},{7,5},{8,10},{10,8},{9,1... | collective-permute-start | bytes 2162696 | tf_op jit(solution)/shard_map/ppermute | solution.py:836
  338.4 28.6 %collective-permute-start.13 = (f32[2,4,72,384]{3,2,1,0:T(8,128)}, f32[2,4,72,384]{3,2,1,0:T(8,128)}, u32[]{:S(2)}, u32[]{:S(2)}) collective-permute-start(f32[2,4,72,384]{3,2,1,0:T(8,128)} %get-tuple-element.117), channel_id=1, source_target_pairs={{0,16},{16,0},{1,17},{17,1},{2,18},{18,2},{3,19},{19,3},{4,20},{20... | collective-permute-start | bytes 2654216 | tf_op jit(solution)/shard_map/ppermute | solution.py:836
  339.9 42.7 %collective-permute-start.15 = (f32[4,2,128,384]{3,2,1,0:T(8,128)}, f32[4,2,128,384]{3,2,1,0:T(8,128)S(1)}, u32[]{:S(2)}, u32[]{:S(2)}) collective-permute-start(f32[4,2,128,384]{3,2,1,0:T(8,128)} %get-tuple-element.119), channel_id=1, source_target_pairs={{0,2},{2,0},{1,3},{3,1},{4,6},{6,4},{5,7},{7,5},{8,10},{10,8},{9,1... | collective-permute-start | bytes 4718600 | tf_op jit(solution)/shard_map/ppermute | solution.py:836
  358.6 49.0 %collective-permute-start.10 = (f32[192,3840]{1,0:T(8,128)}, f32[192,3840]{1,0:T(8,128)}, u32[]{:S(2)}, u32[]{:S(2)}) collective-permute-start(f32[192,3840]{1,0:T(8,128)} %get-tuple-element.110), channel_id=1, source_target_pairs={{0,1},{1,0},{2,3},{3,2},{4,5},{5,4},{6,7},{7,6},{8,9},{9,8},{10,11... | collective-permute-start | bytes 8847368 | tf_op jit(solution)/shard_map/ppermute | solution.py:836
  366.2 201.8 %all-gather.8.cloned.1.call-start = ((), (), s32[]{:S(2)}) async-start(), calls=%async_computation.20 | async-start | bytes 3342336 | tf_op jit(solution)/shard_map/all_gather | solution.py:1031
  369.1 32.6 %collective-permute-start.14 = (f32[4,72,384]{2,1,0:T(8,128)}, f32[4,72,384]{2,1,0:T(8,128)S(1)}, u32[]{:S(2)}, u32[]{:S(2)}) collective-permute-start(f32[4,72,384]{2,1,0:T(8,128)} %fusion.14), channel_id=1, source_target_pairs={{0,2},{2,0},{1,3},{3,1},{4,6},{6,4},{5,7},{7,5},{8,10},{10,8},{9,1... | collective-permute-start | bytes 1327112 | tf_op jit(solution)/shard_map/ppermute | solution.py:836
  403.7 85.6 %collective-permute-start.30 = (f32[2,40,512]{2,1,0:T(8,128)S(1)}, f32[2,40,512]{2,1,0:T(8,128)S(1)}, u32[]{:S(2)}, u32[]{:S(2)}) collective-permute-start(f32[2,40,512]{2,1,0:T(8,128)S(1)} %get-tuple-element.193), channel_id=1, source_target_pairs={{0,1},{1,0},{2,3},{3,2},{4,5},{5,4},{6,7},{7,6},{8,9},{9,8},{10,11... | collective-permute-start | bytes 491528 | tf_op jit(solution)/shard_map/ppermute | solution.py:836
  403.9 84.7 %collective-permute-start.28 = (f32[2,32,128]{2,0,1:T(2,128)S(1)}, f32[2,32,128]{2,0,1:T(2,128)S(1)}, u32[]{:S(2)}, u32[]{:S(2)}) collective-permute-start(f32[2,32,128]{2,0,1:T(2,128)S(1)} %get-tuple-element.187), channel_id=1, source_target_pairs={{0,1},{1,0},{2,3},{3,2},{4,5},{5,4},{6,7},{7,6},{8,9},{9,8},{10,11... | collective-permute-start | bytes 98312 | tf_op jit(solution)/shard_map/ppermute | solution.py:836
  426.3 56.1 %collective-permute-start.19 = (f32[2,4,152,512]{3,2,1,0:T(8,128)}, f32[2,4,152,512]{3,2,1,0:T(8,128)}, u32[]{:S(2)}, u32[]{:S(2)}) collective-permute-start(f32[2,4,152,512]{3,2,1,0:T(8,128)} %get-tuple-element.121), channel_id=1, source_target_pairs={{0,16},{16,0},{1,17},{17,1},{2,18},{18,2},{3,19},{19,3},{4,20},{20... | collective-permute-start | bytes 7471112 | tf_op jit(solution)/shard_map/ppermute | solution.py:836
  445.2 45.4 %collective-permute-start.11 = (f32[8,40,192]{2,1,0:T(8,128)}, f32[8,40,192]{2,1,0:T(8,128)}, u32[]{:S(2)}, u32[]{:S(2)}) collective-permute-start(f32[8,40,192]{2,1,0:T(8,128)} %dynamic-slice_bitcast_fusion), channel_id=1, source_target_pairs={{0,1},{1,0},{2,3},{3,2},{4,5},{5,4},{6,7},{7,6},{8,9},{9,8},{10,11... | collective-permute-start | bytes 737288 | tf_op jit(solution)/shard_map/ppermute | solution.py:836
  445.2 55.4 %all-to-all-start.14 = ((f32[4,128,384]{2,1,0:T(8,128)}), f32[4,128,384]{2,1,0:T(8,128)S(1)}, u32[]{:S(2)}, u32[]{:S(2)}) async-start(f32[4,128,384]{2,1,0:T(8,128)} %fusion.6), calls=%async_computation.14 | async-start | bytes 1572864 | tf_op jit(solution)/shard_map/all_to_all | solution.py:934
  485.4 31.7 %collective-permute-start.20 = (f32[4,152,512]{2,1,0:T(8,128)}, f32[4,152,512]{2,1,0:T(8,128)}, u32[]{:S(2)}, u32[]{:S(2)}) collective-permute-start(f32[4,152,512]{2,1,0:T(8,128)} %fusion), channel_id=1, source_target_pairs={{0,2},{2,0},{1,3},{3,1},{4,6},{6,4},{5,7},{7,5},{8,10},{10,8},{9,1... | collective-permute-start | bytes 3735560 | tf_op jit(solution)/shard_map/ppermute | solution.py:836
  520.3 31.9 %all-to-all-start.15 = ((f32[4,152,512]{2,1,0:T(8,128)}), f32[4,152,512]{2,1,0:T(8,128)S(1)}, u32[]{:S(2)}, u32[]{:S(2)}) async-start(f32[4,152,512]{2,1,0:T(8,128)} %fusion.2), calls=%async_computation.15 | async-start | bytes 2490368 | tf_op jit(solution)/shard_map/all_to_all | solution.py:934
  527.5 31.2 %collective-permute-start.18 = (f32[2,40,384]{2,1,0:T(8,128)}, f32[2,40,384]{2,1,0:T(8,128)}, u32[]{:S(2)}, u32[]{:S(2)}) collective-permute-start(f32[2,40,384]{2,1,0:T(8,128)} %get-tuple-element.195), channel_id=1, source_target_pairs={{0,1},{1,0},{2,3},{3,2},{4,5},{5,4},{6,7},{7,6},{8,9},{9,8},{10,11... | collective-permute-start | bytes 368648 | tf_op jit(solution)/shard_map/ppermute | solution.py:836
  552.2 32.5 %all-to-all-start.10 = ((f32[8,96,384]{2,1,0:T(8,128)}), f32[8,96,384]{2,1,0:T(8,128)}, u32[]{:S(2)}, u32[]{:S(2)}) async-start(f32[8,96,384]{2,1,0:T(8,128)} %get-tuple-element.113), calls=%async_computation.10 | async-start | bytes 2359296 | tf_op jit(solution)/shard_map/all_to_all | solution.py:881
  (84 other events, 809.3 us)
Sparse Core Ops, SparseCore 0:
  11.7 162.4 all-gather.3
  176.9 82.5 all-gather.5
  369.9 55.0 all-gather.7

commit v3 on v2

--- a/solution.py
+++ b/solution.py
@@ -21,7 +21,7 @@
 VMEM_LIMIT = 56 << 20
 ROOT = math.sqrt(2.0 / math.pi)
 CUBE = 0.044715
-CHIP, CORE, SIDE, COLUMN, LENGTH, SHORT_LENGTH = range(6)
+CHIP, CORE, SIDE, COLUMN, DEPTH, LENGTH, SHORT_LENGTH = range(7)
 
 
 def split(value):
@@ -669,12 +669,18 @@
     return pick(zero, first, second), pick(zero, second, first)
 
 
+def place_of(ids_ref, depth, rank, ranks):
+    distance = depth ^ ids_ref[DEPTH]
+    return ((distance & 1) * 2 + (distance >> 1)) * ranks + rank
+
+
 def place_by_column(ids_ref, ref, rows, block, ranks):
     for depth in range(4):
         for column in range(2):
             for rank in range(ranks):
                 chip = (depth * 2 + column) * ranks + rank
-                ref[column ^ ids_ref[COLUMN], depth * ranks + rank, rows, :] = block(chip)
+                place = place_of(ids_ref, depth, rank, ranks)
+                ref[column ^ ids_ref[COLUMN], place, rows, :] = block(chip)
 
 
 def packed_rows(rows):
@@ -714,7 +720,7 @@
         for rank in range(ranks):
             first = ((depth * 2) * ranks + rank) * each
             second = ((depth * 2 + 1) * ranks + rank) * each
-            place = depth * ranks + rank
+            place = place_of(ids_ref, depth, rank, ranks)
             for side in range(2):
                 far = side ^ ids_ref[SIDE]
                 one = products[side][first : first + each]
@@ -724,7 +730,7 @@
     return at + each
 
 
-def middle_products_kernel(ranks, size, each, ids_ref, keep_ref, got_ref, *refs):
+def dense_products_kernel(ranks, size, each, ids_ref, keep_ref, got_ref, *refs):
     up_refs, down_refs = refs[:2], refs[2:]
     factors = Factors(keep_ref, got_ref)
     normed, du, hidden, grad = (factors.take(w * D) for w in (1, 2, 2, 1))
@@ -740,52 +746,30 @@
     place_by_side(ids_ref, down_refs, 0, sides, size // 2, ranks)
 
 
-def first_products_kernel(ranks, size, each, ids_ref, keep_ref, got_ref, *refs):
-    factors = Factors(keep_ref, got_ref)
-    normed, du, hidden, grad = (factors.take(w * D) for w in (1, 2, 2, 1))
-    attended, grad_mixed = factors.take(D), factors.take(D // 2)
-    product = outer(hidden, grad).reshape(D // each, 2, size // 2, D)
-    zero = ids_ref[SIDE] == 0
-    downs = [
-        pick(zero, product[:, far], product[:, 1 - far]).reshape(-1, D) for far in range(2)
-    ]
-    for ref, half, narrow, down in zip(
-        refs, side_halves(ids_ref, du), side_halves(ids_ref, grad_mixed), downs
-    ):
-        at = place_blocks(ids_ref, ref, 0, outer(normed, half), each, ranks)
-        at = place_sums(ids_ref, ref, at, half, ranks)
-        at = place_blocks(ids_ref, ref, at, down, size // 2, ranks)
-        place_packed(ids_ref, ref, at, outer(attended, narrow), each, ranks)
-
-
 def shorten_products_kernel(
     ranks, each, ids_ref, keep_ref, got_ref, up_keep_ref, up_got_ref, *refs
 ):
-    qkv_refs, pool_refs = refs[:2], refs[2:]
     factors = Factors(keep_ref, got_ref)
     normed, dqkv = factors.take(D), factors.take(3 * D // 2)
     shifted = [factors.take(D) for _ in range(3)]
     grad = factors.take(D // 2)
-    for ref, half in zip(qkv_refs, side_halves(ids_ref, dqkv)):
-        at = place_blocks(ids_ref, ref, 0, outer(normed, half), each, ranks)
-        place_sums(ids_ref, ref, at, half, ranks)
-    narrow, wide = D // 4, 3 * D // 4
-    taps = [
-        jnp.concatenate(
-            [outer(rows, grad[:, side * narrow : (side + 1) * narrow]) for rows in shifted],
-            axis=1,
-        )
-        for side in range(2)
-    ]
-    at = place_by_side(ids_ref, pool_refs, 0, taps, each, ranks)
     factors = Factors(up_keep_ref, up_got_ref)
     factors.at = 15 * D // 2
     short, groups = factors.take(D), factors.take(3 * D // 2)
-    taps = [outer(short, groups[:, side * wide : (side + 1) * wide]) for side in range(2)]
-    place_by_side(ids_ref, pool_refs, at, taps, each, ranks)
-
-
-PER_US = 3.3e+09
+    for ref, half, narrow, wide in zip(
+        refs,
+        side_halves(ids_ref, dqkv),
+        side_halves(ids_ref, grad),
+        side_halves(ids_ref, groups),
+    ):
+        at = place_blocks(ids_ref, ref, 0, outer(normed, half), each, ranks)
+        at = place_sums(ids_ref, ref, at, half, ranks)
+        taps = jnp.concatenate([outer(rows, narrow) for rows in shifted], axis=1)
+        at = place_blocks(ids_ref, ref, at, taps, each, ranks)
+        place_blocks(ids_ref, ref, at, outer(short, wide), each, ranks)
+
+
+PER_US = 1.1e+08
 SMEM = pl.BlockSpec(memory_space=pltpu.SMEM)
 VMEM = pl.BlockSpec(memory_space=pltpu.VMEM)
 ANY = pl.BlockSpec(memory_space=pl.ANY)
@@ -858,6 +842,12 @@
     def swap_core(self, value):
         return swap_with(value, "s", 2, 1)
 
+    def exchange_cores(self, value):
+        core = lax.axis_index("s")
+        own = lax.dynamic_index_in_dim(value, core, 0, keepdims=False)
+        away = lax.dynamic_index_in_dim(value, 1 - core, 0, keepdims=False)
+        return by_bit(core, own, self.swap_core(away))
+
     def shift_chip(self, value, distance):
         chips = range(self.chips)
         route = [(i - distance, i) for i in chips if i - distance in chips]
@@ -914,28 +904,24 @@
         self.stage = 0
 
     def step(self):
-        groups = self.layout.groups
-        axis, size = ("b", groups) if self.batch_first == (self.stage == 0) else ("x", 2)
-        if self.stage < 2:
-            got = swap_with(self.send, axis, size, 1)
-        if self.stage == 0 and self.batch_first:
-            self.keep, self.send = self.keep[0] + got[0], self.keep[1] + got[1]
-        elif self.stage == 0:
-            self.keep, self.send = self.keep[:, 0] + got[:, 0], self.keep[:, 1] + got[:, 1]
-        elif self.stage == 1:
-            self.send = self.keep + got
-            self.keep = self.send
+        groups, ranks = self.layout.groups, self.layout.ranks
+        axes = (("b", groups, 1), ("x", 2, 1), ("z", 4, 1), ("z", 4, 2))
+        if not self.batch_first:
+            axes = (axes[1], axes[0]) + axes[2:]
+        got = swap_with(self.send, *axes[self.stage])
+        if self.stage == 0:
+            stay, away = (0, 1) if self.batch_first else ((slice(None), 0), (slice(None), 1))
         else:
-            self.keep = self.over_depth()
+            count = got.shape[0] // 2
+            stay, away = slice(0, count), slice(count, None)
+        if self.stage < 3:
+            self.keep, self.send = self.keep[stay] + got[stay], self.keep[away] + got[away]
+        else:
+            self.keep = self.last(self.keep + got)
         self.stage += 1
 
-    def over_depth(self):
-        ranks = self.layout.ranks
-        got = lax.all_to_all(self.send, "z", 0, 0, tiled=True)
-        own = lax.broadcasted_iota(jnp.int32, got.shape, 0) // ranks == lax.axis_index("z")
-        value = jnp.where(own, self.keep, got)
-        value = jnp.sum(value.reshape((4, ranks) + value.shape[1:]), axis=0)
-        if ranks > 1:
+    def last(self, value):
+        if self.layout.ranks > 1:
             rank = lax.axis_index("r")
             keep = lax.dynamic_index_in_dim(value, rank, 0, keepdims=False)
             send = lax.dynamic_index_in_dim(value, 1 - rank, 0, keepdims=False)
@@ -947,7 +933,7 @@
         return value
 
     def finish(self):
-        while self.stage < 3:
+        while self.stage < 4:
             self.step()
         return self.keep
 
@@ -990,7 +976,8 @@
     side = lax.axis_index("b") % 2
     owner = chip * layout.cores + core
     length = lengths[core]
-    ids = jnp.stack([chip, core, side, lax.axis_index("x"), length, length // 3]).astype(jnp.int32)
+    places = [chip, core, side, lax.axis_index("x"), lax.axis_index("z")]
+    ids = jnp.stack(places + [length, length // 3]).astype(jnp.int32)
     seq = chips * rows
     short_seq = seq // 3
     bits = bit_count(chips)
@@ -1000,7 +987,7 @@
         jnp.zeros((8, D), F32), norm_local, (0, owner * each)
     )
     carried = jnp.concatenate([inputs, jnp.broadcast_to(norm_lanes, (2, 8, D))], axis=1)
-    carried = lax.all_to_all(carried, "s", 0, 0, tiled=True)
+    carried = layout.exchange_cores(carried)
     stream = carried[:, :half].reshape(rows, D)
     masks_a = tuple(1 << i for i in reversed(range(bits)))
     masks_b = (1,) + tuple(1 << i for i in reversed(range(1, bits)))
@@ -1084,7 +1071,7 @@
     )
     saved1 = (outs[3], outs[4], outs[5], outs[1], outs[2])
     got1 = layout.heads_to_rows(outs[0])
-    cot = lax.all_to_all(cotangent, "s", 0, 0, tiled=True).reshape(rows, D)
+    cot = layout.exchange_cores(cotangent).reshape(rows, D)
     middle_wide = 10 * D
     activations, grad_att1, grad_mixed1, keep_a, send_a = call(
         13,
@@ -1112,7 +1099,7 @@
     got_a = layout.swap_core(send_a)
     up_keep, up_send, down_keep, down_send = call(
         6,
-        functools.partial(middle_products_kernel, ranks, ff_each, pair),
+        functools.partial(dense_products_kernel, ranks, ff_each, pair),
         [up_out, up_out, down_out, down_out],
         [],
         ids,
@@ -1139,6 +1126,7 @@
         [*saved1, got, *short_tables, *short_tables_t],
     )
     got = layout.heads_to_rows(to_send)
+    got, red_down1.send = lax.optimization_barrier((got, red_down1.send))
     grad_shifted, keep_b, send_b = call(
         6.5,
         lengthen_grad_kernel,
@@ -1150,20 +1138,19 @@
         6,
     )
     head = layout.shift_chip(grad_shifted[:2], -1)
-    qkv_out = shape(2, depth, up_rows, 3 * D // 4)
-    pool_out = shape(depth, 2, 2 * pair, 3 * D // 4)
-    qkv_keep, qkv_send, pool_keep, pool_send = call(
+    pool_out = shape(2, depth, up_rows + 2 * pair, 3 * D // 4)
+    pool_keep, pool_send = call(
         7,
         functools.partial(shorten_products_kernel, ranks, pair),
-        [qkv_out, qkv_out, pool_out, pool_out],
+        [pool_out, pool_out],
         [],
         ids,
         [keep_b, layout.swap_core(send_b), keep_a, got_a],
     )
-    red_qkv1 = Reduction(layout, True, qkv_keep, qkv_send)
-    red_pool = Reduction(layout, False, pool_keep, pool_send)
+    red_pool = Reduction(layout, True, pool_keep, pool_send)
     red_up1.step()
-    head = tied(head, red_qkv1, red_pool)
+    head = tied(head, red_up1)
+    head = tied(head, red_pool)
     first_wide = 15 * D // 2
     grad_att0, grad_mixed0, keep_c, send_c = call(
         12.5,
@@ -1180,21 +1167,21 @@
         [gathered],
         9,
     )
-    all_out = shape(2, depth, up_rows + ff_each // 2 + each // 2, D)
-    all_keep, all_send = call(
+    up_keep, up_send, down_keep, down_send = call(
         9,
-        functools.partial(first_products_kernel, ranks, ff_each, pair),
-        [all_out, all_out],
+        functools.partial(dense_products_kernel, ranks, ff_each, pair),
+        [up_out, up_out, down_out, down_out],
         [],
         ids,
         [keep_c, layout.swap_core(send_c)],
     )
-    red_first = Reduction(layout, True, all_keep, all_send)
+    red_up0 = Reduction(layout, True, up_keep, up_send)
+    red_down0 = Reduction(layout, False, down_keep, down_send)
     got = layout.rows_to_heads(grad_att0)
+    got = tied(got, red_up0, red_down0)
+    got = tied(got, red_up1, red_down1)
     red_up1.step()
     red_down1.step()
-    red_qkv1.step()
-    got = tied(got, red_first)
     to_send, product = call(
         16,
         functools.partial(first_grad_kernel, half, step, distances),
@@ -1203,12 +1190,10 @@
         ids,
         [*blocks, *saved0, got, *tables, *tables_t],
     )
+    red_pool.step()
+    to_send = tied(to_send, red_pool)
     got = layout.heads_to_rows(to_send)
-    red_up1.step()
-    red_down1.step()
-    red_qkv1.step()
-    red_first.step()
-    red_pool.step()
+    got, product = lax.optimization_barrier((got, product))
     (input_grad,) = call(
         5,
         input_grad_kernel,
@@ -1219,8 +1204,8 @@
         [last],
         3,
     )
-    input_grad = lax.all_to_all(input_grad.reshape(2, half, D), "s", 0, 0, tiled=True)
-    activations = lax.all_to_all(activations.reshape(2, half, D), "s", 0, 0, tiled=True)
+    input_grad = layout.exchange_cores(input_grad.reshape(2, half, D))
+    activations = layout.exchange_cores(activations.reshape(2, half, D))
 
     product = product.reshape(HEADS, ranks, layout.cores, each + 8, 3 * HEAD_DIM)
     product = lax.dynamic_index_in_dim(product, lax.axis_index("r"), 1, keepdims=False)
@@ -1244,23 +1229,24 @@
         value = jnp.transpose(value, (0, 2, 1, 3)).reshape(2, pair, D // 4)
         return plain_columns(layout.join_cores(value, each))
 
-    half_ff = ff_each // 2
     joined = layout.join_sides(
         jnp.concatenate([red_up1.finish(), red_down1.finish()], axis=0)
     )
     up_g1 = up_columns(layout.join_cores(joined[:, :up_rows], each))
     proj_g1 = packed_columns(joined[:, up_rows : up_rows + each // 2])
     down_g1 = joined[:, up_rows + each // 2 :].reshape(ff_each, D)
-    joined = layout.join_sides(jnp.concatenate([red_qkv1.finish(), red_pool.finish()], axis=0))
+    joined = layout.join_sides(red_pool.finish())
     qkv_g1 = plain_columns(layout.join_cores(joined[:, :up_rows], each))
     taps = layout.join_cores(joined[:, up_rows : up_rows + pair], each)
     taps = taps.reshape(2, 2, each, 3, D // 4)
     pool_g0 = jnp.transpose(taps, (2, 3, 0, 1, 4)).reshape(each, 3 * D)
     pool_g1 = plain_columns(layout.join_cores(joined[:, up_rows + pair :], each))
-    joined = layout.join_sides(red_first.finish())
+    joined = layout.join_sides(
+        jnp.concatenate([red_up0.finish(), red_down0.finish()], axis=0)
+    )
     up_g0 = up_columns(layout.join_cores(joined[:, :up_rows], each))
-    down_g0 = joined[:, up_rows : up_rows + half_ff].reshape(ff_each, D)
-    proj_g0 = packed_columns(joined[:, up_rows + half_ff :])
+    proj_g0 = packed_columns(joined[:, up_rows : up_rows + each // 2])
+    down_g0 = joined[:, up_rows + each // 2 :].reshape(ff_each, D)
 
     def own(block, number):
         return norm_w[block][:, number : number + 1]

time: 622 us -> 584 us (0.939)
  starting transfers between devices: 97 us -> 77.4 us
  blocking collectives: 36.6 us -> 18 us
    all_to_all x2 -> x3, waiting for transfers between devices: 8.01 us -> 50.8 us  [rows_to_heads(): got = lax.all_to_all(value, ('z', 'x'), 0, 0, tiled=True)]
    all_to_all x6 -> x0, starting transfers between devices: 27.3 us -> none  [the longest x5 23.8 us: over_depth(): got = lax.all_to_all(self.send, 'z', 0, 0, tiled=True)]
    all_to_all x4 -> x3, waiting for transfers between devices: 41.1 us -> 16.1 us  [heads_to_rows(): return lax.all_to_all(mine, ('z', 'x'), 0, 0, tiled=True)]
    all_to_all x6 -> x0, waiting for transfers between devices: 22 us -> none  [the longest x5 22 us: over_depth(): got = lax.all_to_all(self.send, 'z', 0, 0, tiled=True)]
    all_to_all x4 -> x1, blocking collectives: 36.6 us -> 18 us  [heads_to_rows(): return lax.all_to_all(mine, ('z', 'x'), 0, 0, tiled=True)]
    ppermute x31 -> x45, starting transfers between devices: 27.8 us -> 37.1 us  [swap_with(): return lax.ppermute(value, axis, [(i, i ^ mask) for i in range(size)])]
    all_to_all x2 -> x3, starting transfers between devices: 9.54 us -> 16.2 us  [rows_to_heads(): got = lax.all_to_all(value, ('z', 'x'), 0, 0, tiled=True)]
    reduce_sum x5 -> x0, other arithmetic: 6.44 us -> none  [over_depth(): value = jnp.sum(value.reshape((4, ranks) + value.shape[1:]), axis=0)]
  transfers between devices with their start and end apart: 50 -> 58, of which waited for: 21 -> 26; matrix products, arithmetic and copies ran while one was open for 10% -> 10% of each run, Pallas kernels for 14% -> 13%
where the time goes in v3:
time: 584 us; the launch traced here: 576 us
  waiting for transfers between devices  282 us (48%)
  Pallas kernels  104 us (18%)
  starting transfers between devices  77.4 us (13%)
  other arithmetic  43.7 us (7%)
  local copies, waits for them, and re-layouts  33.3 us (6%)
  blocking collectives  18 us (3%)
  between operations  17.9 us (3%)
    ppermute x45, waiting for transfers between devices, swap_with(): return lax.ppermute(value, axis, [(i, i ^ mask) for i in range(size)])  112 us
    pallas_call x13, Pallas kernels, call(): pl.pallas_call(kernel, out_shape=list(outs), in_specs=[SMEM] + [VMEM] * l...  104 us
    all_to_all x3, waiting for transfers between devices, rows_to_heads(): got = lax.all_to_all(value, ('z', 'x'), 0, 0, tiled=True)  50.8 us
    all_to_all x1, waiting for transfers between devices, shards(): head_w = lax.all_to_all(head_cols, wide_axes, 0, 0, tiled=True)  38.3 us
    ppermute x45, starting transfers between devices, swap_with(): return lax.ppermute(value, axis, [(i, i ^ mask) for i in range(size)])  37.1 us
    all_gather x1, waiting for transfers between devices, shards(): second = lax.all_gather(second, wide_axes, axis=0, tiled=False)  36.2 us
    all_gather x1, waiting for transfers between devices, shards(): gathered = lax.all_gather(packed, wide_axes, axis=0, tiled=False)  21.8 us
    all_to_all x1, blocking collectives, heads_to_rows(): return lax.all_to_all(mine, ('z', 'x'), 0, 0, tiled=True)  18 us
  transfers between devices with their start and end apart: 58, of which 26 were waited for; matrix products, arithmetic and copies ran while one was open for 10% of the time, Pallas kernels for 13%

profile of v3, /device:TPU:0, one launch (start us, length us, event | category | flops | bytes accessed | tf_op | source)
XLA Modules:
  0.0 575.9 jit_solution(9388266174829423155)
XLA Ops:
  26.3 17.0 %collective-permute-done.1 = f32[1,104,512]{2,1,0:T(8,128)S(1)} collective-permute-done((f32[1,104,512]{2,1,0:T(8,128)S(1)}, f32[1,104,512]{2,1,0:T(8,128)S(1)}, u32[]{:S(2)}, u32[]{:S(2)}) %collective-permute-start.1) | collective-permute-done | bytes 213024 | tf_op jit(solution)/shard_map/ppermute | solution.py:820
  43.4 18.9 %collective-permute-done.5 = f32[2,104,512]{2,1,0:T(8,128)S(1)} collective-permute-done((f32[2,104,512]{2,1,0:T(8,128)S(1)}, f32[2,104,512]{2,1,0:T(8,128)S(1)}, u32[]{:S(2)}, u32[]{:S(2)}) %collective-permute-start.5) | collective-permute-done | bytes 426016 | tf_op jit(solution)/shard_map/ppermute | solution.py:820
  63.1 7.6 %collective-permute-done.2 = f32[2,104,512]{2,1,0:T(8,128)S(1)} collective-permute-done((f32[2,104,512]{2,1,0:T(8,128)S(1)}, f32[2,104,512]{2,1,0:T(8,128)S(1)}, u32[]{:S(2)}, u32[]{:S(2)}) %collective-permute-start.2) | collective-permute-done | bytes 426016 | tf_op jit(solution)/shard_map/ppermute | solution.py:820
  82.5 38.3 %all-to-all-done = f32[16,32,192]{2,1,0:T(8,128)S(1)} async-done(((f32[16,32,192]{2,1,0:T(8,128)}), f32[16,32,192]{2,1,0:T(8,128)S(1)}, u32[]{:S(2)}, u32[]{:S(2)}) %all-to-all-start) | async-done | bytes 393248 | tf_op jit(solution)/shard_map/all_to_all | solution.py:1001
  121.6 9.7 %shard_map.476 = (f32[8,96,128]{2,1,0:T(8,128)}, f32[64,1536]{1,0:T(8,128)}, f32[8,1536]{1,0:T(8,128)}, bf16[1536,192]{1,0:T(8,128)(2,1)}, bf16[1536,192]{1,0:T(...) custom-call(s32[7]{0:T(128)} %stack.269.ids_ref.refs_0_, f32[4,104,512]{2,1,0:T(8,128)} %copy-done.1, ...), custom_call_target="tpu_custom_call" | custom-call | flops 1100000000 | tf_op jit(solution)/shard_map/pallas_call | solution.py:798
  135.8 16.0 %all-to-all-done.1.got_ref = f32[8,96,128]{2,1,0:T(8,128)S(1)} async-done(((f32[8,96,128]{2,1,0:T(8,128)}), f32[8,96,128]{2,1,0:T(8,128)S(1)}, u32[]{:S(2)}, u32[]{:S(2)}) %all-to-all-start.1) | async-done | bytes 393248 | tf_op jit(solution)/shard_map/all_to_all | solution.py:871
  151.8 21.8 %all-gather.4.cloned.1.call-done.g_ref.refs_6_ = f32[16,19,32,512]{3,2,1,0:T(8,128)} async-done(((f32[1,19,32,512]{3,2,1,0:T(8,128)}), f32[16,19,32,512]{3,2,1,0:T(8,128)}) %all-gather.4.cloned.1.call-update) | async-done | bytes 19922960 | tf_op jit(solution)/shard_map/all_gather | solution.py:1014
  173.6 8.2 %shard_map.477 = (f32[192,512]{1,0:T(8,128)}, f32[192,512]{1,0:T(8,128)}, f32[192,2048]{1,0:T(8,128)}) custom-call(s32[7]{0:T(128)} %stack.269.ids_ref.refs_0_, f32[192,512]{1,0:T(8,128)} %bitcast.219, f32[8,96,128]{2,1,0:T(8,128)} %copy-done.6, f32[8,512]{1,0:T(8,128)} %get-tuple-element.88.norm_ref.refs_3_, ...), custom_call_target="tpu_custom_call" | custom-call | flops 880000000 | tf_op jit(solution)/shard_map/pallas_call | solution.py:798
  192.8 6.7 %all-to-all-start.2 = ((f32[8,32,384]{2,1,0:T(8,128)}), f32[8,32,384]{2,1,0:T(8,128)S(1)}, u32[]{:S(2)}, u32[]{:S(2)}) async-start(f32[8,32,384]{2,1,0:T(8,128)} %get-tuple-element.91), calls=%async_computation.2 | async-start | bytes 786432 | tf_op jit(solution)/shard_map/all_to_all | solution.py:874
  199.6 15.1 %all-to-all-done.2.packed_ref = f32[8,32,384]{2,1,0:T(8,128)S(1)} async-done(((f32[8,32,384]{2,1,0:T(8,128)}), f32[8,32,384]{2,1,0:T(8,128)S(1)}, u32[]{:S(2)}, u32[]{:S(2)}) %all-to-all-start.2) | async-done | bytes 393248 | tf_op jit(solution)/shard_map/all_to_all | solution.py:874
  222.9 36.2 %all-gather.6.cloned.1.call-done.refs_7_ = f32[16,8,32,512]{3,2,1,0:T(8,128)} async-done(((f32[1,8,32,512]{3,2,1,0:T(8,128)}), f32[16,8,32,512]{3,2,1,0:T(8,128)}) %all-gather.6.cloned.1.call-update) | async-done | bytes 8388624 | tf_op jit(solution)/shard_map/all_gather | solution.py:1016
  259.7 12.8 %shard_map.480 = (f32[192,512]{1,0:T(8,128)}, f32[8,32,128]{2,1,0:T(8,128)}, f32[64,512]{1,0:T(8,128)}, f32[64,5120]{1,0:T(8,128)}, f32[64,5120]{1,0:T(8,128)}) custom-call(s32[7]{0:T(128)} %stack.269.ids_ref.refs_0_, f32[64,512]{1,0:T(8,128)} %get-tuple-element.90.refs_1_.short_ref, f32[8,32,128]{2,1,0:T(8,128)} %copy-done.32, ...), custom_call_target="tpu_custom_call" | custom-call | flops 1430000000 | tf_op jit(solution)/shard_map/pallas_call | solution.py:798
  277.8 5.8 %shard_map.481 = (f32[2,4,88,512]{3,2,1,0:T(8,128)}, f32[2,4,88,512]{3,2,1,0:T(8,128)}, f32[4,2,64,512]{3,2,1,0:T(8,128)}, f32[4,2,64,512]{3,2,1,0:T(8,128)}) custom-call(s32[7]{0:T(128)} %stack.269.ids_ref.refs_0_, f32[64,5120]{1,0:T(8,128)} %get-tuple-element.105.keep_ref.up_keep_ref, f32[64,5120]{1,0:T(8,128)} %copy-done.2), custom_call_target="tpu_custom_call" | custom-call | flops 660000000 | tf_op jit(solution)/shard_map/pallas_call | solution.py:798
  289.7 18.0 %all_to_all.45.got_ref = f32[8,32,384]{2,1,0:T(8,128)} all-to-all(f32[8,32,384]{2,1,0:T(8,128)} %shard_map.482), channel_id=1, replica_groups=mesh['b'=2,'z'=4,'x'=2,'r'=1,'s'=2] {'z','x'}, dimensions={0} | all-to-all | bytes 786432 | tf_op jit(solution)/shard_map/all_to_all | solution.py:871
  307.7 6.6 %shard_map.483 = (f32[192,512]{1,0:T(8,128)}, f32[64,3072]{1,0:T(8,128)}, f32[64,3072]{1,0:T(8,128)}) custom-call(s32[7]{0:T(128)} %stack.269.ids_ref.refs_0_, f32[8,32,384]{2,1,0:T(8,128)} %all_to_all.45.got_ref, f32[64,512]{1,0:T(8,128)} %get-tuple-element.90.refs_1_.short_ref, f32[64,512]{1,0:T(8,128)} %get-tuple-element.112.mixed_ref, ...), custom_call_target="tpu_custom_call" | custom-call | flops 715000000 | tf_op jit(solution)/shard_map/pallas_call | solution.py:798
  321.4 6.1 %shard_map.484 = (f32[2,4,200,384]{3,2,1,0:T(8,128)}, f32[2,4,200,384]{3,2,1,0:T(8,128)}) custom-call(s32[7]{0:T(128)} %stack.269.ids_ref.refs_0_, f32[64,3072]{1,0:T(8,128)} %get-tuple-element.117.keep_ref, f32[64,3072]{1,0:T(8,128)} %copy-done.24, f32[64,5120]{1,0:T(8,128)} %get-tuple-element.105.keep_ref.up_keep_ref, f32[64,5120]{1,0:T(8,128)} %copy-done.2), custom_call_target="tpu_custom_call" | custom-call | flops 770000000 | tf_op jit(solution)/shard_map/pallas_call | solution.py:798
  327.6 12.4 %shard_map.485 = (f32[8,96,128]{2,1,0:T(8,128)}, f32[192,512]{1,0:T(8,128)}, f32[192,3840]{1,0:T(8,128)}, f32[192,3840]{1,0:T(8,128)}) custom-call(s32[7]{0:T(128)} %stack.269.ids_ref.refs_0_, f32[192,512]{1,0:T(8,128)} %get-tuple-element.113.shifted_ref, f32[2,512]{1,0:T(2,128)} %copy-done.58, f32[192,512]{1,0:T(8,128)} %bitcast.218, ...), custom_call_target="tpu_custom_call" | custom-call | flops 1375000064 | tf_op jit(solution)/shard_map/pallas_call | solution.py:798
  344.6 5.7 all-to-all-start.6
  351.9 8.9 %shard_map.486 = (f32[2,4,88,512]{3,2,1,0:T(8,128)}, f32[2,4,88,512]{3,2,1,0:T(8,128)}, f32[4,2,64,512]{3,2,1,0:T(8,128)}, f32[4,2,64,512]{3,2,1,0:T(8,128)}) custom-call(s32[7]{0:T(128)} %stack.269.ids_ref.refs_0_, f32[192,3840]{1,0:T(8,128)} %get-tuple-element.124.keep_ref, f32[192,3840]{1,0:T(8,128)} %collective-permute-done.14.got_ref), custom_call_target="tpu_custom_call" | custom-call | flops 990000000 | tf_op jit(solution)/shard_map/pallas_call | solution.py:798
  360.8 35.6 %all-to-all-done.6.refs_9_ = f32[8,96,128]{2,1,0:T(8,128)S(1)} async-done(((f32[8,96,128]{2,1,0:T(8,128)}), f32[8,96,128]{2,1,0:T(8,128)S(1)}, u32[]{:S(2)}, u32[]{:S(2)}) %all-to-all-start.6) | async-done | bytes 393248 | tf_op jit(solution)/shard_map/all_to_all | solution.py:874
  415.2 15.9 %shard_map.487 = (f32[8,96,384]{2,1,0:T(8,128)}, f32[16,40,192]{2,1,0:T(8,128)}) custom-call(s32[7]{0:T(128)} %stack.269.ids_ref.refs_0_, f32[4,104,512]{2,1,0:T(8,128)} %copy-done.1, f32[4,104,512]{2,1,0:T(8,128)} %collective-permute-done.3.refs_1_, f32[4,104,512]{2,1,0:T(8,128)} %copy-done, f32[4,104,512]{2,1,0:T(8,128)} %collective-permute-done.6.refs_3_, ...), custom_call_target="tpu_custom_call" | custom-call | flops 1760000000 | tf_op jit(solution)/shard_map/pallas_call | solution.py:798
  445.1 22.3 %collective-permute-done.40 = f32[1,64,512]{2,1,0:T(8,128)S(1)} collective-permute-done((f32[1,64,512]{2,1,0:T(8,128)S(1)}, f32[1,64,512]{2,1,0:T(8,128)S(1)}, u32[]{:S(2)}, u32[]{:S(2)}) %collective-permute-start.40) | collective-permute-done | bytes 131104 | tf_op jit(solution)/shard_map/ppermute | solution.py:820
  487.9 8.8 %collective-permute-done.21 = f32[1,200,384]{2,1,0:T(8,128)} collective-permute-done((f32[1,200,384]{2,1,0:T(8,128)}, f32[1,200,384]{2,1,0:T(8,128)}, u32[]{:S(2)}, u32[]{:S(2)}) %collective-permute-start.21) | collective-permute-done | bytes 307232 | tf_op jit(solution)/shard_map/ppermute | solution.py:820
  529.1 7.1 %collective-permute-done.26 = f32[2,88,512]{2,1,0:T(8,128)S(1)} collective-permute-done((f32[2,88,512]{2,1,0:T(8,128)}, f32[2,88,512]{2,1,0:T(8,128)S(1)}, u32[]{:S(2)}, u32[]{:S(2)}) %collective-permute-start.26) | collective-permute-done | bytes 360480 | tf_op jit(solution)/shard_map/ppermute | solution.py:820
  (416 shorter events, 196.5 us)
Async XLA Ops:
  7.2 166.4 %all-gather.4.cloned.1.call-start = ((), (), s32[]{:S(2)}) async-start(), calls=%async_computation.9 | async-start | bytes 21168128 | tf_op jit(solution)/shard_map/all_gather | solution.py:1014
  12.1 247.0 %all-gather.6.cloned.1.call-start = ((), (), s32[]{:S(2)}) async-start(), calls=%async_computation.10 | async-start | bytes 8912896 | tf_op jit(solution)/shard_map/all_gather | solution.py:1016
  17.9 25.4 %collective-permute-start.1 = (f32[1,104,512]{2,1,0:T(8,128)S(1)}, f32[1,104,512]{2,1,0:T(8,128)S(1)}, u32[]{:S(2)}, u32[]{:S(2)}) collective-permute-start(f32[1,104,512]{2,1,0:T(8,128)S(1)} %get-tuple-element.203), channel_id=1, source_target_pairs={{0,8},{2,10},{4,12},{6,14},{8,0},{10,2},{12,4},{14,6},{1,9},{3,11}... | collective-permute-start | bytes 638984 | tf_op jit(solution)/shard_map/ppermute | solution.py:820
  24.8 37.5 %collective-permute-start.5 = (f32[2,104,512]{2,1,0:T(8,128)S(1)}, f32[2,104,512]{2,1,0:T(8,128)S(1)}, u32[]{:S(2)}, u32[]{:S(2)}) collective-permute-start(f32[2,104,512]{2,1,0:T(8,128)S(1)} %pad_maximum_fusion.5), channel_id=1, source_target_pairs={{0,8},{2,10},{4,12},{6,14},{8,0},{10,2},{12,4},{14,6},{1,9},{3,11}... | collective-permute-start | bytes 1277960 | tf_op jit(solution)/shard_map/ppermute | solution.py:820
  43.3 27.4 %collective-permute-start.2 = (f32[2,104,512]{2,1,0:T(8,128)S(1)}, f32[2,104,512]{2,1,0:T(8,128)S(1)}, u32[]{:S(2)}, u32[]{:S(2)}) collective-permute-start(f32[2,104,512]{2,1,0:T(8,128)S(1)} %pad_maximum_fusion.4), channel_id=1, source_target_pairs={{0,4},{2,6},{4,0},{6,2},{8,12},{10,14},{12,8},{14,10},{1,5},{3,7},... | collective-permute-start | bytes 1277960 | tf_op jit(solution)/shard_map/ppermute | solution.py:820
  62.4 58.4 %collective-permute-start.6 = (f32[4,104,512]{2,1,0:T(8,128)S(1)}, f32[4,104,512]{2,1,0:T(8,128)}, u32[]{:S(2)}, u32[]{:S(2)}) collective-permute-start(f32[4,104,512]{2,1,0:T(8,128)S(1)} %pad_maximum_fusion.1.refs_2_), channel_id=1, source_target_pairs={{0,4},{2,6},{4,0},{6,2},{8,12},{10,14},{12,8},{14,10},{1,5},{3,7},... | collective-permute-start | bytes 2555912 | tf_op jit(solution)/shard_map/ppermute | solution.py:820
  70.8 50.0 %collective-permute-start.3 = (f32[4,104,512]{2,1,0:T(8,128)S(1)}, f32[4,104,512]{2,1,0:T(8,128)}, u32[]{:S(2)}, u32[]{:S(2)}) collective-permute-start(f32[4,104,512]{2,1,0:T(8,128)S(1)} %pad_maximum_fusion.refs_0_), channel_id=1, source_target_pairs={{0,2},{2,0},{4,6},{6,4},{8,10},{10,8},{12,14},{14,12},{1,3},{3,1},... | collective-permute-start | bytes 2555912 | tf_op jit(solution)/shard_map/ppermute | solution.py:820
  74.1 46.7 %all-to-all-start = ((f32[16,32,192]{2,1,0:T(8,128)}), f32[16,32,192]{2,1,0:T(8,128)S(1)}, u32[]{:S(2)}, u32[]{:S(2)}) async-start(f32[16,32,192]{2,1,0:T(8,128)} %bitcast.14), calls=%async_computation | async-start | bytes 1048576 | tf_op jit(solution)/shard_map/all_to_all | solution.py:1001
  218.7 40.4 %all-to-all-start.3 = ((f32[8,32,128]{2,1,0:T(8,128)}), f32[8,32,128]{2,1,0:T(8,128)S(1)}, u32[]{:S(2)}, u32[]{:S(2)}) async-start(f32[8,32,128]{2,1,0:T(8,128)} %get-tuple-element.92), calls=%async_computation.3 | async-start | bytes 262144 | tf_op jit(solution)/shard_map/all_to_all | solution.py:871
  283.6 34.1 %collective-permute-start.12 = (f32[2,4,88,512]{3,2,1,0:T(8,128)}, f32[2,4,88,512]{3,2,1,0:T(8,128)}, u32[]{:S(2)}, u32[]{:S(2)}) collective-permute-start(f32[2,4,88,512]{3,2,1,0:T(8,128)} %get-tuple-element.115), channel_id=1, source_target_pairs={{0,16},{16,0},{1,17},{17,1},{2,18},{18,2},{3,19},{19,3},{4,20},{20... | collective-permute-start | bytes 4325384 | tf_op jit(solution)/shard_map/ppermute | solution.py:820
  340.1 59.9 %collective-permute-start.15 = (f32[2,4,200,384]{3,2,1,0:T(8,128)}, f32[2,4,200,384]{3,2,1,0:T(8,128)}, u32[]{:S(2)}, u32[]{:S(2)}) collective-permute-start(f32[2,4,200,384]{3,2,1,0:T(8,128)} %get-tuple-element.134), channel_id=1, source_target_pairs={{0,16},{16,0},{1,17},{17,1},{2,18},{18,2},{3,19},{19,3},{4,20},{20... | collective-permute-start | bytes 7372808 | tf_op jit(solution)/shard_map/ppermute | solution.py:820
  342.5 55.4 %collective-permute-start.37 = (f32[4,2,64,512]{3,2,0,1:T(8,128)}, f32[4,2,64,512]{3,2,0,1:T(8,128)}, u32[]{:S(2)}, u32[]{:S(2)}) collective-permute-start(f32[4,2,64,512]{3,2,0,1:T(8,128)} %copy.119), channel_id=1, source_target_pairs={{0,2},{2,0},{1,3},{3,1},{4,6},{6,4},{5,7},{7,5},{8,10},{10,8},{9,1... | collective-permute-start | bytes 3145736 | tf_op jit(solution)/shard_map/ppermute | solution.py:820
  344.1 52.3 %collective-permute-start.34 = (f32[4,88,512]{2,1,0:T(8,128)}, f32[4,88,512]{2,1,0:T(8,128)S(1)}, u32[]{:S(2)}, u32[]{:S(2)}) collective-permute-start(f32[4,88,512]{2,1,0:T(8,128)} %get-tuple-element.180), channel_id=1, source_target_pairs={{0,2},{2,0},{1,3},{3,1},{4,6},{6,4},{5,7},{7,5},{8,10},{10,8},{9,1... | collective-permute-start | bytes 2162696 | tf_op jit(solution)/shard_map/ppermute | solution.py:820
  344.6 51.8 %all-to-all-start.6 = ((f32[8,96,128]{2,1,0:T(8,128)}), f32[8,96,128]{2,1,0:T(8,128)S(1)}, u32[]{:S(2)}, u32[]{:S(2)}) async-start(f32[8,96,128]{2,1,0:T(8,128)} %get-tuple-element.123), calls=%async_computation.6 | async-start | bytes 786432 | tf_op jit(solution)/shard_map/all_to_all | solution.py:874
  350.2 164.7 %all-gather.8.cloned.1.call-start = ((), (), s32[]{:S(2)}) async-start(), calls=%async_computation.11 | async-start | bytes 3342336 | tf_op jit(solution)/shard_map/all_gather | solution.py:1018
  351.8 53.6 %collective-permute-start.9 = (f32[96,512]{1,0:T(8,128)S(1)}, f32[96,512]{1,0:T(8,128)}, u32[]{:S(2)}, u32[]{:S(2)}) collective-permute-start(f32[96,512]{1,0:T(8,128)S(1)} %get-tuple-element.212), channel_id=1, source_target_pairs={{0,1},{1,0},{2,3},{3,2},{4,5},{5,4},{6,7},{7,6},{8,9},{9,8},{10,11... | collective-permute-start | bytes 589832 | tf_op jit(solution)/shard_map/ppermute | solution.py:820
  403.1 39.1 %collective-permute-start.19 = (f32[4,200,384]{2,1,0:T(8,128)}, f32[4,200,384]{2,1,0:T(8,128)}, u32[]{:S(2)}, u32[]{:S(2)}) collective-permute-start(f32[4,200,384]{2,1,0:T(8,128)} %get-tuple-element.178), channel_id=1, source_target_pairs={{0,2},{2,0},{1,3},{3,1},{4,6},{6,4},{5,7},{7,5},{8,10},{10,8},{9,1... | collective-permute-start | bytes 3686408 | tf_op jit(solution)/shard_map/ppermute | solution.py:820
  411.0 26.7 %collective-permute-start.36 = (f32[1,88,512]{2,1,0:T(8,128)}, f32[1,88,512]{2,1,0:T(8,128)}, u32[]{:S(2)}, u32[]{:S(2)}) collective-permute-start(f32[1,88,512]{2,1,0:T(8,128)} %slice_add_fusion.21), channel_id=1, source_target_pairs={{0,8},{4,12},{8,0},{12,4},{1,9},{5,13},{9,1},{13,5},{2,10},{6,14},... | collective-permute-start | bytes 540680 | tf_op jit(solution)/shard_map/ppermute | solution.py:820
  431.1 81.3 %all-to-all-start.7 = ((f32[8,96,384]{2,1,0:T(8,128)}), f32[8,96,384]{2,1,0:T(8,128)S(1)}, u32[]{:S(2)}, u32[]{:S(2)}) async-start(f32[8,96,384]{2,1,0:T(8,128)} %get-tuple-element.135), calls=%async_computation.7 | async-start | bytes 2359296 | tf_op jit(solution)/shard_map/all_to_all | solution.py:871
  435.0 63.6 %collective-permute-start.24 = (f32[2,4,88,512]{3,2,1,0:T(8,128)}, f32[2,4,88,512]{3,2,1,0:T(8,128)}, u32[]{:S(2)}, u32[]{:S(2)}) collective-permute-start(f32[2,4,88,512]{3,2,1,0:T(8,128)} %get-tuple-element.142), channel_id=1, source_target_pairs={{0,16},{16,0},{1,17},{17,1},{2,18},{18,2},{3,19},{19,3},{4,20},{20... | collective-permute-start | bytes 4325384 | tf_op jit(solution)/shard_map/ppermute | solution.py:820
  435.8 35.4 %collective-permute-start.28 = (f32[4,2,64,512]{3,2,1,0:T(8,128)}, f32[4,2,64,512]{3,2,1,0:T(8,128)S(1)}, u32[]{:S(2)}, u32[]{:S(2)}) collective-permute-start(f32[4,2,64,512]{3,2,1,0:T(8,128)} %get-tuple-element.144), channel_id=1, source_target_pairs={{0,2},{2,0},{1,3},{3,1},{4,6},{6,4},{5,7},{7,5},{8,10},{10,8},{9,1... | collective-permute-start | bytes 3145736 | tf_op jit(solution)/shard_map/ppermute | solution.py:820
  439.8 27.7 %collective-permute-start.40 = (f32[1,64,512]{2,1,0:T(8,128)S(1)}, f32[1,64,512]{2,1,0:T(8,128)S(1)}, u32[]{:S(2)}, u32[]{:S(2)}) collective-permute-start(f32[1,64,512]{2,1,0:T(8,128)S(1)} %slice_add_fusion.25), channel_id=1, source_target_pairs={{0,8},{4,12},{8,0},{12,4},{1,9},{5,13},{9,1},{13,5},{2,10},{6,14},... | collective-permute-start | bytes 393224 | tf_op jit(solution)/shard_map/ppermute | solution.py:820
  443.6 35.1 %collective-permute-start.20 = (f32[2,200,384]{2,1,0:T(8,128)S(1)}, f32[2,200,384]{2,1,0:T(8,128)S(1)}, u32[]{:S(2)}, u32[]{:S(2)}) collective-permute-start(f32[2,200,384]{2,1,0:T(8,128)S(1)} %get-tuple-element.185), channel_id=1, source_target_pairs={{0,4},{4,0},{8,12},{12,8},{1,5},{5,1},{9,13},{13,9},{2,6},{6,2},{1... | collective-permute-start | bytes 1843208 | tf_op jit(solution)/shard_map/ppermute | solution.py:820
  481.1 81.4 %collective-permute-start.42 = (f32[2,32,128]{2,1,0:T(8,128)}, f32[2,32,128]{2,1,0:T(8,128)S(1)}, u32[]{:S(2)}, u32[]{:S(2)}) collective-permute-start(f32[2,32,128]{2,1,0:T(8,128)} %get-tuple-element.235), channel_id=1, source_target_pairs={{0,1},{1,0},{2,3},{3,2},{4,5},{5,4},{6,7},{7,6},{8,9},{9,8},{10,11... | collective-permute-start | bytes 98312 | tf_op jit(solution)/shard_map/ppermute | solution.py:820
  (105 other events, 718.4 us)
Sparse Core Ops, SparseCore 0:
  12.2 161.2 all-gather.3
  176.3 82.7 all-gather.5
  353.9 55.1 all-gather.7

commit v4 on v3

--- a/solution.py
+++ b/solution.py
@@ -440,11 +440,11 @@
 
 def to_blocks(value, buffer):
     for k in range(LANE_BLOCKS):
-        buffer[k] = value[:, k * LANES : (k + 1) * LANES]
-
-
-def from_blocks(buffer):
-    return jnp.concatenate([buffer[k] for k in range(LANE_BLOCKS)], axis=1)
+        buffer[k, : value.shape[0], :] = value[:, k * LANES : (k + 1) * LANES]
+
+
+def from_blocks(buffer, rows):
+    return jnp.concatenate([buffer[k, :rows, :] for k in range(LANE_BLOCKS)], axis=1)
 
 
 def kept_cotangent(ids_ref, cot_ref):
@@ -510,7 +510,7 @@
         store_thirds(act, i, load_thirds(act, i, rows) + matmul(result, tap))
         groups.append(load_thirds(kept, i, rows))
         grad = grad + matmul(groups[i], tap, NT)
-    act_ref[...] = from_blocks(act)
+    act_ref[...] = from_blocks(act, 3 * rows)
     halves = Halves(ids_ref, keep_ref, send_ref)
     grad_mixed, grad_attended = ffn_backward(
         grad,
@@ -565,7 +565,7 @@
     for i in range(3):
         ready(pool_wait[i])
         store_thirds(back, i, matmul(grad, pool[i].reshape(D, D), NT))
-    shifted_ref[...] = from_blocks(back)
+    shifted_ref[...] = from_blocks(back, 3 * rows)
     shift_rows(full_ref, tail_ref, moved)
     halves = Halves(ids_ref, keep_ref, send_ref)
     halves.whole(normed)
@@ -1055,7 +1055,7 @@
         5,
         shorten_kernel,
         [shape(short_rows, D), shape(HEADS, short_half, 6 * HEAD_DIM)],
-        [column_buffer(3), column_buffer(3), blocks_of(rows + 8)],
+        [column_buffer(3), column_buffer(3), blocks_of(rows + 16)],
         ids,
         [full, tail, norm],
         [gathered],
@@ -1084,7 +1084,7 @@
             shape(short_rows, middle_wide),
         ],
         [column_buffer(1), column_buffer(4), row_buffer, column_buffer(3)]
-        + [blocks_of(rows), blocks_of(rows)],
+        + [blocks_of(rows + 8), blocks_of(rows + 8)],
         ids,
         [shortened, got1, norm, full, cot],
         [gathered, second],
@@ -1131,7 +1131,7 @@
         6.5,
         lengthen_grad_kernel,
         [shape(rows, D), shape(short_rows, 6 * D), shape(short_rows, 6 * D)],
-        [column_buffer(3), column_buffer(3), blocks_of(rows + 8), blocks_of(rows)],
+        [column_buffer(3), column_buffer(3), blocks_of(rows + 16), blocks_of(rows + 8)],
         ids,
         [got, shortened, grad_mixed1, norm, full, tail],
         [gathered],

time: 584 us -> 584 us (level)
  no operation moved by 1% of the time
where the time goes in v4:
time: 584 us; the launch traced here: 576 us
  waiting for transfers between devices  282 us (48%)
  Pallas kernels  104 us (18%)
  starting transfers between devices  77.5 us (13%)
  other arithmetic  43.7 us (7%)
  local copies, waits for them, and re-layouts  33.3 us (6%)
  blocking collectives  18 us (3%)
  between operations  17.9 us (3%)
    ppermute x45, waiting for transfers between devices, swap_with(): return lax.ppermute(value, axis, [(i, i ^ mask) for i in range(size)])  112 us
    pallas_call x13, Pallas kernels, call(): pl.pallas_call(kernel, out_shape=list(outs), in_specs=[SMEM] + [VMEM] * l...  104 us
    all_to_all x3, waiting for transfers between devices, rows_to_heads(): got = lax.all_to_all(value, ('z', 'x'), 0, 0, tiled=True)  50.8 us
    all_to_all x1, waiting for transfers between devices, shards(): head_w = lax.all_to_all(head_cols, wide_axes, 0, 0, tiled=True)  38.3 us
    ppermute x45, starting transfers between devices, swap_with(): return lax.ppermute(value, axis, [(i, i ^ mask) for i in range(size)])  37.4 us
    all_gather x1, waiting for transfers between devices, shards(): second = lax.all_gather(second, wide_axes, axis=0, tiled=False)  36.2 us
    all_gather x1, waiting for transfers between devices, shards(): gathered = lax.all_gather(packed, wide_axes, axis=0, tiled=False)  21.8 us
    all_to_all x1, blocking collectives, heads_to_rows(): return lax.all_to_all(mine, ('z', 'x'), 0, 0, tiled=True)  18 us
  transfers between devices with their start and end apart: 58, of which 26 were waited for; matrix products, arithmetic and copies ran while one was open for 10% of the time, Pallas kernels for 13%

profile of v4, /device:TPU:0, one launch (start us, length us, event | category | flops | bytes accessed | tf_op | source)
XLA Modules:
  0.0 576.0 jit_solution(7227823418448454693)
XLA Ops:
  26.3 17.0 %collective-permute-done.1 = f32[1,104,512]{2,1,0:T(8,128)S(1)} collective-permute-done((f32[1,104,512]{2,1,0:T(8,128)S(1)}, f32[1,104,512]{2,1,0:T(8,128)S(1)}, u32[]{:S(2)}, u32[]{:S(2)}) %collective-permute-start.1) | collective-permute-done | bytes 213024 | tf_op jit(solution)/shard_map/ppermute | solution.py:820
  43.4 18.9 %collective-permute-done.5 = f32[2,104,512]{2,1,0:T(8,128)S(1)} collective-permute-done((f32[2,104,512]{2,1,0:T(8,128)S(1)}, f32[2,104,512]{2,1,0:T(8,128)S(1)}, u32[]{:S(2)}, u32[]{:S(2)}) %collective-permute-start.5) | collective-permute-done | bytes 426016 | tf_op jit(solution)/shard_map/ppermute | solution.py:820
  63.1 7.6 %collective-permute-done.2 = f32[2,104,512]{2,1,0:T(8,128)S(1)} collective-permute-done((f32[2,104,512]{2,1,0:T(8,128)S(1)}, f32[2,104,512]{2,1,0:T(8,128)S(1)}, u32[]{:S(2)}, u32[]{:S(2)}) %collective-permute-start.2) | collective-permute-done | bytes 426016 | tf_op jit(solution)/shard_map/ppermute | solution.py:820
  82.5 38.3 %all-to-all-done = f32[16,32,192]{2,1,0:T(8,128)S(1)} async-done(((f32[16,32,192]{2,1,0:T(8,128)}), f32[16,32,192]{2,1,0:T(8,128)S(1)}, u32[]{:S(2)}, u32[]{:S(2)}) %all-to-all-start) | async-done | bytes 393248 | tf_op jit(solution)/shard_map/all_to_all | solution.py:1001
  121.6 9.7 %shard_map.476 = (f32[8,96,128]{2,1,0:T(8,128)}, f32[64,1536]{1,0:T(8,128)}, f32[8,1536]{1,0:T(8,128)}, bf16[1536,192]{1,0:T(8,128)(2,1)}, bf16[1536,192]{1,0:T(...) custom-call(s32[7]{0:T(128)} %stack.269.ids_ref.refs_0_, f32[4,104,512]{2,1,0:T(8,128)} %copy-done.1, ...), custom_call_target="tpu_custom_call" | custom-call | flops 1100000000 | tf_op jit(solution)/shard_map/pallas_call | solution.py:798
  135.8 16.0 %all-to-all-done.1.got_ref = f32[8,96,128]{2,1,0:T(8,128)S(1)} async-done(((f32[8,96,128]{2,1,0:T(8,128)}), f32[8,96,128]{2,1,0:T(8,128)S(1)}, u32[]{:S(2)}, u32[]{:S(2)}) %all-to-all-start.1) | async-done | bytes 393248 | tf_op jit(solution)/shard_map/all_to_all | solution.py:871
  151.8 21.8 %all-gather.4.cloned.1.call-done.g_ref.refs_6_ = f32[16,19,32,512]{3,2,1,0:T(8,128)} async-done(((f32[1,19,32,512]{3,2,1,0:T(8,128)}), f32[16,19,32,512]{3,2,1,0:T(8,128)}) %all-gather.4.cloned.1.call-update) | async-done | bytes 19922960 | tf_op jit(solution)/shard_map/all_gather | solution.py:1014
  173.6 8.2 %shard_map.477 = (f32[192,512]{1,0:T(8,128)}, f32[192,512]{1,0:T(8,128)}, f32[192,2048]{1,0:T(8,128)}) custom-call(s32[7]{0:T(128)} %stack.269.ids_ref.refs_0_, f32[192,512]{1,0:T(8,128)} %bitcast.219, f32[8,96,128]{2,1,0:T(8,128)} %copy-done.6, f32[8,512]{1,0:T(8,128)} %get-tuple-element.88.norm_ref.refs_3_, ...), custom_call_target="tpu_custom_call" | custom-call | flops 880000000 | tf_op jit(solution)/shard_map/pallas_call | solution.py:798
  192.8 6.7 %all-to-all-start.2 = ((f32[8,32,384]{2,1,0:T(8,128)}), f32[8,32,384]{2,1,0:T(8,128)S(1)}, u32[]{:S(2)}, u32[]{:S(2)}) async-start(f32[8,32,384]{2,1,0:T(8,128)} %get-tuple-element.91), calls=%async_computation.2 | async-start | bytes 786432 | tf_op jit(solution)/shard_map/all_to_all | solution.py:874
  199.6 15.1 %all-to-all-done.2.packed_ref = f32[8,32,384]{2,1,0:T(8,128)S(1)} async-done(((f32[8,32,384]{2,1,0:T(8,128)}), f32[8,32,384]{2,1,0:T(8,128)S(1)}, u32[]{:S(2)}, u32[]{:S(2)}) %all-to-all-start.2) | async-done | bytes 393248 | tf_op jit(solution)/shard_map/all_to_all | solution.py:874
  222.9 36.2 %all-gather.6.cloned.1.call-done.refs_7_ = f32[16,8,32,512]{3,2,1,0:T(8,128)} async-done(((f32[1,8,32,512]{3,2,1,0:T(8,128)}), f32[16,8,32,512]{3,2,1,0:T(8,128)}) %all-gather.6.cloned.1.call-update) | async-done | bytes 8388624 | tf_op jit(solution)/shard_map/all_gather | solution.py:1016
  259.7 12.8 %shard_map.480 = (f32[192,512]{1,0:T(8,128)}, f32[8,32,128]{2,1,0:T(8,128)}, f32[64,512]{1,0:T(8,128)}, f32[64,5120]{1,0:T(8,128)}, f32[64,5120]{1,0:T(8,128)}) custom-call(s32[7]{0:T(128)} %stack.269.ids_ref.refs_0_, f32[64,512]{1,0:T(8,128)} %get-tuple-element.90.refs_1_.short_ref, f32[8,32,128]{2,1,0:T(8,128)} %copy-done.32, ...), custom_call_target="tpu_custom_call" | custom-call | flops 1430000000 | tf_op jit(solution)/shard_map/pallas_call | solution.py:798
  277.8 5.8 %shard_map.481 = (f32[2,4,88,512]{3,2,1,0:T(8,128)}, f32[2,4,88,512]{3,2,1,0:T(8,128)}, f32[4,2,64,512]{3,2,1,0:T(8,128)}, f32[4,2,64,512]{3,2,1,0:T(8,128)}) custom-call(s32[7]{0:T(128)} %stack.269.ids_ref.refs_0_, f32[64,5120]{1,0:T(8,128)} %get-tuple-element.105.keep_ref.up_keep_ref, f32[64,5120]{1,0:T(8,128)} %copy-done.2), custom_call_target="tpu_custom_call" | custom-call | flops 660000000 | tf_op jit(solution)/shard_map/pallas_call | solution.py:798
  289.7 18.0 %all_to_all.45.got_ref = f32[8,32,384]{2,1,0:T(8,128)} all-to-all(f32[8,32,384]{2,1,0:T(8,128)} %shard_map.482), channel_id=1, replica_groups=mesh['b'=2,'z'=4,'x'=2,'r'=1,'s'=2] {'z','x'}, dimensions={0} | all-to-all | bytes 786432 | tf_op jit(solution)/shard_map/all_to_all | solution.py:871
  307.7 6.6 %shard_map.483 = (f32[192,512]{1,0:T(8,128)}, f32[64,3072]{1,0:T(8,128)}, f32[64,3072]{1,0:T(8,128)}) custom-call(s32[7]{0:T(128)} %stack.269.ids_ref.refs_0_, f32[8,32,384]{2,1,0:T(8,128)} %all_to_all.45.got_ref, f32[64,512]{1,0:T(8,128)} %get-tuple-element.90.refs_1_.short_ref, f32[64,512]{1,0:T(8,128)} %get-tuple-element.112.mixed_ref, ...), custom_call_target="tpu_custom_call" | custom-call | flops 715000000 | tf_op jit(solution)/shard_map/pallas_call | solution.py:798
  321.5 6.1 %shard_map.484 = (f32[2,4,200,384]{3,2,1,0:T(8,128)}, f32[2,4,200,384]{3,2,1,0:T(8,128)}) custom-call(s32[7]{0:T(128)} %stack.269.ids_ref.refs_0_, f32[64,3072]{1,0:T(8,128)} %get-tuple-element.117.keep_ref, f32[64,3072]{1,0:T(8,128)} %copy-done.24, f32[64,5120]{1,0:T(8,128)} %get-tuple-element.105.keep_ref.up_keep_ref, f32[64,5120]{1,0:T(8,128)} %copy-done.2), custom_call_target="tpu_custom_call" | custom-call | flops 770000000 | tf_op jit(solution)/shard_map/pallas_call | solution.py:798
  327.6 12.4 %shard_map.485 = (f32[8,96,128]{2,1,0:T(8,128)}, f32[192,512]{1,0:T(8,128)}, f32[192,3840]{1,0:T(8,128)}, f32[192,3840]{1,0:T(8,128)}) custom-call(s32[7]{0:T(128)} %stack.269.ids_ref.refs_0_, f32[192,512]{1,0:T(8,128)} %get-tuple-element.113.shifted_ref, f32[2,512]{1,0:T(2,128)} %copy-done.58, f32[192,512]{1,0:T(8,128)} %bitcast.218, ...), custom_call_target="tpu_custom_call" | custom-call | flops 1375000064 | tf_op jit(solution)/shard_map/pallas_call | solution.py:798
  344.6 5.6 all-to-all-start.6
  351.9 8.9 %shard_map.486 = (f32[2,4,88,512]{3,2,1,0:T(8,128)}, f32[2,4,88,512]{3,2,1,0:T(8,128)}, f32[4,2,64,512]{3,2,1,0:T(8,128)}, f32[4,2,64,512]{3,2,1,0:T(8,128)}) custom-call(s32[7]{0:T(128)} %stack.269.ids_ref.refs_0_, f32[192,3840]{1,0:T(8,128)} %get-tuple-element.124.keep_ref, f32[192,3840]{1,0:T(8,128)} %collective-permute-done.14.got_ref), custom_call_target="tpu_custom_call" | custom-call | flops 990000000 | tf_op jit(solution)/shard_map/pallas_call | solution.py:798
  360.8 35.7 %all-to-all-done.6.refs_9_ = f32[8,96,128]{2,1,0:T(8,128)S(1)} async-done(((f32[8,96,128]{2,1,0:T(8,128)}), f32[8,96,128]{2,1,0:T(8,128)S(1)}, u32[]{:S(2)}, u32[]{:S(2)}) %all-to-all-start.6) | async-done | bytes 393248 | tf_op jit(solution)/shard_map/all_to_all | solution.py:874
  415.3 15.9 %shard_map.487 = (f32[8,96,384]{2,1,0:T(8,128)}, f32[16,40,192]{2,1,0:T(8,128)}) custom-call(s32[7]{0:T(128)} %stack.269.ids_ref.refs_0_, f32[4,104,512]{2,1,0:T(8,128)} %copy-done.1, f32[4,104,512]{2,1,0:T(8,128)} %collective-permute-done.3.refs_1_, f32[4,104,512]{2,1,0:T(8,128)} %copy-done, f32[4,104,512]{2,1,0:T(8,128)} %collective-permute-done.6.refs_3_, ...), custom_call_target="tpu_custom_call" | custom-call | flops 1760000000 | tf_op jit(solution)/shard_map/pallas_call | solution.py:798
  445.2 22.3 %collective-permute-done.40 = f32[1,64,512]{2,1,0:T(8,128)S(1)} collective-permute-done((f32[1,64,512]{2,1,0:T(8,128)S(1)}, f32[1,64,512]{2,1,0:T(8,128)S(1)}, u32[]{:S(2)}, u32[]{:S(2)}) %collective-permute-start.40) | collective-permute-done | bytes 131104 | tf_op jit(solution)/shard_map/ppermute | solution.py:820
  487.9 8.7 %collective-permute-done.21 = f32[1,200,384]{2,1,0:T(8,128)} collective-permute-done((f32[1,200,384]{2,1,0:T(8,128)}, f32[1,200,384]{2,1,0:T(8,128)}, u32[]{:S(2)}, u32[]{:S(2)}) %collective-permute-start.21) | collective-permute-done | bytes 307232 | tf_op jit(solution)/shard_map/ppermute | solution.py:820
  529.1 7.1 %collective-permute-done.26 = f32[2,88,512]{2,1,0:T(8,128)S(1)} collective-permute-done((f32[2,88,512]{2,1,0:T(8,128)}, f32[2,88,512]{2,1,0:T(8,128)S(1)}, u32[]{:S(2)}, u32[]{:S(2)}) %collective-permute-start.26) | collective-permute-done | bytes 360480 | tf_op jit(solution)/shard_map/ppermute | solution.py:820
  (416 shorter events, 196.6 us)
Async XLA Ops:
  7.2 166.4 %all-gather.4.cloned.1.call-start = ((), (), s32[]{:S(2)}) async-start(), calls=%async_computation.9 | async-start | bytes 21168128 | tf_op jit(solution)/shard_map/all_gather | solution.py:1014
  12.1 247.0 %all-gather.6.cloned.1.call-start = ((), (), s32[]{:S(2)}) async-start(), calls=%async_computation.10 | async-start | bytes 8912896 | tf_op jit(solution)/shard_map/all_gather | solution.py:1016
  17.9 25.4 %collective-permute-start.1 = (f32[1,104,512]{2,1,0:T(8,128)S(1)}, f32[1,104,512]{2,1,0:T(8,128)S(1)}, u32[]{:S(2)}, u32[]{:S(2)}) collective-permute-start(f32[1,104,512]{2,1,0:T(8,128)S(1)} %get-tuple-element.203), channel_id=1, source_target_pairs={{0,8},{2,10},{4,12},{6,14},{8,0},{10,2},{12,4},{14,6},{1,9},{3,11}... | collective-permute-start | bytes 638984 | tf_op jit(solution)/shard_map/ppermute | solution.py:820
  24.8 37.5 %collective-permute-start.5 = (f32[2,104,512]{2,1,0:T(8,128)S(1)}, f32[2,104,512]{2,1,0:T(8,128)S(1)}, u32[]{:S(2)}, u32[]{:S(2)}) collective-permute-start(f32[2,104,512]{2,1,0:T(8,128)S(1)} %pad_maximum_fusion.5), channel_id=1, source_target_pairs={{0,8},{2,10},{4,12},{6,14},{8,0},{10,2},{12,4},{14,6},{1,9},{3,11}... | collective-permute-start | bytes 1277960 | tf_op jit(solution)/shard_map/ppermute | solution.py:820
  43.3 27.4 %collective-permute-start.2 = (f32[2,104,512]{2,1,0:T(8,128)S(1)}, f32[2,104,512]{2,1,0:T(8,128)S(1)}, u32[]{:S(2)}, u32[]{:S(2)}) collective-permute-start(f32[2,104,512]{2,1,0:T(8,128)S(1)} %pad_maximum_fusion.4), channel_id=1, source_target_pairs={{0,4},{2,6},{4,0},{6,2},{8,12},{10,14},{12,8},{14,10},{1,5},{3,7},... | collective-permute-start | bytes 1277960 | tf_op jit(solution)/shard_map/ppermute | solution.py:820
  62.4 58.4 %collective-permute-start.6 = (f32[4,104,512]{2,1,0:T(8,128)S(1)}, f32[4,104,512]{2,1,0:T(8,128)}, u32[]{:S(2)}, u32[]{:S(2)}) collective-permute-start(f32[4,104,512]{2,1,0:T(8,128)S(1)} %pad_maximum_fusion.1.refs_2_), channel_id=1, source_target_pairs={{0,4},{2,6},{4,0},{6,2},{8,12},{10,14},{12,8},{14,10},{1,5},{3,7},... | collective-permute-start | bytes 2555912 | tf_op jit(solution)/shard_map/ppermute | solution.py:820
  70.8 50.0 %collective-permute-start.3 = (f32[4,104,512]{2,1,0:T(8,128)S(1)}, f32[4,104,512]{2,1,0:T(8,128)}, u32[]{:S(2)}, u32[]{:S(2)}) collective-permute-start(f32[4,104,512]{2,1,0:T(8,128)S(1)} %pad_maximum_fusion.refs_0_), channel_id=1, source_target_pairs={{0,2},{2,0},{4,6},{6,4},{8,10},{10,8},{12,14},{14,12},{1,3},{3,1},... | collective-permute-start | bytes 2555912 | tf_op jit(solution)/shard_map/ppermute | solution.py:820
  74.1 46.7 %all-to-all-start = ((f32[16,32,192]{2,1,0:T(8,128)}), f32[16,32,192]{2,1,0:T(8,128)S(1)}, u32[]{:S(2)}, u32[]{:S(2)}) async-start(f32[16,32,192]{2,1,0:T(8,128)} %bitcast.14), calls=%async_computation | async-start | bytes 1048576 | tf_op jit(solution)/shard_map/all_to_all | solution.py:1001
  218.7 40.4 %all-to-all-start.3 = ((f32[8,32,128]{2,1,0:T(8,128)}), f32[8,32,128]{2,1,0:T(8,128)S(1)}, u32[]{:S(2)}, u32[]{:S(2)}) async-start(f32[8,32,128]{2,1,0:T(8,128)} %get-tuple-element.92), calls=%async_computation.3 | async-start | bytes 262144 | tf_op jit(solution)/shard_map/all_to_all | solution.py:871
  283.7 34.1 %collective-permute-start.12 = (f32[2,4,88,512]{3,2,1,0:T(8,128)}, f32[2,4,88,512]{3,2,1,0:T(8,128)}, u32[]{:S(2)}, u32[]{:S(2)}) collective-permute-start(f32[2,4,88,512]{3,2,1,0:T(8,128)} %get-tuple-element.115), channel_id=1, source_target_pairs={{0,16},{16,0},{1,17},{17,1},{2,18},{18,2},{3,19},{19,3},{4,20},{20... | collective-permute-start | bytes 4325384 | tf_op jit(solution)/shard_map/ppermute | solution.py:820
  340.1 59.9 %collective-permute-start.15 = (f32[2,4,200,384]{3,2,1,0:T(8,128)}, f32[2,4,200,384]{3,2,1,0:T(8,128)}, u32[]{:S(2)}, u32[]{:S(2)}) collective-permute-start(f32[2,4,200,384]{3,2,1,0:T(8,128)} %get-tuple-element.134), channel_id=1, source_target_pairs={{0,16},{16,0},{1,17},{17,1},{2,18},{18,2},{3,19},{19,3},{4,20},{20... | collective-permute-start | bytes 7372808 | tf_op jit(solution)/shard_map/ppermute | solution.py:820
  342.5 55.4 %collective-permute-start.37 = (f32[4,2,64,512]{3,2,0,1:T(8,128)}, f32[4,2,64,512]{3,2,0,1:T(8,128)}, u32[]{:S(2)}, u32[]{:S(2)}) collective-permute-start(f32[4,2,64,512]{3,2,0,1:T(8,128)} %copy.119), channel_id=1, source_target_pairs={{0,2},{2,0},{1,3},{3,1},{4,6},{6,4},{5,7},{7,5},{8,10},{10,8},{9,1... | collective-permute-start | bytes 3145736 | tf_op jit(solution)/shard_map/ppermute | solution.py:820
  344.1 52.3 %collective-permute-start.34 = (f32[4,88,512]{2,1,0:T(8,128)}, f32[4,88,512]{2,1,0:T(8,128)S(1)}, u32[]{:S(2)}, u32[]{:S(2)}) collective-permute-start(f32[4,88,512]{2,1,0:T(8,128)} %get-tuple-element.180), channel_id=1, source_target_pairs={{0,2},{2,0},{1,3},{3,1},{4,6},{6,4},{5,7},{7,5},{8,10},{10,8},{9,1... | collective-permute-start | bytes 2162696 | tf_op jit(solution)/shard_map/ppermute | solution.py:820
  344.6 51.8 %all-to-all-start.6 = ((f32[8,96,128]{2,1,0:T(8,128)}), f32[8,96,128]{2,1,0:T(8,128)S(1)}, u32[]{:S(2)}, u32[]{:S(2)}) async-start(f32[8,96,128]{2,1,0:T(8,128)} %get-tuple-element.123), calls=%async_computation.6 | async-start | bytes 786432 | tf_op jit(solution)/shard_map/all_to_all | solution.py:874
  350.2 164.8 %all-gather.8.cloned.1.call-start = ((), (), s32[]{:S(2)}) async-start(), calls=%async_computation.11 | async-start | bytes 3342336 | tf_op jit(solution)/shard_map/all_gather | solution.py:1018
  351.8 53.7 %collective-permute-start.9 = (f32[96,512]{1,0:T(8,128)S(1)}, f32[96,512]{1,0:T(8,128)}, u32[]{:S(2)}, u32[]{:S(2)}) collective-permute-start(f32[96,512]{1,0:T(8,128)S(1)} %get-tuple-element.212), channel_id=1, source_target_pairs={{0,1},{1,0},{2,3},{3,2},{4,5},{5,4},{6,7},{7,6},{8,9},{9,8},{10,11... | collective-permute-start | bytes 589832 | tf_op jit(solution)/shard_map/ppermute | solution.py:820
  403.1 39.1 %collective-permute-start.19 = (f32[4,200,384]{2,1,0:T(8,128)}, f32[4,200,384]{2,1,0:T(8,128)}, u32[]{:S(2)}, u32[]{:S(2)}) collective-permute-start(f32[4,200,384]{2,1,0:T(8,128)} %get-tuple-element.178), channel_id=1, source_target_pairs={{0,2},{2,0},{1,3},{3,1},{4,6},{6,4},{5,7},{7,5},{8,10},{10,8},{9,1... | collective-permute-start | bytes 3686408 | tf_op jit(solution)/shard_map/ppermute | solution.py:820
  411.0 26.8 %collective-permute-start.36 = (f32[1,88,512]{2,1,0:T(8,128)}, f32[1,88,512]{2,1,0:T(8,128)}, u32[]{:S(2)}, u32[]{:S(2)}) collective-permute-start(f32[1,88,512]{2,1,0:T(8,128)} %slice_add_fusion.21), channel_id=1, source_target_pairs={{0,8},{4,12},{8,0},{12,4},{1,9},{5,13},{9,1},{13,5},{2,10},{6,14},... | collective-permute-start | bytes 540680 | tf_op jit(solution)/shard_map/ppermute | solution.py:820
  431.2 81.3 %all-to-all-start.7 = ((f32[8,96,384]{2,1,0:T(8,128)}), f32[8,96,384]{2,1,0:T(8,128)S(1)}, u32[]{:S(2)}, u32[]{:S(2)}) async-start(f32[8,96,384]{2,1,0:T(8,128)} %get-tuple-element.135), calls=%async_computation.7 | async-start | bytes 2359296 | tf_op jit(solution)/shard_map/all_to_all | solution.py:871
  435.0 63.6 %collective-permute-start.24 = (f32[2,4,88,512]{3,2,1,0:T(8,128)}, f32[2,4,88,512]{3,2,1,0:T(8,128)}, u32[]{:S(2)}, u32[]{:S(2)}) collective-permute-start(f32[2,4,88,512]{3,2,1,0:T(8,128)} %get-tuple-element.142), channel_id=1, source_target_pairs={{0,16},{16,0},{1,17},{17,1},{2,18},{18,2},{3,19},{19,3},{4,20},{20... | collective-permute-start | bytes 4325384 | tf_op jit(solution)/shard_map/ppermute | solution.py:820
  435.8 35.4 %collective-permute-start.28 = (f32[4,2,64,512]{3,2,1,0:T(8,128)}, f32[4,2,64,512]{3,2,1,0:T(8,128)S(1)}, u32[]{:S(2)}, u32[]{:S(2)}) collective-permute-start(f32[4,2,64,512]{3,2,1,0:T(8,128)} %get-tuple-element.144), channel_id=1, source_target_pairs={{0,2},{2,0},{1,3},{3,1},{4,6},{6,4},{5,7},{7,5},{8,10},{10,8},{9,1... | collective-permute-start | bytes 3145736 | tf_op jit(solution)/shard_map/ppermute | solution.py:820
  439.8 27.7 %collective-permute-start.40 = (f32[1,64,512]{2,1,0:T(8,128)S(1)}, f32[1,64,512]{2,1,0:T(8,128)S(1)}, u32[]{:S(2)}, u32[]{:S(2)}) collective-permute-start(f32[1,64,512]{2,1,0:T(8,128)S(1)} %slice_add_fusion.25), channel_id=1, source_target_pairs={{0,8},{4,12},{8,0},{12,4},{1,9},{5,13},{9,1},{13,5},{2,10},{6,14},... | collective-permute-start | bytes 393224 | tf_op jit(solution)/shard_map/ppermute | solution.py:820
  443.6 35.0 %collective-permute-start.20 = (f32[2,200,384]{2,1,0:T(8,128)S(1)}, f32[2,200,384]{2,1,0:T(8,128)S(1)}, u32[]{:S(2)}, u32[]{:S(2)}) collective-permute-start(f32[2,200,384]{2,1,0:T(8,128)S(1)} %get-tuple-element.185), channel_id=1, source_target_pairs={{0,4},{4,0},{8,12},{12,8},{1,5},{5,1},{9,13},{13,9},{2,6},{6,2},{1... | collective-permute-start | bytes 1843208 | tf_op jit(solution)/shard_map/ppermute | solution.py:820
  481.0 81.5 %collective-permute-start.42 = (f32[2,32,128]{2,1,0:T(8,128)}, f32[2,32,128]{2,1,0:T(8,128)S(1)}, u32[]{:S(2)}, u32[]{:S(2)}) collective-permute-start(f32[2,32,128]{2,1,0:T(8,128)} %get-tuple-element.235), channel_id=1, source_target_pairs={{0,1},{1,0},{2,3},{3,2},{4,5},{5,4},{6,7},{7,6},{8,9},{9,8},{10,11... | collective-permute-start | bytes 98312 | tf_op jit(solution)/shard_map/ppermute | solution.py:820
  (105 other events, 718.7 us)
Sparse Core Ops, SparseCore 0:
  12.2 161.2 all-gather.3
  176.3 82.7 all-gather.5
  353.9 55.2 all-gather.7
